TPU v7x, 32 devices: a whole 2x2x4 slice. The times are simulated.
32 devices in a mesh: dp: 8 (over z, x), tensor: 4 (over y, core).
Axes of the slice: x: 2, y: 2, z: 4, core: 2. Of those that a mesh axis runs over, the one named last changes fastest.
Arguments:
- tokens: bfloat16 [8192, 768], P(('dp', 'tensor')), may hold values from -6 to 6
- cotangent: bfloat16 [8192, 768], P(('dp', 'tensor')), may hold values from -6 to 6
- prefix: int32 [8], P('dp'), may hold values from 102 to 512
- w_qkv: bfloat16 [2, 3, 768, 768], P(None, None, None, 'tensor'), may hold values from -0.3125 to 0.3125
- bias_qv: float32 [2, 2, 768], P(None, None, 'tensor'), may hold values from -1.8 to 1.8
- w_out: bfloat16 [2, 768, 768], P(None, 'tensor'), may hold values from -0.625 to 0.625
- bias_out: float32 [2, 768], replicated, may hold values from -1.8 to 1.8
- norm_gain: float32 [2, 2, 768], replicated, may hold values from 0.5 to 1.5
- norm_bias: float32 [2, 2, 768], replicated, may hold values from -1.8 to 1.8
- w_up: bfloat16 [2, 768, 3072], P(None, None, 'tensor'), may hold values from -0.21875 to 0.21875
- bias_up: float32 [2, 3072], P(None, 'tensor'), may hold values from -3 to 3
- w_down: bfloat16 [2, 3072, 768], P(None, 'tensor'), may hold values from -0.15625 to 0.15625
- bias_down: float32 [2, 768], replicated, may hold values from -1.8 to 1.8
Outputs:
- output: float32 [8192, 768], P(('dp', 'tensor'))
- grad_tokens: float32 [8192, 768], P(('dp', 'tensor'))
- grad_w_qkv: float32 [2, 3, 768, 768], P(None, None, 'dp', 'tensor')
- grad_bias_qv: float32 [2, 2, 768], P(None, None, 'tensor')
- grad_w_out: float32 [2, 768, 768], P(None, 'tensor', 'dp')
- grad_bias_out: float32 [2, 768], replicated
- grad_norm_gain: float32 [2, 2, 768], replicated
- grad_norm_bias: float32 [2, 2, 768], replicated
- grad_w_up: float32 [2, 768, 3072], P(None, 'dp', 'tensor')
- grad_bias_up: float32 [2, 3072], P(None, 'tensor')
- grad_w_down: float32 [2, 3072, 768], P(None, 'tensor', 'dp')
- grad_bias_down: float32 [2, 768], replicated
All inputs are finite; a program needn't handle non-finite values.
Results may differ from a plain program's by a relative error of at most 0.025.
The roundings to bfloat16 on the way count: a program that leaves them out, or rounds other values in their place, can miss the bound.
Values may be sent and summed in bfloat16 or wider, within the bound.
A program may use at most 192 MiB of HBM per device.

v0:
```python
import functools
import math

import jax
import jax.numpy as jnp
from jax import lax
from jax.sharding import PartitionSpec as P

HDIM = 64
LEN = 1024
MEM = 10


EPSILON = 1e-06
HIGHEST = lax.Precision.HIGHEST


def gather_rows(values_in):
    return lax.all_gather(values_in, "tensor", axis=0, tiled=True)


def sum_rows(term_fn, row_count):
    return lax.psum_scatter(
        term_fn(jnp.int32(0), lax.axis_size("tensor") * row_count),
        "tensor",
        scatter_dimension=0,
        tiled=True,
    )


def gather_grad(values_in):
    return lax.all_gather(values_in, "tensor", axis=0, tiled=True)


def sum_grad(term_fn, row_count):
    return lax.psum_scatter(
        term_fn(jnp.int32(0), lax.axis_size("tensor") * row_count),
        "tensor",
        scatter_dimension=0,
        tiled=True,
    )


def normalize(total, gain, shift):
    row_mean = jnp.mean(total, axis=-1, keepdims=True)
    centered = total - row_mean
    spread = jnp.mean(centered * centered, axis=-1, keepdims=True)
    recip = lax.rsqrt(spread + EPSILON)
    normal = centered * recip
    return (normal * gain + shift, normal, recip)


def normalize_back(grad_in, normal, recip, gain):
    scaled = grad_in * gain
    inner = (
        scaled
        - jnp.mean(scaled, axis=-1, keepdims=True)
        - normal * jnp.mean(scaled * normal, axis=-1, keepdims=True)
    )
    return (recip * inner, jnp.sum(grad_in * normal, axis=0), jnp.sum(grad_in, axis=0))


def probabilities(query_block, keys_seq, first_row, prefix_len):
    block_rows = query_block.shape[0]
    scale = 1.0 / math.sqrt(HDIM)
    scores = (
        jnp.einsum("bhd,khd->hbk", query_block, keys_seq, preferred_element_type=jnp.float32)
        * scale
    )
    row_pos = first_row + lax.broadcasted_iota(jnp.int32, (block_rows, LEN), 0)
    col_pos = lax.broadcasted_iota(jnp.int32, (block_rows, LEN), 1)
    visible = (
        (col_pos <= row_pos) | (col_pos < prefix_len) | (row_pos < MEM) | (row_pos >= LEN - MEM)
    )
    scores = jnp.where(visible[None], scores, -1e30)
    row_max = jnp.max(scores, axis=-1, keepdims=True)
    expo = jnp.exp(scores - row_max)
    return expo / jnp.sum(expo, axis=-1, keepdims=True)


def attention_forward(query, keys, values, prefix):
    seq_count = prefix.shape[0]
    width = query.shape[1]
    local_heads = width // HDIM
    block_rows = min(512, LEN)
    block_count = LEN // block_rows
    shape_four = (seq_count, LEN, local_heads, HDIM)

    def per_sequence(sequence):
        query_seq, keys_seq, values_seq, prefix_len = sequence

        def per_block(block_index):
            first_row = block_index * block_rows
            query_block = lax.dynamic_slice_in_dim(query_seq, first_row, block_rows, 0)
            probs = probabilities(query_block, keys_seq, first_row, prefix_len)
            return jnp.einsum(
                "hbk,khd->bhd",
                probs.astype(jnp.bfloat16),
                values_seq,
                preferred_element_type=jnp.float32,
            ).astype(jnp.bfloat16)

        blocks = lax.map(per_block, jnp.arange(block_count, dtype=jnp.int32))
        return blocks.reshape(LEN, local_heads, HDIM)

    context = lax.map(
        per_sequence,
        (query.reshape(shape_four), keys.reshape(shape_four), values.reshape(shape_four), prefix),
    )
    return context.reshape(seq_count * LEN, width)


def attention_backward(query, keys, values, grad_context, prefix):
    seq_count = prefix.shape[0]
    width = query.shape[1]
    local_heads = width // HDIM
    block_rows = min(512, LEN)
    block_count = LEN // block_rows
    scale = 1.0 / math.sqrt(HDIM)
    shape_four = (seq_count, LEN, local_heads, HDIM)

    def per_sequence(sequence):
        query_seq, keys_seq, values_seq, grad_seq, prefix_len = sequence

        def per_block(running, block_index):
            keys_acc, values_acc = running
            first_row = block_index * block_rows
            query_block = lax.dynamic_slice_in_dim(query_seq, first_row, block_rows, 0)
            grad_block = lax.dynamic_slice_in_dim(grad_seq, first_row, block_rows, 0)
            probs = probabilities(query_block, keys_seq, first_row, prefix_len)
            probs_low = probs.astype(jnp.bfloat16)
            grad_probs = jnp.einsum(
                "bhd,khd->hbk",
                grad_block,
                values_seq,
                precision=HIGHEST,
                preferred_element_type=jnp.float32,
            )
            grad_scores = probs * (grad_probs - jnp.sum(probs * grad_probs, axis=-1, keepdims=True))
            grad_query = (
                jnp.einsum(
                    "hbk,khd->bhd",
                    grad_scores,
                    keys_seq,
                    precision=HIGHEST,
                    preferred_element_type=jnp.float32,
                )
                * scale
            )
            keys_acc = (
                keys_acc
                + jnp.einsum(
                    "hbk,bhd->khd",
                    grad_scores,
                    query_block,
                    precision=HIGHEST,
                    preferred_element_type=jnp.float32,
                )
                * scale
            )
            values_acc = values_acc + jnp.einsum(
                "hbk,bhd->khd",
                probs_low,
                grad_block,
                precision=HIGHEST,
                preferred_element_type=jnp.float32,
            )
            return ((keys_acc, values_acc), grad_query)

        zero_acc = jnp.zeros((LEN, local_heads, HDIM), jnp.float32)
        (keys_acc, values_acc), grad_query = lax.scan(
            per_block, (zero_acc, zero_acc), jnp.arange(block_count, dtype=jnp.int32)
        )
        return (grad_query.reshape(LEN, local_heads, HDIM), keys_acc, values_acc)

    grad_q, grad_k, grad_v = lax.map(
        per_sequence,
        (
            query.reshape(shape_four),
            keys.reshape(shape_four),
            values.reshape(shape_four),
            grad_context.reshape(shape_four),
            prefix,
        ),
    )
    flat = (seq_count * LEN, width)
    return (grad_q.reshape(flat), grad_k.reshape(flat), grad_v.reshape(flat))


def local(
    tokens,
    cotangent,
    prefix,
    w_qkv,
    bias_qv,
    w_out,
    bias_out,
    norm_gain,
    norm_bias,
    w_up,
    bias_up,
    w_down,
    bias_down,
):
    my_rows = tokens.shape[0]
    layer_count = w_qkv.shape[0]
    state = tokens.astype(jnp.float32)
    stored = []
    for layer_index in range(layer_count):
        input_whole = gather_rows(state.astype(jnp.bfloat16))
        query = (
            jnp.dot(input_whole, w_qkv[layer_index, 0], preferred_element_type=jnp.float32)
            + bias_qv[layer_index, 0]
        ).astype(jnp.bfloat16)
        keys = jnp.dot(
            input_whole, w_qkv[layer_index, 1], preferred_element_type=jnp.float32
        ).astype(jnp.bfloat16)
        values = (
            jnp.dot(input_whole, w_qkv[layer_index, 2], preferred_element_type=jnp.float32)
            + bias_qv[layer_index, 1]
        ).astype(jnp.bfloat16)
        context = attention_forward(query, keys, values, prefix)

        def attn_term(row_start, row_count):
            return jnp.dot(context, w_out[layer_index], preferred_element_type=jnp.float32)

        attn_share = sum_rows(attn_term, my_rows)
        normed, normal_one, recip_one = normalize(
            state + attn_share + bias_out[layer_index],
            norm_gain[layer_index, 0],
            norm_bias[layer_index, 0],
        )
        normed_whole = gather_rows(normed.astype(jnp.bfloat16))
        hidden = (
            jnp.dot(normed_whole, w_up[layer_index], preferred_element_type=jnp.float32)
            + bias_up[layer_index]
        )
        active = jax.nn.gelu(hidden, approximate=False).astype(jnp.bfloat16)

        def ffn_term(row_start, row_count):
            return jnp.dot(active, w_down[layer_index], preferred_element_type=jnp.float32)

        ffn_share = sum_rows(ffn_term, my_rows)
        state, normal_two, recip_two = normalize(
            normed + ffn_share + bias_down[layer_index],
            norm_gain[layer_index, 1],
            norm_bias[layer_index, 1],
        )
        stored.append(
            (
                input_whole,
                query,
                keys,
                values,
                context,
                normal_one,
                recip_one,
                normed_whole,
                hidden,
                active,
                normal_two,
                recip_two,
            )
        )
    grad_state = cotangent.astype(jnp.float32)
    weight_grads = [None] * layer_count
    bias_grads = [None] * layer_count
    shared_grads = [None] * layer_count
    for layer_index in reversed(range(layer_count)):
        (
            input_whole,
            query,
            keys,
            values,
            context,
            normal_one,
            recip_one,
            normed_whole,
            hidden,
            active,
            normal_two,
            recip_two,
        ) = stored[layer_index]
        grad_two, gain_two, shift_two = normalize_back(
            grad_state, normal_two, recip_two, norm_gain[layer_index, 1]
        )
        ffn_grad_whole = gather_grad(grad_two.astype(jnp.bfloat16))
        grad_down = jnp.einsum(
            "rf,rd->fd", active, ffn_grad_whole, preferred_element_type=jnp.float32
        )
        grad_active = jnp.einsum(
            "rd,fd->rf", ffn_grad_whole, w_down[layer_index], preferred_element_type=jnp.float32
        )
        _, gelu_pull = jax.vjp(functools.partial(jax.nn.gelu, approximate=False), hidden)
        grad_hidden = gelu_pull(grad_active)[0]
        grad_up = jnp.einsum(
            "rd,rf->df",
            normed_whole,
            grad_hidden,
            precision=HIGHEST,
            preferred_element_type=jnp.float32,
        )
        grad_bias_up = jnp.sum(grad_hidden, axis=0)

        def ffn_back_term(row_start, row_count):
            return jnp.einsum(
                "rf,df->rd",
                grad_hidden,
                w_up[layer_index],
                precision=HIGHEST,
                preferred_element_type=jnp.float32,
            )

        grad_normed = sum_grad(ffn_back_term, my_rows) + grad_two
        grad_one, gain_one, shift_one = normalize_back(
            grad_normed, normal_one, recip_one, norm_gain[layer_index, 0]
        )
        attn_grad_whole = gather_grad(grad_one.astype(jnp.bfloat16))
        grad_out = jnp.einsum(
            "rh,rd->hd", context, attn_grad_whole, preferred_element_type=jnp.float32
        )
        grad_context = jnp.einsum(
            "rd,hd->rh", attn_grad_whole, w_out[layer_index], preferred_element_type=jnp.float32
        )
        grad_query, grad_keys, grad_values = attention_backward(
            query, keys, values, grad_context, prefix
        )
        grad_qkv = jnp.stack(
            [
                jnp.einsum(
                    "rd,rh->dh",
                    input_whole,
                    grad_query,
                    precision=HIGHEST,
                    preferred_element_type=jnp.float32,
                ),
                jnp.einsum(
                    "rd,rh->dh",
                    input_whole,
                    grad_keys,
                    precision=HIGHEST,
                    preferred_element_type=jnp.float32,
                ),
                jnp.einsum(
                    "rd,rh->dh",
                    input_whole,
                    grad_values,
                    precision=HIGHEST,
                    preferred_element_type=jnp.float32,
                ),
            ]
        )
        grad_bias_qv = jnp.stack([jnp.sum(grad_query, axis=0), jnp.sum(grad_values, axis=0)])

        def input_back_term(row_start, row_count):
            total = jnp.einsum(
                "rh,dh->rd",
                grad_query,
                w_qkv[layer_index, 0],
                precision=HIGHEST,
                preferred_element_type=jnp.float32,
            )
            total = total + jnp.einsum(
                "rh,dh->rd",
                grad_keys,
                w_qkv[layer_index, 1],
                precision=HIGHEST,
                preferred_element_type=jnp.float32,
            )
            return total + jnp.einsum(
                "rh,dh->rd",
                grad_values,
                w_qkv[layer_index, 2],
                precision=HIGHEST,
                preferred_element_type=jnp.float32,
            )

        grad_state = sum_grad(input_back_term, my_rows) + grad_one
        weight_grads[layer_index] = (grad_qkv, grad_out, grad_up, grad_down)
        bias_grads[layer_index] = (grad_bias_qv, grad_bias_up)
        shared_grads[layer_index] = (
            jnp.sum(grad_one, axis=0),
            jnp.stack([gain_one, gain_two]),
            jnp.stack([shift_one, shift_two]),
            jnp.sum(grad_two, axis=0),
        )
    stacked_weights = tuple(
        (
            jnp.stack([weight_grads[level][member] for level in range(layer_count)])
            for member in range(4)
        )
    )
    summed_qkv, summed_out, summed_up, summed_down = (
        lax.psum_scatter(stacked_weights[0], "dp", scatter_dimension=2, tiled=True),
        lax.psum_scatter(stacked_weights[1], "dp", scatter_dimension=2, tiled=True),
        lax.psum_scatter(stacked_weights[2], "dp", scatter_dimension=1, tiled=True),
        lax.psum_scatter(stacked_weights[3], "dp", scatter_dimension=2, tiled=True),
    )
    stacked_bias_qv = jnp.stack([bias_grads[level][0] for level in range(layer_count)])
    stacked_bias_up = jnp.stack([bias_grads[level][1] for level in range(layer_count)])
    summed_bias_qv, summed_bias_up = lax.psum((stacked_bias_qv, stacked_bias_up), "dp")
    stacked_shared = tuple(
        (
            jnp.stack([shared_grads[level][member] for level in range(layer_count)])
            for member in range(4)
        )
    )
    summed_bias_out, summed_gain, summed_shift, summed_bias_down = lax.psum(
        stacked_shared, ("dp", "tensor")
    )
    return (
        state,
        grad_state,
        summed_qkv,
        summed_bias_qv,
        summed_out,
        summed_bias_out,
        summed_gain,
        summed_shift,
        summed_up,
        summed_bias_up,
        summed_down,
        summed_bias_down,
    )


def solution(mesh):
    in_specs = (
        P(("dp", "tensor"), None),
        P(("dp", "tensor"), None),
        P("dp"),
        P(None, None, None, "tensor"),
        P(None, None, "tensor"),
        P(None, "tensor", None),
        P(),
        P(),
        P(),
        P(None, None, "tensor"),
        P(None, "tensor"),
        P(None, "tensor", None),
        P(),
    )
    out_specs = (
        P(("dp", "tensor"), None),
        P(("dp", "tensor"), None),
        P(None, None, "dp", "tensor"),
        P(None, None, "tensor"),
        P(None, "tensor", "dp"),
        P(),
        P(),
        P(),
        P(None, "dp", "tensor"),
        P(None, "tensor"),
        P(None, "tensor", "dp"),
        P(),
    )
    return jax.shard_map(local, mesh=mesh, in_specs=in_specs, out_specs=out_specs, check_vma=False)
```

profile of v0, /device:TPU:0, one launch (start us, length us, event | category | flops | bytes accessed | tf_op | source)
XLA Modules:
  0.0 1125.5 jit_solution(9122916788855121678)
XLA Ops:
  8.7 23.2 %all-gather.9.cloned.1.call-done = bf16[1024,768]{1,0:T(8,128)(2,1)} async-done(((bf16[256,768]{1,0:T(8,128)(2,1)}), bf16[1024,768]{1,0:T(8,128)(2,1)}) %all-gather.9.cloned.1.call-update) | async-done | bytes 1572880 | tf_op jit(solution)/shard_map/all_gather | solution.py:19
  38.0 23.0 %while.86 = (s32[]{:T(128)}, bf16[2,512,3,64]{1,3,2,0:T(8,128)(2,1)S(1)}, s32[2]{0:T(128)S(1)}, s32[]{:T(128)}, bf16[1024,3,64]{0,2,1:T(8,128)(2,1)S(1)}, /*inde...) while((s32[]{:T(128)}, ...), condition=%wide.region_3.4_spmd, body=%wide.region_0.3_spmd.sunk | while | flops 414289920 | bytes 14833859 | solution.py:103
  65.6 37.9 %reduce-scatter.16.cloned.1.call-done = f32[256,768]{1,0:T(8,128)} async-done(((f32[1024,768]{1,0:T(8,128)}), f32[256,768]{1,0:T(8,128)}) %reduce-scatter.16.cloned.1.call-update) | async-done | bytes 786448 | tf_op jit(solution)/shard_map/reduce_scatter | solution.py:23
  106.3 19.5 %all-gather.11.cloned.1.call-done = bf16[1024,768]{1,0:T(8,128)(2,1)} async-done(((bf16[256,768]{1,0:T(8,128)(2,1)}), bf16[1024,768]{1,0:T(8,128)(2,1)}) %all-gather.11.cloned.1.call-update) | async-done | bytes 1572880 | tf_op jit(solution)/shard_map/all_gather | solution.py:19
  125.8 11.6 %multiply_convert_fusion.1 = (bf16[1024,768]{1,0:T(8,128)(2,1)S(1)}, f32[1024,768]{1,0:T(8,128)}, f32[1024,768]{1,0:T(8,128)}) fusion(f32[768]{0:T(1024)S(1)} %get-tuple-element.421, bf16[1024,768]{1,0:T(8,128)(2,1)} %all-gather.11.cloned.1.call-done, bf16[2,768,768]{2,1,0:T(8,128)(2,1)} %param.30), kind=kOutput, calls=%fused_computation.170 | convolution fusion | flops 1259864064 | bytes 10619904 | tf_op jit(solution)/shard_map/dot_general | solution.py:235
  142.4 37.4 %reduce-scatter.18.cloned.1.call-done = f32[256,768]{1,0:T(8,128)} async-done(((f32[1024,768]{1,0:T(8,128)}), f32[256,768]{1,0:T(8,128)}) %reduce-scatter.18.cloned.1.call-update) | async-done | bytes 786448 | tf_op jit(solution)/shard_map/reduce_scatter | solution.py:23
  182.6 19.8 %all-gather.13.cloned.1.call-done = bf16[1024,768]{1,0:T(8,128)(2,1)} async-done(((bf16[256,768]{1,0:T(8,128)(2,1)}), bf16[1024,768]{1,0:T(8,128)(2,1)}) %all-gather.13.cloned.1.call-update) | async-done | bytes 1572880 | tf_op jit(solution)/shard_map/all_gather | solution.py:19
  209.2 24.9 %while.87 = (s32[]{:T(128)}, bf16[2,512,3,64]{1,3,2,0:T(8,128)(2,1)S(1)}, s32[2]{0:T(128)S(1)}, s32[]{:T(128)}, bf16[1024,3,64]{0,2,1:T(8,128)(2,1)}, /*index=5*...) while((s32[]{:T(128)}, ...), condition=%wide.region_13.14_spmd, body=%wide.region_10.13_spmd.sunk | while | flops 414289920 | bytes 14833859 | solution.py:103
  238.1 37.6 %reduce-scatter.20.cloned.1.call-done = f32[256,768]{1,0:T(8,128)} async-done(((f32[1024,768]{1,0:T(8,128)}), f32[256,768]{1,0:T(8,128)}) %reduce-scatter.20.cloned.1.call-update) | async-done | bytes 786448 | tf_op jit(solution)/shard_map/reduce_scatter | solution.py:23
  278.5 19.8 %all-gather.15.cloned.1.call-done = bf16[1024,768]{1,0:T(8,128)(2,1)} async-done(((bf16[256,768]{1,0:T(8,128)(2,1)}), bf16[1024,768]{1,0:T(8,128)(2,1)}) %all-gather.15.cloned.1.call-update) | async-done | bytes 1572880 | tf_op jit(solution)/shard_map/all_gather | solution.py:19
  298.2 11.5 %multiply_convert_fusion = (bf16[1024,768]{1,0:T(8,128)(2,1)S(1)}, f32[1024,768]{1,0:T(8,128)}, f32[1024,768]{1,0:T(8,128)}) fusion(f32[768]{0:T(1024)S(1)} %get-tuple-element.420, bf16[1024,768]{1,0:T(8,128)(2,1)} %all-gather.15.cloned.1.call-done, bf16[2,768,768]{2,1,0:T(8,128)(2,1)} %param.30), kind=kOutput, calls=%fused_computation.157 | convolution fusion | flops 1259864064 | bytes 10619904 | tf_op jit(solution)/shard_map/dot_general | solution.py:235
  314.0 38.0 %reduce-scatter.22.cloned.1.call-done = f32[256,768]{1,0:T(8,128)} async-done(((f32[1024,768]{1,0:T(8,128)}), f32[256,768]{1,0:T(8,128)}) %reduce-scatter.22.cloned.1.call-update) | async-done | bytes 786448 | tf_op jit(solution)/shard_map/reduce_scatter | solution.py:23
  357.4 19.8 %all-gather.17.cloned.1.call-done = bf16[1024,768]{1,0:T(8,128)(2,1)} async-done(((bf16[256,768]{1,0:T(8,128)(2,1)}), bf16[1024,768]{1,0:T(8,128)(2,1)}) %all-gather.17.cloned.1.call-update) | async-done | bytes 1572880 | tf_op jit(solution)/shard_map/all_gather | solution.py:32
  377.2 6.5 fusion.279
  391.3 38.1 %reduce-scatter.24.cloned.1.call-done = f32[256,768]{1,0:T(8,128)} async-done(((f32[1024,768]{1,0:T(8,128)}), f32[256,768]{1,0:T(8,128)}) %reduce-scatter.24.cloned.1.call-update) | async-done | bytes 786448 | tf_op jit(solution)/shard_map/reduce_scatter | solution.py:36
  435.1 18.8 %all-gather.19.cloned.1.call-done = bf16[1024,768]{1,0:T(8,128)(2,1)} async-done(((bf16[256,768]{1,0:T(8,128)(2,1)}), bf16[1024,768]{1,0:T(8,128)(2,1)}) %all-gather.19.cloned.1.call-update) | async-done | bytes 1572880 | tf_op jit(solution)/shard_map/all_gather | solution.py:32
  457.0 51.0 %while.88 = (s32[]{:T(128)}, f32[1024,3,64]{0,2,1:T(8,128)S(1)}, f32[1024,3,64]{0,2,1:T(8,128)S(1)}, f32[2,512,3,64]{1,3,2,0:T(8,128)S(1)}, s32[2]{0:T(128)S(1)}...) while((s32[]{:T(128)}, f32[1024,3,64]{0,2,1:T(8,128)S(1)}, ...), condition=%wide.region_29.30_spmd.clone, body=%wide.region_25.29_spmd.clone.sunk | while | flops 5059938816 | bytes 90376584 | solution.py:171
  459.6 6.1 fusion.406
  484.9 6.1 fusion.406
  517.8 38.0 %reduce-scatter.26.cloned.1.call-done = f32[256,768]{1,0:T(8,128)} async-done(((f32[1024,768]{1,0:T(8,128)}), f32[256,768]{1,0:T(8,128)}) %reduce-scatter.26.cloned.1.call-update) | async-done | bytes 786448 | tf_op jit(solution)/shard_map/reduce_scatter | solution.py:36
  560.1 19.4 %all-gather.21.cloned.1.call-done = bf16[1024,768]{1,0:T(8,128)(2,1)} async-done(((bf16[256,768]{1,0:T(8,128)(2,1)}), bf16[1024,768]{1,0:T(8,128)(2,1)}) %all-gather.21.cloned.1.call-update) | async-done | bytes 1572880 | tf_op jit(solution)/shard_map/all_gather | solution.py:32
  579.5 6.5 fusion.280
  593.6 38.0 %reduce-scatter.28.cloned.1.call-done = f32[256,768]{1,0:T(8,128)} async-done(((f32[1024,768]{1,0:T(8,128)}), f32[256,768]{1,0:T(8,128)}) %reduce-scatter.28.cloned.1.call-update) | async-done | bytes 786448 | tf_op jit(solution)/shard_map/reduce_scatter | solution.py:36
  643.4 8.2 copy.37
  669.0 50.6 %while.89 = (s32[]{:T(128)}, f32[1024,3,64]{0,2,1:T(8,128)}, f32[1024,3,64]{0,2,1:T(8,128)S(1)}, f32[2,512,3,64]{1,3,2,0:T(8,128)S(1)}, s32[2]{0:T(128)S(1)}, /*...) while((s32[]{:T(128)}, f32[1024,3,64]{0,2,1:T(8,128)}, ...), condition=%wide.region_40.41_spmd.clone, body=%wide.region_36.40_spmd.clone.sunk | while | flops 5059938816 | bytes 95097240 | solution.py:171
  743.2 8.0 reshape.422
  768.1 61.7 %all-reduce.5.cloned.1.call-done = f32[2,768,768]{1,0,2:T(2,128)} async-done(((f32[2,768,768]{1,0,2:T(2,128)}), f32[2,768,768]{1,0,2:T(2,128)}) %all-reduce.5.cloned.1.call-update) | async-done | bytes 4718608
  832.0 40.7 %all-reduce.1 = (f32[2,768]{1,0:T(2,128)}, f32[2,2,768]{2,1,0:T(2,128)}, f32[2,2,768]{2,1,0:T(2,128)}, f32[2,768]{1,0:T(2,128)}) all-reduce(f32[2,768]{1,0:T(2,128)S(1)} %pad_maximum_fusion.6, f32[2,2,768]{2,1,0:T(2,128)S(1)} %pad_maximum_fusion.4, ...), channel_id=1, replica_groups=mesh['dp'=8,'tensor'=4] {'dp','tensor'}, use_global_device_ids=true, to_apply=%region_51.52 | all-reduce | flops 9216 | bytes 73728 | tf_op jit(solution)/shard_map/psum | solution.py:408
  873.1 36.9 %all-reduce.2 = (f32[2,2,192]{2,1,0:T(2,128)}, f32[2,768]{1,0:T(2,128)}) all-reduce(f32[2,2,192]{2,1,0:T(2,128)S(1)} %pad_maximum_fusion.9, f32[2,768]{1,0:T(2,128)S(1)} %pad_maximum_fusion.7), channel_id=1, replica_groups=mesh['dp'=8,'tensor'=4] {'dp'}, use_global_device_ids=true, to_apply=%region_47.48 | all-reduce | flops 2304 | bytes 18432 | tf_op jit(solution)/shard_map/psum | solution.py:401
  911.9 24.4 %reduce-scatter.30.cloned.1.call-done = f32[256,768]{1,0:T(8,128)} async-done(((f32[1024,768]{1,0:T(8,128)}), f32[256,768]{1,0:T(8,128)}) %reduce-scatter.30.cloned.1.call-update) | async-done | bytes 786448 | tf_op jit(solution)/shard_map/reduce_scatter | solution.py:36
  938.5 80.7 %reduce-scatter.34.cloned.1.call-done = f32[96,1152]{1,0:T(8,128)} async-done(((f32[768,1152]{1,0:T(8,128)}), f32[96,1152]{1,0:T(8,128)}) %reduce-scatter.34.cloned.1.call-update) | async-done | bytes 442384
  1021.7 96.7 %reduce-scatter.32.cloned.1.call-done = f32[2,96,768]{2,1,0:T(8,128)} async-done(((f32[2,768,768]{2,1,0:T(8,128)}), f32[2,96,768]{2,1,0:T(8,128)}) %reduce-scatter.32.cloned.1.call-update) | async-done | bytes 589840 | tf_op jit(solution)/shard_map/reduce_scatter | solution.py:396
  (488 shorter events, 291.5 us)
Async XLA Ops:
  7.2 24.8 %all-gather.9.cloned.1.call-start = ((), (), s32[]{:S(2)}) async-start(), calls=%async_computation.11 | async-start | bytes 1966080 | tf_op jit(solution)/shard_map/all_gather | solution.py:19
  7.9 95.5 %reduce-scatter.16.cloned.1.call-start = ((), (), s32[]{:S(2)}) async-start(), calls=%async_computation.12 | async-start | bytes 3932160 | tf_op jit(solution)/shard_map/reduce_scatter | solution.py:23
  65.4 60.5 %all-gather.11.cloned.1.call-start = ((), (), s32[]{:S(2)}) async-start(), calls=%async_computation.13 | async-start | bytes 1966080 | tf_op jit(solution)/shard_map/all_gather | solution.py:19
  65.5 114.3 %copy-start.50 = (f32[768]{0:T(1024)}, f32[768]{0:T(1024)S(1)}, u32[]{:S(2)}) copy-start(f32[768]{0:T(1024)S(1)} %get-tuple-element.555) | copy-start | bytes 9220
  65.6 210.1 %copy-start.52 = (f32[768]{0:T(1024)}, f32[768]{0:T(1024)S(1)}, u32[]{:S(2)}) copy-start(f32[768]{0:T(1024)S(1)} %get-tuple-element.556) | copy-start | bytes 9220
  104.8 75.1 %copy-start = (f32[256,768]{1,0:T(8,128)}, f32[256,768]{1,0:T(8,128)S(1)}, u32[]{:S(2)}) copy-start(f32[256,768]{1,0:T(8,128)S(1)} %get-tuple-element.520) | copy-start | bytes 2359300
  104.8 75.1 %copy-start.54 = (f32[256]{0:T(256)}, f32[256]{0:T(256)S(1)}, u32[]{:S(2)}) copy-start(f32[256]{0:T(256)S(1)} %broadcast_multiply_fusion.11) | copy-start | bytes 3076
  105.0 74.8 %copy-start.58 = (f32[256]{0:T(256)}, f32[256]{0:T(256)S(1)}, u32[]{:S(2)}) copy-start(f32[256]{0:T(256)S(1)} %add_rsqrt_fusion.3) | copy-start | bytes 3076
  106.0 73.9 %reduce-scatter.18.cloned.1.call-start = ((), (), s32[]{:S(2)}) async-start(), calls=%async_computation.14 | async-start | bytes 3932160 | tf_op jit(solution)/shard_map/reduce_scatter | solution.py:23
  141.7 60.7 %all-gather.13.cloned.1.call-start = ((), (), s32[]{:S(2)}) async-start(), calls=%async_computation.15 | async-start | bytes 1966080 | tf_op jit(solution)/shard_map/all_gather | solution.py:19
  181.3 94.3 %copy-start.2 = (f32[256,768]{1,0:T(8,128)}, f32[256,768]{1,0:T(8,128)S(1)}, u32[]{:S(2)}) copy-start(f32[256,768]{1,0:T(8,128)S(1)} %get-tuple-element.516) | copy-start | bytes 2359300
  181.4 94.3 %copy-start.56 = (f32[256]{0:T(256)}, f32[256]{0:T(256)S(1)}, u32[]{:S(2)}) copy-start(f32[256]{0:T(256)S(1)} %broadcast_multiply_fusion.10) | copy-start | bytes 3076
  181.6 94.1 %copy-start.60 = (f32[256]{0:T(256)}, f32[256]{0:T(256)S(1)}, u32[]{:S(2)}) copy-start(f32[256]{0:T(256)S(1)} %add_rsqrt_fusion.2) | copy-start | bytes 3076
  182.6 93.1 %reduce-scatter.20.cloned.1.call-start = ((), (), s32[]{:S(2)}) async-start(), calls=%async_computation.16 | async-start | bytes 3932160 | tf_op jit(solution)/shard_map/reduce_scatter | solution.py:23
  237.6 60.6 %all-gather.15.cloned.1.call-start = ((), (), s32[]{:S(2)}) async-start(), calls=%async_computation.17 | async-start | bytes 1966080 | tf_op jit(solution)/shard_map/all_gather | solution.py:19
  278.4 73.7 %reduce-scatter.22.cloned.1.call-start = ((), (), s32[]{:S(2)}) async-start(), calls=%async_computation.18 | async-start | bytes 3932160 | tf_op jit(solution)/shard_map/reduce_scatter | solution.py:23
  314.0 63.2 %all-gather.17.cloned.1.call-start = ((), (), s32[]{:S(2)}) async-start(), calls=%async_computation.19 | async-start | bytes 1966080 | tf_op jit(solution)/shard_map/all_gather | solution.py:32
  357.4 72.0 %reduce-scatter.24.cloned.1.call-start = ((), (), s32[]{:S(2)}) async-start(), calls=%async_computation.20 | async-start | bytes 3932160 | tf_op jit(solution)/shard_map/reduce_scatter | solution.py:36
  391.3 62.7 %all-gather.19.cloned.1.call-start = ((), (), s32[]{:S(2)}) async-start(), calls=%async_computation.21 | async-start | bytes 1966080 | tf_op jit(solution)/shard_map/all_gather | solution.py:32
  434.1 121.7 %reduce-scatter.26.cloned.1.call-start = ((), (), s32[]{:S(2)}) async-start(), calls=%async_computation.22 | async-start | bytes 3932160 | tf_op jit(solution)/shard_map/reduce_scatter | solution.py:36
  517.7 61.8 %all-gather.21.cloned.1.call-start = ((), (), s32[]{:S(2)}) async-start(), calls=%async_computation.23 | async-start | bytes 1966080 | tf_op jit(solution)/shard_map/all_gather | solution.py:32
  559.7 72.0 %reduce-scatter.28.cloned.1.call-start = ((), (), s32[]{:S(2)}) async-start(), calls=%async_computation.24 | async-start | bytes 3932160 | tf_op jit(solution)/shard_map/reduce_scatter | solution.py:36
  593.6 62.7 %all-gather.23.cloned.1.call-start = ((), (), s32[]{:S(2)}) async-start(), calls=%async_computation.25 | async-start | bytes 1966080 | tf_op jit(solution)/shard_map/all_gather | solution.py:32
  636.5 193.4 %all-reduce.5.cloned.1.call-start = ((), (), s32[]{:S(2)}) async-start(), calls=%async_computation.30 | async-start | bytes 9437184
  651.7 258.3 %reduce-scatter.36.cloned.1.call-start = ((), (), s32[]{:S(2)}) async-start(), calls=%async_computation.29 | async-start | bytes 1327104
  667.2 269.2 %reduce-scatter.30.cloned.1.call-start = ((), (), s32[]{:S(2)}) async-start(), calls=%async_computation.26 | async-start | bytes 3932160 | tf_op jit(solution)/shard_map/reduce_scatter | solution.py:36
  729.1 290.0 %reduce-scatter.34.cloned.1.call-start = ((), (), s32[]{:S(2)}) async-start(), calls=%async_computation.28 | async-start | bytes 3981312
  751.2 367.2 %reduce-scatter.32.cloned.1.call-start = ((), (), s32[]{:S(2)}) async-start(), calls=%async_computation.27 | async-start | bytes 5308416 | tf_op jit(solution)/shard_map/reduce_scatter | solution.py:396
  765.6 66.2 %copy-start.71 = (f32[768]{0:T(1024)S(1)}, f32[768]{0:T(1024)}, u32[]{:S(2)}) copy-start(f32[768]{0:T(1024)} %get-tuple-element.405) | copy-start | bytes 9220
  765.6 107.1 %copy-start.19 = (f32[2,512,3,64]{1,3,2,0:T(8,128)S(1)}, f32[2,512,3,64]{1,3,2,0:T(8,128)}, u32[]{:S(2)}) copy-start(f32[2,512,3,64]{1,3,2,0:T(8,128)} %copy-done.18) | copy-start | bytes 2359300
  765.6 107.3 %copy-start.12 = (f32[1024,3,64]{0,2,1:T(8,128)S(1)}, f32[1024,3,64]{0,2,1:T(8,128)}, u32[]{:S(2)}) copy-start(f32[1024,3,64]{0,2,1:T(8,128)} %copy-done.10) | copy-start | bytes 2359300
  767.7 168.7 %copy-start.21 = (f32[256,768]{1,0:T(8,128)S(1)}, f32[256,768]{1,0:T(8,128)}, u32[]{:S(2)}) copy-start(f32[256,768]{1,0:T(8,128)} %copy-done.20) | copy-start | bytes 2359300
  (104 other events, 1058.6 us)
Sparse Core Ops, SparseCore 0:
  9.6 22.3 all-gather.8
  65.5 37.9 reduce-scatter.15
  106.1 19.6 all-gather.10
  141.9 37.9 reduce-scatter.17
  182.7 19.6 all-gather.12
  237.7 37.9 reduce-scatter.19
  278.5 19.6 all-gather.14
  314.1 37.9 reduce-scatter.21
  357.5 19.6 all-gather.16
  391.4 37.9 reduce-scatter.23
  434.2 19.6 all-gather.18
  517.8 37.9 reduce-scatter.25
  559.8 19.6 all-gather.20
  593.7 37.9 reduce-scatter.27
  636.6 19.6 all-gather.22
  660.2 169.6 all-reduce.4
  833.5 63.2 reduce-scatter.35
  899.3 36.9 reduce-scatter.29
  940.0 79.0 reduce-scatter.33
  1023.2 95.1 reduce-scatter.31
where the time goes:
time: 1130 us
  waiting for transfers between devices  672 us (59%)
  matrix products  242 us (21%)
  blocking collectives  77.6 us (7%)
  local copies, waits for them, and re-layouts  63.5 us (6%)
  other arithmetic  45.1 us (4%)
  between operations  16.6 us (1%)
    reduce_scatter x4, waiting for transfers between devices, sum_rows(): lax.psum_scatter(term_fn(jnp.int32(0), lax.axis_size('tensor') * row_coun...  151 us
    unnamed x23, waiting for transfers between devices  143 us
    reduce_scatter x4, waiting for transfers between devices, sum_grad(): lax.psum_scatter(term_fn(jnp.int32(0), lax.axis_size('tensor') * row_coun...  139 us
    reduce_scatter x1, waiting for transfers between devices, local(): lax.psum_scatter(stacked_weights[2], 'dp', scatter_dimension=1, tiled=True)  96.7 us
    all_gather x4, waiting for transfers between devices, gather_rows(): return lax.all_gather(values_in, 'tensor', axis=0, tiled=True)  82.3 us
    all_gather x4, waiting for transfers between devices, gather_grad(): return lax.all_gather(values_in, 'tensor', axis=0, tiled=True)  59.8 us
    unnamed x203, local copies, waits for them, and re-layouts  45.9 us
    sub x8, matrix products, probabilities(): expo = jnp.exp(scores - row_max)  45.9 us
  transfers between devices with their start and end apart: 20, of which 19 were waited for; matrix products, arithmetic and copies ran while one was open for 12% of the time, Pallas kernels for 0%

commit v1 on v0

--- a/solution.py
+++ b/solution.py
@@ -4,15 +4,431 @@
 import jax
 import jax.numpy as jnp
 from jax import lax
+from jax.experimental import pallas as pl
+from jax.experimental.pallas import tpu as pltpu
 from jax.sharding import PartitionSpec as P
 
 HDIM = 64
 LEN = 1024
 MEM = 10
-
-
+LANES = 128
+GROUP = 4
+PIECES = 2
 EPSILON = 1e-06
+VMEM_BYTES = 56 * 1024 * 1024
 HIGHEST = lax.Precision.HIGHEST
+MESH = pl.DeviceIdType.MESH
+F32 = jnp.float32
+BF16 = jnp.bfloat16
+VM = pl.BlockSpec(memory_space=pltpu.VMEM)
+SM = pl.BlockSpec(memory_space=pltpu.SMEM)
+
+
+def dot(left, right):
+    return jnp.dot(left, right, preferred_element_type=F32)
+
+
+def dot_nt(left, right):
+    return lax.dot_general(left, right, (((1,), (1,)), ((), ())), preferred_element_type=F32)
+
+
+def remote(src, dst, send_sem, recv_sem, tensor_index):
+    return pltpu.make_async_remote_copy(
+        src_ref=src,
+        dst_ref=dst,
+        send_sem=send_sem,
+        recv_sem=recv_sem,
+        device_id={"tensor": tensor_index},
+        device_id_type=MESH,
+    )
+
+
+def places():
+    mine = lax.axis_index("tensor")
+    chip = mine // 2
+    core = mine - 2 * chip
+    partner = mine + 1 - 2 * core
+    across = mine + 2 - 4 * chip
+    diagonal = across + 1 - 2 * core
+    return mine, partner, across, diagonal
+
+
+def group_barrier(others):
+    barrier = pltpu.get_barrier_semaphore()
+    for other in others:
+        pl.semaphore_signal(barrier, inc=1, device_id={"tensor": other}, device_id_type=MESH)
+    pl.semaphore_wait(barrier, len(others))
+
+
+class Gather:
+    def __init__(self, whole, send_sems, recv_sems):
+        self.whole = whole
+        self.mine, self.partner, self.across, self.diagonal = places()
+        self.rows = whole.shape[1] // PIECES
+        self.send_sems, self.recv_sems = send_sems, recv_sems
+
+    def piece(self, chunk, part):
+        return self.whole.at[chunk, pl.ds(part * self.rows, self.rows)]
+
+    def to_partner(self):
+        return remote(
+            self.whole.at[self.mine], self.whole.at[self.mine],
+            self.send_sems.at[0], self.recv_sems.at[0], self.partner,
+        )
+
+    def to_across(self, part):
+        return remote(
+            self.piece(self.mine, part), self.piece(self.mine, part),
+            self.send_sems.at[1 + part], self.recv_sems.at[1 + part], self.across,
+        )
+
+    def onward(self, part):
+        return remote(
+            self.piece(self.across, part), self.piece(self.across, part),
+            self.send_sems.at[1 + PIECES + part], self.recv_sems.at[1 + PIECES + part], self.partner,
+        )
+
+    def start(self):
+        for part in range(PIECES):
+            self.to_across(part).start()
+        self.to_partner().start()
+
+    def wait_partner(self):
+        remote(
+            self.whole.at[self.partner], self.whole.at[self.partner],
+            self.send_sems.at[0], self.recv_sems.at[0], self.partner,
+        ).wait_recv()
+
+    def wait_across(self, part):
+        remote(
+            self.piece(self.across, part), self.piece(self.across, part),
+            self.send_sems.at[1 + part], self.recv_sems.at[1 + part], self.across,
+        ).wait_recv()
+
+    def wait_diagonal(self, part):
+        remote(
+            self.piece(self.diagonal, part), self.piece(self.diagonal, part),
+            self.send_sems.at[1 + PIECES + part], self.recv_sems.at[1 + PIECES + part], self.partner,
+        ).wait_recv()
+
+    def wait_sends(self):
+        self.to_partner().wait_send()
+        for part in range(PIECES):
+            self.to_across(part).wait_send()
+            self.onward(part).wait_send()
+
+
+GATHER_SEMS = 1 + 2 * PIECES
+
+
+def layer_norm(total, gain, shift):
+    row_mean = jnp.mean(total, axis=-1, keepdims=True)
+    centered = total - row_mean
+    spread = jnp.mean(centered * centered, axis=-1, keepdims=True)
+    recip = lax.rsqrt(spread + EPSILON)
+    normal = centered * recip
+    return normal * gain + shift, normal, recip
+
+
+def visible_keys(chunk, rows):
+    first, last = chunk * rows, (chunk + 1) * rows - 1
+    if first < MEM or last >= LEN - MEM:
+        return LEN
+    return max(last + 1, LEN // 2)
+
+
+def query_limits(chunk, rows, prefix_len):
+    spots = chunk * rows + lax.broadcasted_iota(jnp.int32, (1, rows), 1)
+    limits = jnp.maximum(spots, prefix_len - 1)
+    return jnp.where((spots < MEM) | (spots >= LEN - MEM), LEN - 1, limits)
+
+
+def attention_forward_kernel(
+    state_ref, low_ref, wqkv_ref, bias_ref, wout_ref, bias_out_ref, gain_ref, shift_ref, prefix_ref,
+    next_ref, next_low_ref, normal_ref, recip_ref, whole_ref, qt_ref, q2_ref, kz_ref, kt_ref,
+    v2_ref, ct_ref, stats_ref,
+    vt_ref, cf_ref, wo_ref,
+    g_send, g_recv, c_send, c_recv, w_send, w_recv,
+):
+    mine, partner, across, diagonal = places()
+    rows = low_ref.shape[0]
+    heads = qt_ref.shape[0]
+    group_barrier((partner, across, diagonal))
+    gather = Gather(whole_ref, g_send, g_recv)
+    whole_ref[mine] = low_ref[...]
+    gather.start()
+    wo_ref[mine] = wout_ref[...]
+    lane_low = lax.broadcasted_iota(jnp.int32, (rows, LANES), 1) < HDIM
+
+    def project(chunk):
+        spots = pl.ds(pl.multiple_of(chunk * rows, rows), rows)
+        values = whole_ref[chunk]
+        for head in range(heads):
+            def part(kind):
+                columns = pl.ds((kind * heads + head) * LANES, LANES)
+                return dot(values, wqkv_ref[:, columns]) + bias_ref[:, columns]
+            query, key, value = part(0), part(1), part(2)
+            q2_ref[head, spots] = query.astype(BF16)
+            qt_ref[head, :, spots] = query.T.astype(BF16)
+            kz_ref[head, spots] = jnp.where(lane_low, key, 0.0).astype(BF16)
+            kt_ref[head, :, spots] = key.T.astype(BF16)
+            v2_ref[head, spots] = value.astype(BF16)
+            vt_ref[head, :, spots] = value.T[:HDIM].astype(BF16)
+
+    def wout_to_partner(source):
+        slot = 0 if source is mine else 2
+        return remote(wo_ref.at[source], wo_ref.at[source], w_send.at[slot], w_recv.at[slot], partner)
+
+    wout_to_across = remote(wo_ref.at[mine], wo_ref.at[mine], w_send.at[1], w_recv.at[1], across)
+    wout_from_across = remote(wo_ref.at[across], wo_ref.at[across], w_send.at[1], w_recv.at[1], across)
+    wout_from_partner = remote(wo_ref.at[partner], wo_ref.at[partner], w_send.at[0], w_recv.at[0], partner)
+    wout_from_diagonal = remote(wo_ref.at[diagonal], wo_ref.at[diagonal], w_send.at[2], w_recv.at[2], partner)
+
+    project(mine)
+    gather.wait_partner()
+    project(partner)
+    for part in range(PIECES):
+        gather.wait_across(part)
+        gather.onward(part).start()
+    wout_to_across.start()
+    wout_to_partner(mine).start()
+    project(across)
+    for part in range(PIECES):
+        gather.wait_diagonal(part)
+    project(diagonal)
+
+    def context_copy(step, chunk):
+        return remote(ct_ref.at[chunk], cf_ref.at[mine], c_send.at[step], c_recv.at[step], chunk)
+
+    def context_from(step, chunk):
+        return remote(ct_ref.at[mine], cf_ref.at[chunk], c_send.at[step], c_recv.at[step], chunk)
+
+    def attend(chunk):
+        keys = visible_keys(chunk, rows)
+        limits = query_limits(chunk, rows, prefix_ref[0])
+        visible = lax.broadcasted_iota(jnp.int32, (keys, rows), 0) <= limits
+        spots = pl.ds(chunk * rows, rows)
+
+        def one_head(head, carry):
+            scores = dot(kz_ref[head, pl.ds(0, keys)], qt_ref[head, :, spots])
+            scores = jnp.where(visible, scores, -1e30)
+            top = jnp.max(scores, axis=0, keepdims=True)
+            expo = jnp.exp(scores - top)
+            recip = 1.0 / jnp.sum(expo, axis=0, keepdims=True)
+            probs = (expo * recip).astype(BF16)
+            context = dot(vt_ref[head, :, pl.ds(0, keys)], probs)
+            ct_ref[chunk, pl.ds(pl.multiple_of(head * HDIM, HDIM), HDIM)] = context.astype(BF16)
+            first = lax.broadcasted_iota(jnp.int32, (8, rows), 0) == 0
+            stats_ref[head, :, spots] = jnp.where(first, top, recip)
+            return carry
+
+        lax.fori_loop(0, heads, one_head, 0)
+
+    chip, core = mine // 2, mine - 2 * (mine // 2)
+
+    def step_chunk(step):
+        near = step // 2
+        flip = lax.rem(lax.rem(step, 2) + near, 2)
+        to_chip = (1 - near) * (1 - chip) + near * chip
+        return 2 * to_chip + core + flip * (1 - 2 * core)
+
+    def one_step(step, carry):
+        chunk = step_chunk(step)
+        for each in range(GROUP):
+            @pl.when(chunk == each)
+            def _():
+                attend(each)
+
+        @pl.when(step < 3)
+        def _():
+            context_copy(step, chunk).start()
+
+        @pl.when(step == 1)
+        def _():
+            wout_from_across.wait_recv()
+            wout_to_partner(across).start()
+        return carry
+
+    lax.fori_loop(0, GROUP, one_step, 0)
+    cf_ref[mine] = ct_ref[mine]
+    wout_from_partner.wait_recv()
+    wout_from_diagonal.wait_recv()
+    for step, chunk in enumerate((across, diagonal, partner)):
+        context_from(step, chunk).wait_recv()
+    depth = GROUP * wout_ref.shape[0]
+    context = cf_ref[...].reshape(depth, rows).astype(F32).T.astype(BF16)
+    total = state_ref[...] + dot(context, wo_ref[...].reshape(depth, -1)) + bias_out_ref[...]
+    result, normal, recip = layer_norm(total, gain_ref[...], shift_ref[...])
+    next_ref[...] = result
+    next_low_ref[...] = result.astype(BF16)
+    normal_ref[...] = normal
+    recip_ref[...] = jnp.broadcast_to(recip, recip_ref.shape)
+    gather.wait_sends()
+    wout_to_across.wait_send()
+    wout_to_partner(mine).wait_send()
+    wout_to_partner(across).wait_send()
+    for step, chunk in enumerate((across, diagonal, partner)):
+        context_copy(step, chunk).wait_send()
+
+
+def shape(dims, kind=F32):
+    return jax.ShapeDtypeStruct(dims, kind)
+
+
+def dma_sems(count):
+    return pltpu.SemaphoreType.DMA((count,))
+
+
+def params(collective_id):
+    return pltpu.CompilerParams(
+        collective_id=collective_id, has_side_effects=True, vmem_limit_bytes=VMEM_BYTES
+    )
+
+
+def attention_layer(state, low, wqkv, bias, wout, bias_out, gain, shift, prefix):
+    rows, width = low.shape
+    depth = wout.shape[0]
+    heads = depth // HDIM
+    tall = GROUP * rows
+    return pl.pallas_call(
+        attention_forward_kernel,
+        out_shape=(
+            shape((rows, width)), shape((rows, width), BF16), shape((rows, width)),
+            shape((rows, LANES)), shape((GROUP, rows, width), BF16),
+            shape((heads, LANES, tall), BF16), shape((heads, tall, LANES), BF16),
+            shape((heads, tall, LANES), BF16), shape((heads, LANES, tall), BF16),
+            shape((heads, tall, LANES), BF16), shape((GROUP, depth, rows), BF16),
+            shape((heads, 8, tall)),
+        ),
+        in_specs=[VM] * 8 + [SM],
+        out_specs=(VM,) * 12,
+        scratch_shapes=[
+            pltpu.VMEM((heads, HDIM, tall), BF16),
+            pltpu.VMEM((GROUP, depth, rows), BF16),
+            pltpu.VMEM((GROUP, depth, width), BF16),
+            dma_sems(GATHER_SEMS), dma_sems(GATHER_SEMS),
+            dma_sems(3), dma_sems(3), dma_sems(3), dma_sems(3),
+        ],
+        compiler_params=params(1),
+        name="attention_fwd",
+    )(state, low, wqkv, bias, wout, bias_out, gain, shift, prefix)
+
+
+def ffn_forward_kernel(
+    state_ref, low_ref, wup_ref, bias_up_ref, wdown_ref, bias_down_ref, gain_ref, shift_ref,
+    next_ref, next_low_ref, normal_ref, recip_ref, whole_ref, active_ref, slope_ref,
+    terms_ref, near_ref, relay_ref, sum_ref, far_ref,
+    g_send, g_recv, n_send, n_recv, r_send, r_recv, f_send, f_recv,
+):
+    mine, partner, across, diagonal = places()
+    rows = low_ref.shape[0]
+    part_rows = rows // PIECES
+    group_barrier((partner, across, diagonal))
+    gather = Gather(whole_ref, g_send, g_recv)
+    whole_ref[mine] = low_ref[...]
+    gather.start()
+
+    def spot(part):
+        return pl.ds(part * part_rows, part_rows)
+
+    def units(chunk, part):
+        hidden = dot(whole_ref[chunk, spot(part)], wup_ref[...]) + bias_up_ref[...]
+        below = 0.5 * (1.0 + lax.erf(hidden * math.sqrt(0.5)))
+        density = jnp.exp(-0.5 * hidden * hidden) * (1.0 / math.sqrt(2.0 * math.pi))
+        active = (hidden * below).astype(BF16)
+        active_ref[chunk, spot(part)] = active
+        slope_ref[chunk, spot(part)] = below + hidden * density
+        terms_ref[chunk, spot(part)] = dot(active, wdown_ref[...])
+
+    def near_copy(part):
+        return remote(
+            terms_ref.at[partner, spot(part)], near_ref.at[spot(part)],
+            n_send.at[part], n_recv.at[part], partner,
+        )
+
+    def relay_copy(part):
+        return remote(
+            terms_ref.at[diagonal, spot(part)], relay_ref.at[spot(part)],
+            r_send.at[part], r_recv.at[part], partner,
+        )
+
+    def far_copy(part):
+        return remote(
+            sum_ref.at[spot(part)], far_ref.at[spot(part)], f_send.at[part], f_recv.at[part], across
+        )
+
+    def pass_on(part):
+        relay_copy(part).wait_recv()
+        sum_ref[spot(part)] = terms_ref[across, spot(part)] + relay_ref[spot(part)]
+        far_copy(part).start()
+
+    for part in range(PIECES):
+        units(mine, part)
+    for part in range(PIECES):
+        gather.wait_across(part)
+        gather.onward(part).start()
+        units(across, part)
+        gather.wait_diagonal(part)
+        units(diagonal, part)
+        relay_copy(part).start()
+        if part > 0:
+            pass_on(part - 1)
+    gather.wait_partner()
+    units(partner, 0)
+    near_copy(0).start()
+    pass_on(PIECES - 1)
+    for part in range(1, PIECES):
+        units(partner, part)
+        near_copy(part).start()
+    for part in range(PIECES):
+        near_copy(part).wait_recv()
+        far_copy(part).wait_recv()
+        total = (
+            state_ref[spot(part)]
+            + ((terms_ref[mine, spot(part)] + near_ref[spot(part)]) + far_ref[spot(part)])
+            + bias_down_ref[...]
+        )
+        result, normal, recip = layer_norm(total, gain_ref[...], shift_ref[...])
+        next_ref[spot(part)] = result
+        next_low_ref[spot(part)] = result.astype(BF16)
+        normal_ref[spot(part)] = normal
+        recip_ref[spot(part)] = jnp.broadcast_to(recip, (part_rows, LANES))
+    gather.wait_sends()
+    for part in range(PIECES):
+        near_copy(part).wait_send()
+        relay_copy(part).wait_send()
+        far_copy(part).wait_send()
+
+
+def ffn_layer(state, low, wup, bias_up, wdown, bias_down, gain, shift):
+    rows, width = low.shape
+    units = wup.shape[1]
+    return pl.pallas_call(
+        ffn_forward_kernel,
+        out_shape=(
+            shape((rows, width)), shape((rows, width), BF16), shape((rows, width)),
+            shape((rows, LANES)), shape((GROUP, rows, width), BF16),
+            shape((GROUP, rows, units), BF16), shape((GROUP, rows, units)),
+        ),
+        in_specs=[VM] * 8,
+        out_specs=(VM,) * 7,
+        scratch_shapes=[
+            pltpu.VMEM((GROUP, rows, width), F32),
+            pltpu.VMEM((rows, width), F32), pltpu.VMEM((rows, width), F32),
+            pltpu.VMEM((rows, width), F32), pltpu.VMEM((rows, width), F32),
+            dma_sems(GATHER_SEMS), dma_sems(GATHER_SEMS),
+            dma_sems(PIECES), dma_sems(PIECES), dma_sems(PIECES), dma_sems(PIECES),
+            dma_sems(PIECES), dma_sems(PIECES),
+        ],
+        compiler_params=params(2),
+        name="ffn_fwd",
+    )(state, low, wup, bias_up, wdown, bias_down, gain, shift)
+
+
+def doubled(values, heads):
+    lead = values.shape[:-1]
+    split = values.reshape(lead + (heads, 1, HDIM))
+    return jnp.broadcast_to(split, lead + (heads, 2, HDIM)).reshape(lead + (heads * LANES,))
 
 
 def gather_rows(values_in):
@@ -41,7 +457,7 @@
     )
 
 
-def normalize(total, gain, shift):
+def normalize_unused(total, gain, shift):
     row_mean = jnp.mean(total, axis=-1, keepdims=True)
     centered = total - row_mean
     spread = jnp.mean(centered * centered, axis=-1, keepdims=True)
@@ -204,62 +620,43 @@
 ):
     my_rows = tokens.shape[0]
     layer_count = w_qkv.shape[0]
-    state = tokens.astype(jnp.float32)
+    state = tokens.astype(F32)
+    low = tokens
+    depth = w_out.shape[1]
+    heads = depth // HDIM
+    scale = jnp.array([1.0 / math.sqrt(HDIM), 1.0, 1.0], BF16).reshape(1, 3, 1, 1)
+    wqkv = doubled(w_qkv * scale, heads)
+    wqkv = jnp.moveaxis(wqkv, 1, 2).reshape(layer_count, w_qkv.shape[2], -1)
+    bias3 = jnp.stack(
+        [bias_qv[:, 0] * (1.0 / math.sqrt(HDIM)), jnp.zeros_like(bias_qv[:, 0]), bias_qv[:, 1]], axis=1
+    )
+    bias3 = doubled(bias3, heads).reshape(layer_count, 1, -1)
     stored = []
     for layer_index in range(layer_count):
-        input_whole = gather_rows(state.astype(jnp.bfloat16))
-        query = (
-            jnp.dot(input_whole, w_qkv[layer_index, 0], preferred_element_type=jnp.float32)
-            + bias_qv[layer_index, 0]
-        ).astype(jnp.bfloat16)
-        keys = jnp.dot(
-            input_whole, w_qkv[layer_index, 1], preferred_element_type=jnp.float32
-        ).astype(jnp.bfloat16)
-        values = (
-            jnp.dot(input_whole, w_qkv[layer_index, 2], preferred_element_type=jnp.float32)
-            + bias_qv[layer_index, 1]
-        ).astype(jnp.bfloat16)
-        context = attention_forward(query, keys, values, prefix)
-
-        def attn_term(row_start, row_count):
-            return jnp.dot(context, w_out[layer_index], preferred_element_type=jnp.float32)
-
-        attn_share = sum_rows(attn_term, my_rows)
-        normed, normal_one, recip_one = normalize(
-            state + attn_share + bias_out[layer_index],
-            norm_gain[layer_index, 0],
-            norm_bias[layer_index, 0],
-        )
-        normed_whole = gather_rows(normed.astype(jnp.bfloat16))
-        hidden = (
-            jnp.dot(normed_whole, w_up[layer_index], preferred_element_type=jnp.float32)
-            + bias_up[layer_index]
-        )
-        active = jax.nn.gelu(hidden, approximate=False).astype(jnp.bfloat16)
-
-        def ffn_term(row_start, row_count):
-            return jnp.dot(active, w_down[layer_index], preferred_element_type=jnp.float32)
-
-        ffn_share = sum_rows(ffn_term, my_rows)
-        state, normal_two, recip_two = normalize(
-            normed + ffn_share + bias_down[layer_index],
-            norm_gain[layer_index, 1],
-            norm_bias[layer_index, 1],
-        )
+        (
+            state, low, normal_one, recip_one, input_whole, qt, q2, kz, kt, v2, ct, stats,
+        ) = attention_layer(
+            state, low, wqkv[layer_index], bias3[layer_index], w_out[layer_index],
+            bias_out[layer_index][None], norm_gain[layer_index, 0][None],
+            norm_bias[layer_index, 0][None], prefix,
+        )
+        (
+            state, low, normal_two, recip_two, normed_whole, active, slope,
+        ) = ffn_layer(
+            state, low, w_up[layer_index], bias_up[layer_index][None], w_down[layer_index],
+            bias_down[layer_index][None], norm_gain[layer_index, 1][None],
+            norm_bias[layer_index, 1][None],
+        )
+        total = GROUP * my_rows
+        input_whole = input_whole.reshape(total, -1)
+        normed_whole = normed_whole.reshape(total, -1)
+        pick = lambda v: jnp.moveaxis(v[:, :, :HDIM], 0, 1).reshape(total, depth)
         stored.append(
             (
-                input_whole,
-                query,
-                keys,
-                values,
-                context,
-                normal_one,
-                recip_one,
-                normed_whole,
-                hidden,
-                active,
-                normal_two,
-                recip_two,
+                input_whole, pick(q2) * 8, pick(kz), pick(v2),
+                jnp.moveaxis(ct, 1, 2).reshape(total, depth), normal_one, recip_one[:, :1],
+                normed_whole, slope.reshape(total, -1), active.reshape(total, -1), normal_two,
+                recip_two[:, :1],
             )
         )
     grad_state = cotangent.astype(jnp.float32)
@@ -291,8 +688,7 @@
         grad_active = jnp.einsum(
             "rd,fd->rf", ffn_grad_whole, w_down[layer_index], preferred_element_type=jnp.float32
         )
-        _, gelu_pull = jax.vjp(functools.partial(jax.nn.gelu, approximate=False), hidden)
-        grad_hidden = gelu_pull(grad_active)[0]
+        grad_hidden = grad_active * hidden
         grad_up = jnp.einsum(
             "rd,rf->df",
             normed_whole,

time: 1130 us -> 954 us (0.84)
  waiting for transfers between devices: 672 us -> 425 us
  Pallas kernels: 0 us -> 140 us
  matrix products: 242 us -> 153 us
  local copies, waits for them, and re-layouts: 63.5 us -> 92.1 us
    reduce_scatter x4 -> x0, waiting for transfers between devices: 151 us -> none  [sum_rows(): lax.psum_scatter(term_fn(jnp.int32(0), lax.axis_size('tensor') * row_coun...]
    pallas_call x0 -> x4, Pallas kernels: none -> 140 us  [the longest x2 75.1 us: ffn_layer(): pl.pallas_call(ffn_forward_kernel, out_shape=(shape((rows, width)), shape...]
    all_gather x4 -> x0, waiting for transfers between devices: 82.3 us -> none  [gather_rows(): return lax.all_gather(values_in, 'tensor', axis=0, tiled=True)]
    dot_general x16 -> x0, matrix products: 62.2 us -> none  [the longest x2 23.1 us: local(): jnp.dot(normed_whole, w_up[layer_index], preferred_element_type=jnp.float32)]
    sub x8 -> x4, matrix products: 45.9 us -> 24.2 us  [probabilities(): expo = jnp.exp(scores - row_max)]
    squeeze x0 -> x6, local copies, waits for them, and re-layouts: none -> 15.2 us  [the longest x2 6.23 us: local(): wqkv[layer_index]]
    unnamed x203 -> x162, local copies, waits for them, and re-layouts: 45.9 us -> 52.1 us
    unnamed x23 -> x15, waiting for transfers between devices: 143 us -> 139 us
  transfers between devices with their start and end apart: 20 -> 12, of which waited for: 19 -> 10; matrix products, arithmetic and copies ran while one was open for 12% -> 15% of each run, Pallas kernels for 0% -> 0%
where the time goes in v1:
time: 954 us; the launch traced here: 945 us
  waiting for transfers between devices  425 us (45%)
  matrix products  153 us (16%)
  Pallas kernels  140 us (15%)
  local copies, waits for them, and re-layouts  92.1 us (10%)
  blocking collectives  77.5 us (8%)
  other arithmetic  34.6 us (4%)
  between operations  17 us (2%)
    unnamed x15, waiting for transfers between devices  139 us
    reduce_scatter x4, waiting for transfers between devices, sum_grad(): lax.psum_scatter(term_fn(jnp.int32(0), lax.axis_size('tensor') * row_coun...  136 us
    reduce_scatter x1, waiting for transfers between devices, local(): lax.psum_scatter(stacked_weights[2], 'dp', scatter_dimension=1, tiled=True)  96.7 us
    pallas_call x2, Pallas kernels, ffn_layer(): pl.pallas_call(ffn_forward_kernel, out_shape=(shape((rows, width)), shape...  75.1 us
    pallas_call x2, Pallas kernels, attention_layer(): pl.pallas_call(attention_forward_kernel, out_shape=(shape((rows, width)),...  64.7 us
    all_gather x4, waiting for transfers between devices, gather_grad(): return lax.all_gather(values_in, 'tensor', axis=0, tiled=True)  53.6 us
    unnamed x162, local copies, waits for them, and re-layouts  52.1 us
    psum x1, blocking collectives, local(): lax.psum(stacked_shared, ('dp', 'tensor'))  40.8 us
  transfers between devices with their start and end apart: 12, of which 10 were waited for; matrix products, arithmetic and copies ran while one was open for 15% of the time, Pallas kernels for 0%

profile of v1, /device:TPU:0, one launch (start us, length us, event | category | flops | bytes accessed | tf_op | source)
XLA Modules:
  0.0 945.1 jit_solution(3047191592231104005)
XLA Ops:
  32.0 33.2 %attention_fwd.2 = (f32[256,768]{1,0:T(8,128)}, bf16[256,768]{1,0:T(8,128)(2,1)}, f32[256,768]{1,0:T(8,128)}, f32[256,128]{1,0:T(8,128)}, bf16[4,256,768]{2,1,0:...) custom-call(f32[256,768]{1,0:T(8,128)} %convert_element_type.24.stat, ...), custom_call_target="tpu_custom_call" | custom-call | tf_op jit(solution)/shard_map/attention_fwd/pallas_call | solution.py:293
  65.2 37.7 %ffn_fwd.2 = (f32[256,768]{1,0:T(8,128)}, bf16[256,768]{1,0:T(8,128)(2,1)}, f32[256,768]{1,0:T(8,128)}, f32[256,128]{1,0:T(8,128)}, bf16[4,256,768]{2,1,0:T(8,12...) custom-call(f32[256,768]{1,0:T(8,128)} %get-tuple-element.205.state_ref, ...), custom_call_target="tpu_custom_call" | custom-call | tf_op jit(solution)/shard_map/ffn_fwd/pallas_call | solution.py:406
  103.0 31.4 %attention_fwd.3 = (f32[256,768]{1,0:T(8,128)}, bf16[256,768]{1,0:T(8,128)(2,1)}, f32[256,768]{1,0:T(8,128)}, f32[256,128]{1,0:T(8,128)}, bf16[4,256,768]{2,1,0:...) custom-call(f32[256,768]{1,0:T(8,128)} %get-tuple-element.207.state_, ...), custom_call_target="tpu_custom_call" | custom-call | tf_op jit(solution)/shard_map/attention_fwd/pallas_call | solution.py:293
  134.4 37.4 %ffn_fwd.3 = (f32[256,768]{1,0:T(8,128)}, bf16[256,768]{1,0:T(8,128)(2,1)}, f32[256,768]{1,0:T(8,128)}, f32[256,128]{1,0:T(8,128)}, bf16[4,256,768]{2,1,0:T(8,12...) custom-call(f32[256,768]{1,0:T(8,128)} %get-tuple-element.209.state_ref, ...), custom_call_target="tpu_custom_call" | custom-call | tf_op jit(solution)/shard_map/ffn_fwd/pallas_call | solution.py:406
  177.7 21.1 %all-gather.5.cloned.1.call-done = bf16[1024,768]{1,0:T(8,128)(2,1)} async-done(((bf16[256,768]{1,0:T(8,128)(2,1)}), bf16[1024,768]{1,0:T(8,128)(2,1)}) %all-gather.5.cloned.1.call-update) | async-done | bytes 1572880 | tf_op jit(solution)/shard_map/all_gather | solution.py:448
  205.3 5.8 fusion.124
  212.1 37.1 %reduce-scatter.12.cloned.1.call-done = f32[256,768]{1,0:T(8,128)} async-done(((f32[1024,768]{1,0:T(8,128)}), f32[256,768]{1,0:T(8,128)}) %reduce-scatter.12.cloned.1.call-update) | async-done | bytes 786448 | tf_op jit(solution)/shard_map/reduce_scatter | solution.py:452
  261.0 12.6 %all-gather.7.cloned.1.call-done = bf16[1024,768]{1,0:T(8,128)(2,1)} async-done(((bf16[256,768]{1,0:T(8,128)(2,1)}), bf16[1024,768]{1,0:T(8,128)(2,1)}) %all-gather.7.cloned.1.call-update) | async-done | bytes 1572880 | tf_op jit(solution)/shard_map/all_gather | solution.py:448
  276.7 50.9 %while.52 = (s32[]{:T(128)}, f32[1024,3,64]{0,2,1:T(8,128)S(1)}, f32[1024,3,64]{0,2,1:T(8,128)S(1)}, f32[2,512,3,64]{1,3,2,0:T(8,128)S(1)}, s32[2]{0:T(128)S(1)}...) while((s32[]{:T(128)}, f32[1024,3,64]{0,2,1:T(8,128)S(1)}, ...), condition=%wide.region_9.0_spmd.clone, body=%wide.region_5.9_spmd.clone.sunk | while | flops 5059938816 | bytes 90376584 | solution.py:587
  279.3 6.1 fusion.226
  285.3 4.9 fusion.228
  304.6 6.1 fusion.226
  310.7 4.9 fusion.228
  338.4 37.1 %reduce-scatter.14.cloned.1.call-done = f32[256,768]{1,0:T(8,128)} async-done(((f32[1024,768]{1,0:T(8,128)}), f32[256,768]{1,0:T(8,128)}) %reduce-scatter.14.cloned.1.call-update) | async-done | bytes 786448 | tf_op jit(solution)/shard_map/reduce_scatter | solution.py:452
  380.5 19.8 %all-gather.9.cloned.1.call-done = bf16[1024,768]{1,0:T(8,128)(2,1)} async-done(((bf16[256,768]{1,0:T(8,128)(2,1)}), bf16[1024,768]{1,0:T(8,128)(2,1)}) %all-gather.9.cloned.1.call-update) | async-done | bytes 1572880 | tf_op jit(solution)/shard_map/all_gather | solution.py:448
  406.5 5.8 fusion.123
  413.3 37.1 %reduce-scatter.16.cloned.1.call-done = f32[256,768]{1,0:T(8,128)} async-done(((f32[1024,768]{1,0:T(8,128)}), f32[256,768]{1,0:T(8,128)}) %reduce-scatter.16.cloned.1.call-update) | async-done | bytes 786448 | tf_op jit(solution)/shard_map/reduce_scatter | solution.py:452
  462.1 8.2 copy.61
  490.0 50.9 %while.53 = (s32[]{:T(128)}, f32[1024,3,64]{0,2,1:T(8,128)}, f32[1024,3,64]{0,2,1:T(8,128)S(1)}, f32[2,512,3,64]{1,3,2,0:T(8,128)S(1)}, s32[2]{0:T(128)S(1)}, /*...) while((s32[]{:T(128)}, f32[1024,3,64]{0,2,1:T(8,128)}, ...), condition=%wide.region_20.21_spmd.clone, body=%wide.region_16.20_spmd.clone.sunk | while | flops 5059938816 | bytes 95097240 | solution.py:587
  492.6 6.0 fusion.239
  498.7 4.8 fusion.241
  517.8 6.1 fusion.239
  523.9 4.8 fusion.241
  560.6 4.8 copy.64
  565.4 8.1 reshape.311
  575.4 5.6 convolution_bitcast_fusion.2
  590.2 58.4 %all-reduce.5.cloned.1.call-done = f32[2,768,768]{1,0,2:T(2,128)} async-done(((f32[2,768,768]{1,0,2:T(2,128)}), f32[2,768,768]{1,0,2:T(2,128)}) %all-reduce.5.cloned.1.call-update) | async-done | bytes 4718608
  650.7 40.8 %all-reduce.1 = (f32[2,768]{1,0:T(2,128)}, f32[2,2,768]{2,1,0:T(2,128)}, f32[2,2,768]{2,1,0:T(2,128)}, f32[2,768]{1,0:T(2,128)}) all-reduce(f32[2,768]{1,0:T(2,128)S(1)} %pad_maximum_fusion.7, f32[2,2,768]{2,1,0:T(2,128)S(1)} %pad_maximum_fusion.5, ...), channel_id=1, replica_groups=mesh['dp'=8,'tensor'=4] {'dp','tensor'}, use_global_device_ids=true, to_apply=%region_31.32 | all-reduce | flops 9216 | bytes 73728 | tf_op jit(solution)/shard_map/psum | solution.py:804
  691.9 36.8 %all-reduce.2 = (f32[2,2,192]{2,1,0:T(2,128)}, f32[2,768]{1,0:T(2,128)}) all-reduce(f32[2,2,192]{2,1,0:T(2,128)S(1)} %pad_maximum_fusion.10, f32[2,768]{1,0:T(2,128)S(1)} %pad_maximum_fusion.8), channel_id=1, replica_groups=mesh['dp'=8,'tensor'=4] {'dp'}, use_global_device_ids=true, to_apply=%region_27.28 | all-reduce | flops 2304 | bytes 18432 | tf_op jit(solution)/shard_map/psum | solution.py:797
  730.6 24.6 %reduce-scatter.18.cloned.1.call-done = f32[256,768]{1,0:T(8,128)} async-done(((f32[1024,768]{1,0:T(8,128)}), f32[256,768]{1,0:T(8,128)}) %reduce-scatter.18.cloned.1.call-update) | async-done | bytes 786448 | tf_op jit(solution)/shard_map/reduce_scatter | solution.py:452
  757.3 80.6 %reduce-scatter.22.cloned.1.call-done = f32[96,1152]{1,0:T(8,128)} async-done(((f32[768,1152]{1,0:T(8,128)}), f32[96,1152]{1,0:T(8,128)}) %reduce-scatter.22.cloned.1.call-update) | async-done | bytes 442384
  840.4 96.7 %reduce-scatter.20.cloned.1.call-done = f32[2,96,768]{2,1,0:T(8,128)} async-done(((f32[2,768,768]{2,1,0:T(8,128)}), f32[2,96,768]{2,1,0:T(8,128)}) %reduce-scatter.20.cloned.1.call-update) | async-done | bytes 589840 | tf_op jit(solution)/shard_map/reduce_scatter | solution.py:792
  (387 shorter events, 199.8 us)
Async XLA Ops:
  7.2 11.9 %copy-start.76 = (bf16[3]{0:T(256)(128)(2,1)S(1)}, bf16[3]{0:T(256)(128)(2,1)}, u32[]{:S(2)}) copy-start(bf16[3]{0:T(256)(128)(2,1)} %constant.108.clone) | copy-start | bytes 22
  7.2 11.9 %copy-start.9 = (bf16[2,3,768,192]{2,3,1,0:T(8,128)(2,1)S(1)}, bf16[2,3,768,192]{2,3,1,0:T(8,128)(2,1)}, u32[]{:S(2)}) copy-start(bf16[2,3,768,192]{2,3,1,0:T(8,128)(2,1)} %param.21) | copy-start | bytes 5308420
  7.2 191.7 %all-gather.5.cloned.1.call-start = ((), (), s32[]{:S(2)}) async-start(), calls=%async_computation.7 | async-start | bytes 1966080 | tf_op jit(solution)/shard_map/all_gather | solution.py:448
  134.4 38.4 %copy-start.40 = (bf16[256,768]{1,0:T(8,128)(2,1)S(1)}, bf16[256,768]{1,0:T(8,128)(2,1)}, u32[]{:S(2)}) copy-start(bf16[256,768]{1,0:T(8,128)(2,1)} %param.19) | copy-start | bytes 1179652
  177.7 71.6 %reduce-scatter.12.cloned.1.call-start = ((), (), s32[]{:S(2)}) async-start(), calls=%async_computation.8 | async-start | bytes 3932160 | tf_op jit(solution)/shard_map/reduce_scatter | solution.py:452
  211.1 38.1 %copy-start.32 = (f32[256,768]{1,0:T(8,128)S(1)}, f32[256,768]{1,0:T(8,128)}, u32[]{:S(2)}) copy-start(f32[256,768]{1,0:T(8,128)} %get-tuple-element.222) | copy-start | bytes 2359300
  211.1 62.5 %all-gather.7.cloned.1.call-start = ((), (), s32[]{:S(2)}) async-start(), calls=%async_computation.9 | async-start | bytes 1966080 | tf_op jit(solution)/shard_map/all_gather | solution.py:448
  253.8 121.7 %reduce-scatter.14.cloned.1.call-start = ((), (), s32[]{:S(2)}) async-start(), calls=%async_computation.10 | async-start | bytes 3932160 | tf_op jit(solution)/shard_map/reduce_scatter | solution.py:452
  327.6 6.1 copy-start.21
  337.4 38.1 %copy-start.17 = (f32[256,768]{1,0:T(8,128)S(1)}, f32[256,768]{1,0:T(8,128)}, u32[]{:S(2)}) copy-start(f32[256,768]{1,0:T(8,128)} %copy-done.16) | copy-start | bytes 2359300
  337.4 38.1 %copy-start.31 = (f32[256,768]{1,0:T(8,128)S(1)}, f32[256,768]{1,0:T(8,128)}, u32[]{:S(2)}) copy-start(f32[256,768]{1,0:T(8,128)} %get-tuple-element.227) | copy-start | bytes 2359300
  337.4 38.1 %copy-start.59 = (f32[768]{0:T(1024)S(1)}, f32[768]{0:T(1024)}, u32[]{:S(2)}) copy-start(f32[768]{0:T(1024)} %get-tuple-element.421) | copy-start | bytes 9220
  337.4 62.9 %all-gather.9.cloned.1.call-start = ((), (), s32[]{:S(2)}) async-start(), calls=%async_computation.11 | async-start | bytes 1966080 | tf_op jit(solution)/shard_map/all_gather | solution.py:448
  377.6 22.7 %copy-start.8 = (bf16[2,768,768]{2,1,0:T(8,128)(2,1)S(1)}, bf16[2,768,768]{2,1,0:T(8,128)(2,1)}, u32[]{:S(2)}) copy-start(bf16[2,768,768]{2,1,0:T(8,128)(2,1)} %param.29) | copy-start | bytes 7077892
  380.5 70.0 %reduce-scatter.16.cloned.1.call-start = ((), (), s32[]{:S(2)}) async-start(), calls=%async_computation.12 | async-start | bytes 3932160 | tf_op jit(solution)/shard_map/reduce_scatter | solution.py:452
  400.3 6.2 copy-start.7
  412.3 38.1 %copy-start.30 = (f32[256,768]{1,0:T(8,128)S(1)}, f32[256,768]{1,0:T(8,128)}, u32[]{:S(2)}) copy-start(f32[256,768]{1,0:T(8,128)} %get-tuple-element.229) | copy-start | bytes 2359300
  412.3 38.1 %copy-start.58 = (f32[768]{0:T(1024)S(1)}, f32[768]{0:T(1024)}, u32[]{:S(2)}) copy-start(f32[768]{0:T(1024)} %get-tuple-element.420) | copy-start | bytes 9220
  412.4 67.9 %all-gather.11.cloned.1.call-start = ((), (), s32[]{:S(2)}) async-start(), calls=%async_computation.13 | async-start | bytes 1966080 | tf_op jit(solution)/shard_map/all_gather | solution.py:448
  455.1 193.5 %all-reduce.5.cloned.1.call-start = ((), (), s32[]{:S(2)}) async-start(), calls=%async_computation.18 | async-start | bytes 9437184
  470.3 258.4 %reduce-scatter.24.cloned.1.call-start = ((), (), s32[]{:S(2)}) async-start(), calls=%async_computation.17 | async-start | bytes 1327104
  472.7 7.1 copy-start.48
  488.1 267.1 %reduce-scatter.18.cloned.1.call-start = ((), (), s32[]{:S(2)}) async-start(), calls=%async_computation.14 | async-start | bytes 3932160 | tf_op jit(solution)/shard_map/reduce_scatter | solution.py:452
  550.3 287.5 %reduce-scatter.22.cloned.1.call-start = ((), (), s32[]{:S(2)}) async-start(), calls=%async_computation.16 | async-start | bytes 3981312
  573.5 363.7 %reduce-scatter.20.cloned.1.call-start = ((), (), s32[]{:S(2)}) async-start(), calls=%async_computation.15 | async-start | bytes 5308416 | tf_op jit(solution)/shard_map/reduce_scatter | solution.py:792
  587.6 62.9 %copy-start.72 = (f32[768]{0:T(1024)S(1)}, f32[768]{0:T(1024)}, u32[]{:S(2)}) copy-start(f32[768]{0:T(1024)} %get-tuple-element.404) | copy-start | bytes 9220
  587.7 62.9 %copy-start.73 = (f32[768]{0:T(1024)S(1)}, f32[768]{0:T(1024)}, u32[]{:S(2)}) copy-start(f32[768]{0:T(1024)} %get-tuple-element.476) | copy-start | bytes 9220
  587.7 62.9 %copy-start.71 = (f32[768]{0:T(1024)S(1)}, f32[768]{0:T(1024)}, u32[]{:S(2)}) copy-start(f32[768]{0:T(1024)} %get-tuple-element.415) | copy-start | bytes 9220
  587.7 103.8 %copy-start.27 = (f32[2,512,3,64]{1,3,2,0:T(8,128)S(1)}, f32[2,512,3,64]{1,3,2,0:T(8,128)}, u32[]{:S(2)}) copy-start(f32[2,512,3,64]{1,3,2,0:T(8,128)} %copy-done.26) | copy-start | bytes 2359300
  589.6 102.1 %copy-start.20 = (f32[1024,3,64]{0,2,1:T(8,128)S(1)}, f32[1024,3,64]{0,2,1:T(8,128)}, u32[]{:S(2)}) copy-start(f32[1024,3,64]{0,2,1:T(8,128)} %copy-done.18) | copy-start | bytes 2359300
  590.2 165.0 %copy-start.13 = (f32[256,768]{1,0:T(8,128)S(1)}, f32[256,768]{1,0:T(8,128)}, u32[]{:S(2)}) copy-start(f32[256,768]{1,0:T(8,128)} %copy-done.12) | copy-start | bytes 2359300
  730.6 206.5 %copy-start.45 = (f32[256,768]{1,0:T(8,128)S(1)}, f32[256,768]{1,0:T(8,128)}, u32[]{:S(2)}) copy-start(f32[256,768]{1,0:T(8,128)} %get-tuple-element.773) | copy-start | bytes 2359300
  (73 other events, 227.6 us)
Sparse Core Ops, SparseCore 0:
  177.8 21.0 all-gather.4
  211.2 37.9 reduce-scatter.11
  253.9 19.6 all-gather.6
  337.5 37.9 reduce-scatter.13
  380.6 19.6 all-gather.8
  412.5 37.9 reduce-scatter.15
  455.2 19.6 all-gather.10
  479.0 169.6 all-reduce.4
  652.4 63.2 reduce-scatter.23
  718.2 36.9 reduce-scatter.17
  758.8 79.0 reduce-scatter.21
  841.9 95.1 reduce-scatter.19

commit v2 on v1

--- a/solution.py
+++ b/solution.py
@@ -431,176 +431,629 @@
     return jnp.broadcast_to(split, lead + (heads, 2, HDIM)).reshape(lead + (heads * LANES,))
 
 
-def gather_rows(values_in):
-    return lax.all_gather(values_in, "tensor", axis=0, tiled=True)
-
-
-def sum_rows(term_fn, row_count):
-    return lax.psum_scatter(
-        term_fn(jnp.int32(0), lax.axis_size("tensor") * row_count),
-        "tensor",
-        scatter_dimension=0,
-        tiled=True,
-    )
-
-
-def gather_grad(values_in):
-    return lax.all_gather(values_in, "tensor", axis=0, tiled=True)
-
-
-def sum_grad(term_fn, row_count):
-    return lax.psum_scatter(
-        term_fn(jnp.int32(0), lax.axis_size("tensor") * row_count),
-        "tensor",
-        scatter_dimension=0,
-        tiled=True,
-    )
-
-
-def normalize_unused(total, gain, shift):
-    row_mean = jnp.mean(total, axis=-1, keepdims=True)
-    centered = total - row_mean
-    spread = jnp.mean(centered * centered, axis=-1, keepdims=True)
-    recip = lax.rsqrt(spread + EPSILON)
-    normal = centered * recip
-    return (normal * gain + shift, normal, recip)
-
-
-def normalize_back(grad_in, normal, recip, gain):
+def layer_norm_back(grad_in, normal, recip, gain):
     scaled = grad_in * gain
     inner = (
         scaled
         - jnp.mean(scaled, axis=-1, keepdims=True)
         - normal * jnp.mean(scaled * normal, axis=-1, keepdims=True)
     )
-    return (recip * inner, jnp.sum(grad_in * normal, axis=0), jnp.sum(grad_in, axis=0))
-
-
-def probabilities(query_block, keys_seq, first_row, prefix_len):
-    block_rows = query_block.shape[0]
+    return recip * inner
+
+
+def column_sum(values):
+    return jnp.sum(values, axis=0, keepdims=True)
+
+
+def high_low(values):
+    high = values.astype(BF16)
+    return high, (values - high.astype(F32)).astype(BF16)
+
+
+def dot_tn(left, right):
+    return lax.dot_general(left, right, (((0,), (0,)), ((), ())), preferred_element_type=F32)
+
+
+def remote_dp(src, dst, send_sem, recv_sem, dp_index):
+    return pltpu.make_async_remote_copy(
+        src_ref=src,
+        dst_ref=dst,
+        send_sem=send_sem,
+        recv_sem=recv_sem,
+        device_id={"dp": dp_index},
+        device_id_type=MESH,
+    )
+
+
+class Sequences:
+    def __init__(self, count):
+        self.pairs = count // 2
+        self.index = lax.axis_index("dp")
+        self.pair = self.index // 2
+        self.side = self.index - 2 * self.pair
+        self.neighbour = self.index + 1 - 2 * self.side
+
+    def other_pair(self, offset):
+        return lax.rem(self.pair + offset, self.pairs)
+
+    def peer(self, offset):
+        return 2 * self.other_pair(offset) + self.side
+
+    def everyone(self):
+        return [self.neighbour] + [self.peer(offset) for offset in range(1, self.pairs)]
+
+
+def full_barrier(group, sequences):
+    barrier = pltpu.get_barrier_semaphore()
+    for other in group:
+        pl.semaphore_signal(barrier, inc=1, device_id={"tensor": other}, device_id_type=MESH)
+    others = sequences.everyone() if sequences is not None else []
+    for other in others:
+        pl.semaphore_signal(barrier, inc=1, device_id={"dp": other}, device_id_type=MESH)
+    pl.semaphore_wait(barrier, len(group) + len(others))
+
+
+class GradSum:
+    def __init__(self, sequences, source, result, columns, first_out, first_in, second_out, second_in, sems):
+        self.at = sequences
+        self.source, self.result, self.columns = source, result, columns
+        self.first_out, self.first_in = first_out, first_in
+        self.second_out, self.second_in = second_out, second_in
+        self.sems = sems
+        self.rows = result.shape[0]
+
+    def terms(self, pair, side):
+        start = pl.multiple_of((2 * pair + side) * self.rows, 16)
+        return self.source[pl.ds(start, self.rows), self.columns]
+
+    def first_copy(self):
+        return remote_dp(
+            self.first_out.at[:, :, self.columns], self.first_in.at[:, :, self.columns],
+            self.sems[0], self.sems[1], self.at.neighbour,
+        )
+
+    def second_copy(self, offset):
+        return remote_dp(
+            self.second_out.at[offset - 1, :, self.columns], self.second_in.at[offset - 1, :, self.columns],
+            self.sems[2].at[offset - 1], self.sems[3].at[offset - 1], self.at.peer(offset),
+        )
+
+    def first(self):
+        for pair in range(self.at.pairs):
+            self.first_out[pair, :, self.columns] = self.terms(pair, 1 - self.at.side).astype(BF16)
+        self.first_copy().start()
+
+    def second(self):
+        self.first_copy().wait_recv()
+        for offset in range(1, self.at.pairs):
+            pair = self.at.other_pair(offset)
+            half = self.terms(pair, self.at.side) + self.first_in[pair, :, self.columns].astype(F32)
+            self.second_out[offset - 1, :, self.columns] = half.astype(BF16)
+            self.second_copy(offset).start()
+        own = self.terms(self.at.pair, self.at.side)
+        self.result[:, self.columns] = own + self.first_in[self.at.pair, :, self.columns].astype(F32)
+
+    def third(self):
+        total = self.result[:, self.columns]
+        for offset in range(1, self.at.pairs):
+            self.second_copy(offset).wait_recv()
+            total = total + self.second_in[offset - 1, :, self.columns].astype(F32)
+        self.result[:, self.columns] = total
+
+    def wait_sends(self):
+        self.first_copy().wait_send()
+        for offset in range(1, self.at.pairs):
+            self.second_copy(offset).wait_send()
+
+
+def grad_sum_scratch(count, width, columns, blocks):
+    rows, pairs = width // count, count // 2
+    return [
+        pltpu.VMEM((pairs, rows, columns), BF16), pltpu.VMEM((pairs, rows, columns), BF16),
+        pltpu.VMEM((pairs - 1, rows, columns), BF16), pltpu.VMEM((pairs - 1, rows, columns), BF16),
+        dma_sems(blocks), dma_sems(blocks),
+        pltpu.SemaphoreType.DMA((blocks, pairs - 1)), pltpu.SemaphoreType.DMA((blocks, pairs - 1)),
+    ]
+
+
+def grad_sums(sequences, source, result, scratch, blocks):
+    step = source.shape[1] // blocks
+    sems = scratch[4:]
+    return [
+        GradSum(
+            sequences, source, result, slice(block * step, (block + 1) * step), *scratch[:4],
+            (sems[0].at[block], sems[1].at[block], sems[2].at[block], sems[3].at[block]),
+        )
+        for block in range(blocks)
+    ]
+
+
+class SmallSum:
+    def __init__(self, sequences, source, result, shared_rows, slots, sems):
+        self.at = sequences
+        self.source, self.result, self.shared_rows = source, result, shared_rows
+        self.group_slots, self.side_slots, self.pair_slots = slots
+        self.g_send, self.g_recv, self.s_send, self.s_recv, self.p_send, self.p_recv = sems
+        self.mine, self.partner, self.across, self.diagonal = places()
+
+    def group_copy(self, index, to, slot):
+        return remote(
+            self.group_slots.at[slot], self.group_slots.at[slot],
+            self.g_send.at[index], self.g_recv.at[index], to,
+        )
+
+    def start(self):
+        if self.shared_rows:
+            self.group_slots[self.mine] = self.source[...]
+            for index, other in enumerate((self.partner, self.across, self.diagonal)):
+                self.group_copy(index, other, self.mine).start()
+
+    def side_copy(self, slot):
+        return remote_dp(
+            self.side_slots.at[slot], self.side_slots.at[slot],
+            self.s_send.at[0], self.s_recv.at[0], self.at.neighbour,
+        )
+
+    def first(self):
+        values = self.source[...]
+        if self.shared_rows:
+            for index, other in enumerate((self.partner, self.across, self.diagonal)):
+                self.group_copy(index, other, other).wait_recv()
+            total = self.group_slots[0]
+            for slot in range(1, GROUP):
+                total = total + self.group_slots[slot]
+            shared = lax.broadcasted_iota(jnp.int32, values.shape, 0) < self.shared_rows
+            values = jnp.where(shared, total, values)
+        self.side_slots[self.at.side] = values
+        self.side_copy(self.at.side).start()
+
+    def pair_copy(self, offset, slot):
+        return remote_dp(
+            self.pair_slots.at[slot], self.pair_slots.at[slot],
+            self.p_send.at[offset - 1], self.p_recv.at[offset - 1], self.at.peer(offset),
+        )
+
+    def second(self):
+        self.side_copy(1 - self.at.side).wait_recv()
+        self.pair_slots[self.at.pair] = self.side_slots[0] + self.side_slots[1]
+        for offset in range(1, self.at.pairs):
+            self.pair_copy(offset, self.at.pair).start()
+
+    def third(self):
+        for offset in range(1, self.at.pairs):
+            self.pair_copy(offset, self.at.other_pair(self.at.pairs - offset)).wait_recv()
+        total = self.pair_slots[0]
+        for slot in range(1, self.at.pairs):
+            total = total + self.pair_slots[slot]
+        self.result[...] = total
+
+    def wait_sends(self):
+        if self.shared_rows:
+            for index, other in enumerate((self.partner, self.across, self.diagonal)):
+                self.group_copy(index, other, self.mine).wait_send()
+        self.side_copy(self.at.side).wait_send()
+        for offset in range(1, self.at.pairs):
+            self.pair_copy(offset, self.at.pair).wait_send()
+
+
+def small_sum_scratch(count, width):
+    pairs = count // 2
+    return [
+        pltpu.VMEM((GROUP, 8, width), F32), pltpu.VMEM((2, 8, width), F32), pltpu.VMEM((pairs, 8, width), F32),
+        dma_sems(3), dma_sems(3), dma_sems(1), dma_sems(1), dma_sems(pairs - 1), dma_sems(pairs - 1),
+    ]
+
+
+class Exchange:
+    def __init__(self, terms, near, relay, total, far, sems):
+        self.terms, self.near, self.relay, self.total, self.far = terms, near, relay, total, far
+        self.n_send, self.n_recv, self.r_send, self.r_recv, self.f_send, self.f_recv = sems
+        self.mine, self.partner, self.across, self.diagonal = places()
+        self.rows = terms.shape[1] // PIECES
+
+    def spot(self, part):
+        return pl.ds(part * self.rows, self.rows)
+
+    def near_copy(self, part):
+        return remote(
+            self.terms.at[self.partner, self.spot(part)], self.near.at[self.spot(part)],
+            self.n_send.at[part], self.n_recv.at[part], self.partner,
+        )
+
+    def relay_copy(self, part):
+        return remote(
+            self.terms.at[self.diagonal, self.spot(part)], self.relay.at[self.spot(part)],
+            self.r_send.at[part], self.r_recv.at[part], self.partner,
+        )
+
+    def far_copy(self, part):
+        return remote(
+            self.total.at[self.spot(part)], self.far.at[self.spot(part)],
+            self.f_send.at[part], self.f_recv.at[part], self.across,
+        )
+
+    def pass_on(self, part):
+        spot = self.spot(part)
+        self.relay_copy(part).wait_recv()
+        self.total[spot] = (self.terms[self.across, spot] + self.relay[spot]).astype(self.total.dtype)
+        self.far_copy(part).start()
+
+    def result(self, part):
+        spot = self.spot(part)
+        self.near_copy(part).wait_recv()
+        self.far_copy(part).wait_recv()
+        return (self.terms[self.mine, spot] + self.near[spot]) + self.far[spot].astype(F32)
+
+    def wait_sends(self):
+        for part in range(PIECES):
+            self.near_copy(part).wait_send()
+            self.relay_copy(part).wait_send()
+            self.far_copy(part).wait_send()
+
+
+def exchange_scratch(rows, width, kind):
+    return [
+        pltpu.VMEM((GROUP, rows, width), F32),
+        pltpu.VMEM((rows, width), F32), pltpu.VMEM((rows, width), F32),
+        pltpu.VMEM((rows, width), kind), pltpu.VMEM((rows, width), kind),
+    ] + [dma_sems(PIECES)] * 6
+
+
+class Refs:
+    def __init__(self, refs):
+        self.refs = list(refs)
+
+    def take(self, count):
+        taken, self.refs = self.refs[:count], self.refs[count:]
+        return taken
+
+
+ATTN_BLOCKS = 2
+FFN_BLOCKS = 4
+
+
+def ffn_backward_kernel(count, behind, *refs):
+    refs = Refs(refs)
+    (
+        grad_ref, normal2_ref, recip2_ref, gain2_ref, wdown_ref, wup_ref, active_ref, slope_ref,
+        normed_ref, normal1_ref, recip1_ref, gain1_ref,
+    ) = refs.take(12)
+    earlier = refs.take(1) if behind else None
+    du_ref, low_ref, grads_ref, smalls_ref = refs.take(4)
+    earlier_sum = refs.take(1) if behind else None
+    df_ref, du2_ref, high_ref, lowbits_ref = refs.take(4)
+    terms_ref, near_ref, relay_ref, sum_ref, far_ref = refs.take(5)
+    exchange_sems = refs.take(6)
+    g_send, g_recv = refs.take(2)
+    mine, partner, across, diagonal = places()
+    rows, width = grad_ref.shape
+    units = wup_ref.shape[1]
+    grad = grad_ref[...]
+    normal2 = normal2_ref[...]
+    du2 = layer_norm_back(grad, normal2, recip2_ref[:, :1], gain2_ref[...])
+    du2_ref[...] = du2
+    df_ref[mine] = du2.astype(BF16)
+    sequences = Sequences(count) if behind else None
+    full_barrier((partner, across, diagonal), sequences)
+    gather = Gather(df_ref, g_send, g_recv)
+    gather.start()
+    blocks = grad_sums(sequences, earlier[0], earlier_sum[0], refs.take(8), ATTN_BLOCKS) if behind else []
+    for block in blocks:
+        block.first()
+    exchange = Exchange(terms_ref, near_ref, relay_ref, sum_ref, far_ref, exchange_sems)
+    smalls_ref[0:1] = column_sum(du2)
+    smalls_ref[1:2] = column_sum(grad * normal2)
+    smalls_ref[2:3] = column_sum(grad)
+    smalls_ref[6:8] = jnp.zeros((2, width), F32)
+
+    def back(chunk, part):
+        spot = exchange.spot(part)
+        grad_active = dot_nt(df_ref[chunk, spot], wdown_ref[...])
+        grad_hidden = grad_active * slope_ref[chunk, spot]
+        smalls_ref[6:7] = smalls_ref[6:7] + column_sum(grad_hidden)
+        high, low = high_low(grad_hidden)
+        high_ref[chunk, spot] = high
+        lowbits_ref[chunk, spot] = low
+        terms_ref[chunk, spot] = dot_nt(high, wup_ref[...]) + dot_nt(low, wup_ref[...])
+
+    for part in range(PIECES):
+        back(mine, part)
+    for part in range(PIECES):
+        gather.wait_across(part)
+        gather.onward(part).start()
+        back(across, part)
+        gather.wait_diagonal(part)
+        back(diagonal, part)
+        exchange.relay_copy(part).start()
+        if part > 0:
+            exchange.pass_on(part - 1)
+    gather.wait_partner()
+    back(partner, 0)
+    exchange.near_copy(0).start()
+    exchange.pass_on(PIECES - 1)
+    for part in range(1, PIECES):
+        back(partner, part)
+        exchange.near_copy(part).start()
+    for block in blocks:
+        block.second()
+    tall = GROUP * rows
+    grads_ref[:, :units] = dot_tn(normed_ref[...].reshape(tall, width), high_ref[...].reshape(tall, units)) + dot_tn(
+        normed_ref[...].reshape(tall, width), lowbits_ref[...].reshape(tall, units)
+    )
+    grads_ref[:, units:] = dot_tn(df_ref[...].reshape(tall, width), active_ref[...].reshape(tall, units))
+    for part in range(PIECES):
+        spot = exchange.spot(part)
+        grad_normed = exchange.result(part) + du2_ref[spot]
+        normal1 = normal1_ref[spot]
+        du = layer_norm_back(grad_normed, normal1, recip1_ref[spot, :1], gain1_ref[...])
+        du_ref[spot] = du
+        low_ref[spot] = du.astype(BF16)
+        sums = (column_sum(grad_normed * normal1), column_sum(grad_normed), column_sum(du))
+        for index, value in enumerate(sums):
+            place = slice(3 + index, 4 + index)
+            smalls_ref[place] = value if part == 0 else smalls_ref[place] + value
+    for block in blocks:
+        block.third()
+    gather.wait_sends()
+    exchange.wait_sends()
+    for block in blocks:
+        block.wait_sends()
+
+
+def ffn_layer_back(count, grad, normal2, recip2, gain2, wdown, wup, active, slope, normed, normal1, recip1, gain1, earlier, collective):
+    rows, width = grad.shape
+    units = wup.shape[1]
+    behind = earlier is not None
+    outs = [shape((rows, width)), shape((rows, width), BF16), shape((width, 2 * units)), shape((8, width))]
+    scratch = [
+        pltpu.VMEM((GROUP, rows, width), BF16),
+        pltpu.VMEM((rows, width), F32),
+        pltpu.VMEM((GROUP, rows, units), BF16), pltpu.VMEM((GROUP, rows, units), BF16),
+    ]
+    scratch += exchange_scratch(rows, width, BF16) + [dma_sems(GATHER_SEMS), dma_sems(GATHER_SEMS)]
+    extra = []
+    if behind:
+        extra = [earlier]
+        outs.append(shape((width // count, earlier.shape[1])))
+        scratch += grad_sum_scratch(count, width, earlier.shape[1], ATTN_BLOCKS)
+    return pl.pallas_call(
+        functools.partial(ffn_backward_kernel, count, behind),
+        out_shape=tuple(outs),
+        in_specs=[VM] * (12 + len(extra)),
+        out_specs=(VM,) * len(outs),
+        scratch_shapes=scratch,
+        compiler_params=params(collective),
+        name="ffn_bwd",
+    )(grad, normal2, recip2, gain2, wdown, wup, active, slope, normed, normal1, recip1, gain1, *extra)
+
+
+def attention_backward_kernel(count, behind, last, *refs):
+    refs = Refs(refs)
+    (
+        low_ref, du_ref, wout_ref, qt_ref, q2_ref, kz_ref, kt_ref, v2_ref, ct_ref, stats_ref, input_ref,
+        wqkv_ref, prefix_ref,
+    ) = refs.take(13)
+    earlier, smalls_in, bias_in = refs.take(3) if behind else (None,) * 3
+    dx_ref, grads_ref, bias_ref = refs.take(3)
+    earlier_sum, smalls_sum = refs.take(2) if behind else (None,) * 2
+    grads_sum, bias_sum = refs.take(2) if last else (None,) * 2
+    do_ref, dc_ref, dct_ref, dq_ref, dk_ref, dv_ref, packed_ref = refs.take(7)
+    terms_ref, near_ref, relay_ref, sum_ref, far_ref = refs.take(5)
+    exchange_sems = refs.take(6)
+    g_send, g_recv = refs.take(2)
+    mine, partner, across, diagonal = places()
+    rows, width = low_ref.shape
+    heads = qt_ref.shape[0]
     scale = 1.0 / math.sqrt(HDIM)
-    scores = (
-        jnp.einsum("bhd,khd->hbk", query_block, keys_seq, preferred_element_type=jnp.float32)
-        * scale
-    )
-    row_pos = first_row + lax.broadcasted_iota(jnp.int32, (block_rows, LEN), 0)
-    col_pos = lax.broadcasted_iota(jnp.int32, (block_rows, LEN), 1)
-    visible = (
-        (col_pos <= row_pos) | (col_pos < prefix_len) | (row_pos < MEM) | (row_pos >= LEN - MEM)
-    )
-    scores = jnp.where(visible[None], scores, -1e30)
-    row_max = jnp.max(scores, axis=-1, keepdims=True)
-    expo = jnp.exp(scores - row_max)
-    return expo / jnp.sum(expo, axis=-1, keepdims=True)
-
-
-def attention_forward(query, keys, values, prefix):
-    seq_count = prefix.shape[0]
-    width = query.shape[1]
-    local_heads = width // HDIM
-    block_rows = min(512, LEN)
-    block_count = LEN // block_rows
-    shape_four = (seq_count, LEN, local_heads, HDIM)
-
-    def per_sequence(sequence):
-        query_seq, keys_seq, values_seq, prefix_len = sequence
-
-        def per_block(block_index):
-            first_row = block_index * block_rows
-            query_block = lax.dynamic_slice_in_dim(query_seq, first_row, block_rows, 0)
-            probs = probabilities(query_block, keys_seq, first_row, prefix_len)
-            return jnp.einsum(
-                "hbk,khd->bhd",
-                probs.astype(jnp.bfloat16),
-                values_seq,
-                preferred_element_type=jnp.float32,
-            ).astype(jnp.bfloat16)
-
-        blocks = lax.map(per_block, jnp.arange(block_count, dtype=jnp.int32))
-        return blocks.reshape(LEN, local_heads, HDIM)
-
-    context = lax.map(
-        per_sequence,
-        (query.reshape(shape_four), keys.reshape(shape_four), values.reshape(shape_four), prefix),
-    )
-    return context.reshape(seq_count * LEN, width)
-
-
-def attention_backward(query, keys, values, grad_context, prefix):
-    seq_count = prefix.shape[0]
-    width = query.shape[1]
-    local_heads = width // HDIM
-    block_rows = min(512, LEN)
-    block_count = LEN // block_rows
-    scale = 1.0 / math.sqrt(HDIM)
-    shape_four = (seq_count, LEN, local_heads, HDIM)
-
-    def per_sequence(sequence):
-        query_seq, keys_seq, values_seq, grad_seq, prefix_len = sequence
-
-        def per_block(running, block_index):
-            keys_acc, values_acc = running
-            first_row = block_index * block_rows
-            query_block = lax.dynamic_slice_in_dim(query_seq, first_row, block_rows, 0)
-            grad_block = lax.dynamic_slice_in_dim(grad_seq, first_row, block_rows, 0)
-            probs = probabilities(query_block, keys_seq, first_row, prefix_len)
-            probs_low = probs.astype(jnp.bfloat16)
-            grad_probs = jnp.einsum(
-                "bhd,khd->hbk",
-                grad_block,
-                values_seq,
-                precision=HIGHEST,
-                preferred_element_type=jnp.float32,
-            )
-            grad_scores = probs * (grad_probs - jnp.sum(probs * grad_probs, axis=-1, keepdims=True))
-            grad_query = (
-                jnp.einsum(
-                    "hbk,khd->bhd",
-                    grad_scores,
-                    keys_seq,
-                    precision=HIGHEST,
-                    preferred_element_type=jnp.float32,
-                )
-                * scale
-            )
-            keys_acc = (
-                keys_acc
-                + jnp.einsum(
-                    "hbk,bhd->khd",
-                    grad_scores,
-                    query_block,
-                    precision=HIGHEST,
-                    preferred_element_type=jnp.float32,
-                )
-                * scale
-            )
-            values_acc = values_acc + jnp.einsum(
-                "hbk,bhd->khd",
-                probs_low,
-                grad_block,
-                precision=HIGHEST,
-                preferred_element_type=jnp.float32,
-            )
-            return ((keys_acc, values_acc), grad_query)
-
-        zero_acc = jnp.zeros((LEN, local_heads, HDIM), jnp.float32)
-        (keys_acc, values_acc), grad_query = lax.scan(
-            per_block, (zero_acc, zero_acc), jnp.arange(block_count, dtype=jnp.int32)
-        )
-        return (grad_query.reshape(LEN, local_heads, HDIM), keys_acc, values_acc)
-
-    grad_q, grad_k, grad_v = lax.map(
-        per_sequence,
-        (
-            query.reshape(shape_four),
-            keys.reshape(shape_four),
-            values.reshape(shape_four),
-            grad_context.reshape(shape_four),
-            prefix,
-        ),
-    )
-    flat = (seq_count * LEN, width)
-    return (grad_q.reshape(flat), grad_k.reshape(flat), grad_v.reshape(flat))
+    sequences = Sequences(count) if behind else None
+    full_barrier((partner, across, diagonal), sequences)
+    gather = Gather(do_ref, g_send, g_recv)
+    do_ref[mine] = low_ref[...]
+    gather.start()
+    exchange = Exchange(terms_ref, near_ref, relay_ref, sum_ref, far_ref, exchange_sems)
+    blocks, own_blocks, small, own_small = [], [], None, None
+    if behind:
+        blocks = grad_sums(sequences, earlier, earlier_sum, refs.take(8), FFN_BLOCKS)
+        small_source = refs.take(1)[0]
+        is_bias = lax.broadcasted_iota(jnp.int32, small_source.shape, 0) == 7
+        small_source[...] = jnp.where(is_bias, bias_in[...], smalls_in[...])
+        small = SmallSum(sequences, small_source, smalls_sum, 6, refs.take(3), refs.take(6))
+        small.start()
+        blocks[0].first()
+        blocks[1].first()
+    if last:
+        own_blocks = grad_sums(sequences, grads_ref, grads_sum, refs.take(8), ATTN_BLOCKS)
+        own_small = SmallSum(sequences, bias_ref, bias_sum, 0, refs.take(3), refs.take(6))
+    dk_ref[...] = jnp.zeros_like(dk_ref)
+    dv_ref[...] = jnp.zeros_like(dv_ref)
+    lane_low = lax.broadcasted_iota(jnp.int32, (rows, LANES), 1) < HDIM
+
+    def pack(values):
+        high = values.astype(BF16).astype(F32)
+        return jnp.where(lane_low, high, values - high)
+
+    def context_grad(chunk):
+        spots = pl.ds(pl.multiple_of(chunk * rows, rows), rows)
+        for head in range(heads):
+            both = pack(dot(do_ref[chunk], wout_ref[:, pl.ds(head * LANES, LANES)]))
+            dc_ref[head, spots] = both.astype(BF16)
+            dct_ref[head, :, spots] = both.T.astype(BF16)
+
+    def attend_back(chunk):
+        keys = visible_keys(chunk, rows)
+        limits = query_limits(chunk, rows, prefix_ref[0])
+        visible = lax.broadcasted_iota(jnp.int32, (keys, rows), 0) <= limits
+        spots = pl.ds(chunk * rows, rows)
+        seen = pl.ds(0, keys)
+
+        def one_head(head, carry):
+            scores = dot(kz_ref[head, seen], qt_ref[head, :, spots])
+            top = stats_ref[head, 0:1, spots]
+            recip = stats_ref[head, 1:2, spots]
+            probs = jnp.exp(jnp.where(visible, scores - top, -1e30)) * recip
+            grad_probs = dot(v2_ref[head, seen], dct_ref[head, :, spots])
+            inner = column_sum(probs * grad_probs)
+            grad_scores = (probs * (grad_probs - inner)).astype(BF16)
+            dv_ref[head, seen] = dv_ref[head, seen] + dot(probs.astype(BF16), dc_ref[head, spots])
+            dk_ref[head, seen] = dk_ref[head, seen] + dot(grad_scores, q2_ref[head, spots])
+            dq_ref[head, spots] = dot(kt_ref[head, :, seen], grad_scores).T * scale
+            return carry
+
+        lax.fori_loop(0, heads, one_head, 0)
+
+    chip, core = mine // 2, mine - 2 * (mine // 2)
+
+    def one_step(step, carry):
+        near = 1 - step // 2
+        flip = lax.rem(step, 2)
+        to_chip = (1 - near) * (1 - chip) + near * chip
+        chunk = 2 * to_chip + core + flip * (1 - 2 * core)
+
+        @pl.when(step == 1)
+        def _():
+            gather.wait_partner()
+            if behind:
+                small.first()
+                blocks[2].first()
+
+        @pl.when(step == 2)
+        def _():
+            for part in range(PIECES):
+                gather.wait_across(part)
+                gather.onward(part).start()
+            if behind:
+                blocks[0].second()
+                blocks[3].first()
+
+        @pl.when(step == 3)
+        def _():
+            for part in range(PIECES):
+                gather.wait_diagonal(part)
+            if behind:
+                blocks[1].second()
+
+        context_grad(chunk)
+        for each in range(GROUP):
+            @pl.when(chunk == each)
+            def _():
+                attend_back(each)
+        return carry
+
+    lax.fori_loop(0, GROUP, one_step, 0)
+    if behind:
+        blocks[2].second()
+        small.second()
+
+    def pack_chunk(chunk, carry):
+        spots = pl.ds(pl.multiple_of(chunk * rows, rows), rows)
+        for head in range(heads):
+            dv_wide = dv_ref[head, spots]
+            parts = (dq_ref[head, spots], dk_ref[head, spots], dv_wide + pltpu.roll(dv_wide, HDIM, 1))
+            for kind, values in enumerate(parts):
+                packed_ref[chunk, :, pl.ds((kind * heads + head) * LANES, LANES)] = pack(values).astype(BF16)
+                if kind != 1:
+                    place = pl.ds(((kind // 2) * heads + head) * LANES, LANES)
+                    bias_ref[:, place] = bias_ref[:, place] + column_sum(values)
+        return carry
+
+    bias_ref[...] = jnp.zeros_like(bias_ref)
+    lax.fori_loop(0, GROUP, pack_chunk, 0)
+
+    tall = GROUP * rows
+    depth = heads * HDIM
+
+    def weight_grads():
+        out_wide = dot(ct_ref[0], do_ref[0])
+        for chunk in range(1, GROUP):
+            out_wide = out_wide + dot(ct_ref[chunk], do_ref[chunk])
+        grads_ref[:, :depth] = out_wide.T
+        whole_in = input_ref[...].reshape(tall, width)
+        for index in range(3 * heads):
+            wide = dot_tn(whole_in, packed_ref[:, :, pl.ds(index * LANES, LANES)].reshape(tall, LANES))
+            wide = wide + pltpu.roll(wide, HDIM, 1)
+            grads_ref[:, depth + index * HDIM : depth + (index + 1) * HDIM] = wide[:, :HDIM]
+
+    def input_terms(chunk, part):
+        spot = exchange.spot(part)
+        terms_ref[chunk, spot] = dot(packed_ref[chunk, spot], wqkv_ref[...])
+
+    if last:
+        weight_grads()
+        own_small.first()
+        for block in own_blocks:
+            block.first()
+    if behind:
+        blocks[3].second()
+    for part in range(PIECES):
+        input_terms(diagonal, part)
+        exchange.relay_copy(part).start()
+        input_terms(across, part)
+        if part > 0:
+            exchange.pass_on(part - 1)
+    input_terms(partner, 0)
+    exchange.near_copy(0).start()
+    exchange.pass_on(PIECES - 1)
+    for part in range(1, PIECES):
+        input_terms(partner, part)
+        exchange.near_copy(part).start()
+    for part in range(PIECES):
+        input_terms(mine, part)
+    if behind:
+        small.third()
+        blocks[0].third()
+        blocks[1].third()
+    if last:
+        own_small.second()
+        for block in own_blocks:
+            block.second()
+    else:
+        weight_grads()
+    for part in range(PIECES):
+        spot = exchange.spot(part)
+        dx_ref[spot] = exchange.result(part) + du_ref[spot]
+    if behind:
+        blocks[2].third()
+        blocks[3].third()
+    if last:
+        own_small.third()
+        for block in own_blocks:
+            block.third()
+    gather.wait_sends()
+    exchange.wait_sends()
+    for item in blocks + own_blocks + [each for each in (small, own_small) if each is not None]:
+        item.wait_sends()
+
+
+def attention_layer_back(count, behind, last, low, du, wout, qt, q2, kz, kt, v2, ct, stats, whole, wqkv, prefix, extra, collective):
+    rows, width = low.shape
+    heads = qt.shape[0]
+    tall = GROUP * rows
+    columns = 4 * heads * HDIM
+    outs = [shape((rows, width)), shape((width, columns)), shape((8, 2 * heads * LANES))]
+    scratch = [
+        pltpu.VMEM((GROUP, rows, width), BF16),
+        pltpu.VMEM((heads, tall, LANES), BF16), pltpu.VMEM((heads, LANES, tall), BF16),
+        pltpu.VMEM((heads, tall, LANES), F32), pltpu.VMEM((heads, tall, LANES), F32),
+        pltpu.VMEM((heads, tall, LANES), F32),
+        pltpu.VMEM((GROUP, rows, 3 * heads * LANES), BF16),
+    ]
+    scratch += exchange_scratch(rows, width, BF16) + [dma_sems(GATHER_SEMS), dma_sems(GATHER_SEMS)]
+    if behind:
+        outs += [shape((width // count, extra[0].shape[1])), shape((8, width))]
+        scratch += grad_sum_scratch(count, width, extra[0].shape[1], FFN_BLOCKS)
+        scratch += [pltpu.VMEM((8, width), F32)] + small_sum_scratch(count, width)
+    if last:
+        outs += [shape((width // count, columns)), shape((8, width))]
+        scratch += grad_sum_scratch(count, width, columns, ATTN_BLOCKS) + small_sum_scratch(count, width)
+    return pl.pallas_call(
+        functools.partial(attention_backward_kernel, count, behind, last),
+        out_shape=tuple(outs),
+        in_specs=[VM] * 12 + [SM] + [VM] * len(extra),
+        out_specs=(VM,) * len(outs),
+        scratch_shapes=scratch,
+        compiler_params=params(collective),
+        name="attention_bwd",
+    )(low, du, wout, qt, q2, kz, kt, v2, ct, stats, whole, wqkv, prefix, *extra)
 
 
 def local(
@@ -618,205 +1071,94 @@
     w_down,
     bias_down,
 ):
-    my_rows = tokens.shape[0]
+    my_rows, width = tokens.shape
     layer_count = w_qkv.shape[0]
-    state = tokens.astype(F32)
-    low = tokens
     depth = w_out.shape[1]
     heads = depth // HDIM
-    scale = jnp.array([1.0 / math.sqrt(HDIM), 1.0, 1.0], BF16).reshape(1, 3, 1, 1)
-    wqkv = doubled(w_qkv * scale, heads)
-    wqkv = jnp.moveaxis(wqkv, 1, 2).reshape(layer_count, w_qkv.shape[2], -1)
-    bias3 = jnp.stack(
-        [bias_qv[:, 0] * (1.0 / math.sqrt(HDIM)), jnp.zeros_like(bias_qv[:, 0]), bias_qv[:, 1]], axis=1
-    )
+    root = 1.0 / math.sqrt(HDIM)
+    scale = jnp.array([root, 1.0, 1.0], BF16).reshape(1, 3, 1, 1)
+    wqkv = jnp.moveaxis(doubled(w_qkv * scale, heads), 1, 2).reshape(layer_count, width, -1)
+    wqkv_back = jnp.swapaxes(doubled(w_qkv, heads), 2, 3).reshape(layer_count, -1, width)
+    wout_back = doubled(jnp.swapaxes(w_out, 1, 2), heads)
+    bias3 = jnp.stack([bias_qv[:, 0] * root, jnp.zeros_like(bias_qv[:, 0]), bias_qv[:, 1]], axis=1)
     bias3 = doubled(bias3, heads).reshape(layer_count, 1, -1)
+    state, low = tokens.astype(F32), tokens
     stored = []
-    for layer_index in range(layer_count):
-        (
-            state, low, normal_one, recip_one, input_whole, qt, q2, kz, kt, v2, ct, stats,
-        ) = attention_layer(
-            state, low, wqkv[layer_index], bias3[layer_index], w_out[layer_index],
-            bias_out[layer_index][None], norm_gain[layer_index, 0][None],
-            norm_bias[layer_index, 0][None], prefix,
-        )
-        (
-            state, low, normal_two, recip_two, normed_whole, active, slope,
-        ) = ffn_layer(
-            state, low, w_up[layer_index], bias_up[layer_index][None], w_down[layer_index],
-            bias_down[layer_index][None], norm_gain[layer_index, 1][None],
-            norm_bias[layer_index, 1][None],
-        )
-        total = GROUP * my_rows
-        input_whole = input_whole.reshape(total, -1)
-        normed_whole = normed_whole.reshape(total, -1)
-        pick = lambda v: jnp.moveaxis(v[:, :, :HDIM], 0, 1).reshape(total, depth)
+    for layer in range(layer_count):
+        state, low, normal1, recip1, whole, qt, q2, kz, kt, v2, ct, stats = attention_layer(
+            state, low, wqkv[layer], bias3[layer], w_out[layer], bias_out[layer][None],
+            norm_gain[layer, 0][None], norm_bias[layer, 0][None], prefix,
+        )
+        state, low, normal2, recip2, normed, active, slope = ffn_layer(
+            state, low, w_up[layer], bias_up[layer][None], w_down[layer],
+            bias_down[layer][None], norm_gain[layer, 1][None], norm_bias[layer, 1][None],
+        )
         stored.append(
-            (
-                input_whole, pick(q2) * 8, pick(kz), pick(v2),
-                jnp.moveaxis(ct, 1, 2).reshape(total, depth), normal_one, recip_one[:, :1],
-                normed_whole, slope.reshape(total, -1), active.reshape(total, -1), normal_two,
-                recip_two[:, :1],
-            )
-        )
-    grad_state = cotangent.astype(jnp.float32)
-    weight_grads = [None] * layer_count
-    bias_grads = [None] * layer_count
-    shared_grads = [None] * layer_count
-    for layer_index in reversed(range(layer_count)):
-        (
-            input_whole,
-            query,
-            keys,
-            values,
-            context,
-            normal_one,
-            recip_one,
-            normed_whole,
-            hidden,
-            active,
-            normal_two,
-            recip_two,
-        ) = stored[layer_index]
-        grad_two, gain_two, shift_two = normalize_back(
-            grad_state, normal_two, recip_two, norm_gain[layer_index, 1]
-        )
-        ffn_grad_whole = gather_grad(grad_two.astype(jnp.bfloat16))
-        grad_down = jnp.einsum(
-            "rf,rd->fd", active, ffn_grad_whole, preferred_element_type=jnp.float32
-        )
-        grad_active = jnp.einsum(
-            "rd,fd->rf", ffn_grad_whole, w_down[layer_index], preferred_element_type=jnp.float32
-        )
-        grad_hidden = grad_active * hidden
-        grad_up = jnp.einsum(
-            "rd,rf->df",
-            normed_whole,
-            grad_hidden,
-            precision=HIGHEST,
-            preferred_element_type=jnp.float32,
-        )
-        grad_bias_up = jnp.sum(grad_hidden, axis=0)
-
-        def ffn_back_term(row_start, row_count):
-            return jnp.einsum(
-                "rf,df->rd",
-                grad_hidden,
-                w_up[layer_index],
-                precision=HIGHEST,
-                preferred_element_type=jnp.float32,
-            )
-
-        grad_normed = sum_grad(ffn_back_term, my_rows) + grad_two
-        grad_one, gain_one, shift_one = normalize_back(
-            grad_normed, normal_one, recip_one, norm_gain[layer_index, 0]
-        )
-        attn_grad_whole = gather_grad(grad_one.astype(jnp.bfloat16))
-        grad_out = jnp.einsum(
-            "rh,rd->hd", context, attn_grad_whole, preferred_element_type=jnp.float32
-        )
-        grad_context = jnp.einsum(
-            "rd,hd->rh", attn_grad_whole, w_out[layer_index], preferred_element_type=jnp.float32
-        )
-        grad_query, grad_keys, grad_values = attention_backward(
-            query, keys, values, grad_context, prefix
-        )
-        grad_qkv = jnp.stack(
-            [
-                jnp.einsum(
-                    "rd,rh->dh",
-                    input_whole,
-                    grad_query,
-                    precision=HIGHEST,
-                    preferred_element_type=jnp.float32,
-                ),
-                jnp.einsum(
-                    "rd,rh->dh",
-                    input_whole,
-                    grad_keys,
-                    precision=HIGHEST,
-                    preferred_element_type=jnp.float32,
-                ),
-                jnp.einsum(
-                    "rd,rh->dh",
-                    input_whole,
-                    grad_values,
-                    precision=HIGHEST,
-                    preferred_element_type=jnp.float32,
-                ),
-            ]
-        )
-        grad_bias_qv = jnp.stack([jnp.sum(grad_query, axis=0), jnp.sum(grad_values, axis=0)])
-
-        def input_back_term(row_start, row_count):
-            total = jnp.einsum(
-                "rh,dh->rd",
-                grad_query,
-                w_qkv[layer_index, 0],
-                precision=HIGHEST,
-                preferred_element_type=jnp.float32,
-            )
-            total = total + jnp.einsum(
-                "rh,dh->rd",
-                grad_keys,
-                w_qkv[layer_index, 1],
-                precision=HIGHEST,
-                preferred_element_type=jnp.float32,
-            )
-            return total + jnp.einsum(
-                "rh,dh->rd",
-                grad_values,
-                w_qkv[layer_index, 2],
-                precision=HIGHEST,
-                preferred_element_type=jnp.float32,
-            )
-
-        grad_state = sum_grad(input_back_term, my_rows) + grad_one
-        weight_grads[layer_index] = (grad_qkv, grad_out, grad_up, grad_down)
-        bias_grads[layer_index] = (grad_bias_qv, grad_bias_up)
-        shared_grads[layer_index] = (
-            jnp.sum(grad_one, axis=0),
-            jnp.stack([gain_one, gain_two]),
-            jnp.stack([shift_one, shift_two]),
-            jnp.sum(grad_two, axis=0),
-        )
-    stacked_weights = tuple(
-        (
-            jnp.stack([weight_grads[level][member] for level in range(layer_count)])
-            for member in range(4)
-        )
-    )
-    summed_qkv, summed_out, summed_up, summed_down = (
-        lax.psum_scatter(stacked_weights[0], "dp", scatter_dimension=2, tiled=True),
-        lax.psum_scatter(stacked_weights[1], "dp", scatter_dimension=2, tiled=True),
-        lax.psum_scatter(stacked_weights[2], "dp", scatter_dimension=1, tiled=True),
-        lax.psum_scatter(stacked_weights[3], "dp", scatter_dimension=2, tiled=True),
-    )
-    stacked_bias_qv = jnp.stack([bias_grads[level][0] for level in range(layer_count)])
-    stacked_bias_up = jnp.stack([bias_grads[level][1] for level in range(layer_count)])
-    summed_bias_qv, summed_bias_up = lax.psum((stacked_bias_qv, stacked_bias_up), "dp")
-    stacked_shared = tuple(
-        (
-            jnp.stack([shared_grads[level][member] for level in range(layer_count)])
-            for member in range(4)
-        )
-    )
-    summed_bias_out, summed_gain, summed_shift, summed_bias_down = lax.psum(
-        stacked_shared, ("dp", "tensor")
-    )
+            ((normal2, recip2), (active, slope, normed, normal1, recip1),
+             (qt, q2, kz, kt, v2, ct, stats, whole))
+        )
+    count = lax.axis_size("dp")
+    behind = count > 2 and count % 2 == 0 and (width // count) % 16 == 0
+    grad = cotangent.astype(F32)
+    attn_grads, ffn_grads, smalls, biases = [], [], [], []
+    attn_sums, ffn_sums, small_sums = [], [], []
+    earlier = None
+    bias = jnp.zeros((8, width), F32)
+    for layer in reversed(range(layer_count)):
+        second, middle, first = stored[layer]
+        last = behind and layer == 0
+        du, low, ffn_grad, small, *sums = ffn_layer_back(
+            count, grad, *second, norm_gain[layer, 1][None], w_down[layer], w_up[layer], *middle,
+            norm_gain[layer, 0][None], earlier, 3 if earlier is None else 5,
+        )
+        attn_sums = sums + attn_sums
+        extra = (ffn_grad, small, bias) if behind else ()
+        grad, attn_grad, bias, *sums = attention_layer_back(
+            count, behind, last, low, du, wout_back[layer], *first, wqkv_back[layer], prefix, extra,
+            6 if last else 4,
+        )
+        if behind:
+            earlier = attn_grad
+            ffn_sums.insert(0, sums[0])
+            small_sums.insert(0, sums[1])
+            if last:
+                attn_sums.insert(0, sums[2])
+                small_sums.insert(0, sums[3])
+        attn_grads.insert(0, attn_grad)
+        ffn_grads.insert(0, ffn_grad)
+        smalls.insert(0, small)
+        biases.insert(0, bias)
+
+    def head_columns(rows):
+        return rows.reshape(layer_count, 2, heads, 2, HDIM)[:, :, :, 0].reshape(layer_count, 2, depth)
+
+    if behind:
+        attn_sum, ffn_sum = jnp.stack(attn_sums), jnp.stack(ffn_sums)
+        shared = jnp.stack([each[:6] for each in small_sums[1:]])
+        bias_qv_sum = head_columns(jnp.stack([each[7] for each in small_sums[: layer_count]]))
+        bias_up_sum = jnp.stack([each[6] for each in small_sums[1:]])
+    else:
+        attn_sum = lax.psum_scatter(jnp.stack(attn_grads), "dp", scatter_dimension=1, tiled=True)
+        ffn_sum = lax.psum_scatter(jnp.stack(ffn_grads), "dp", scatter_dimension=1, tiled=True)
+        shared = lax.psum(jnp.stack(smalls)[:, :6], ("dp", "tensor"))
+        bias_qv_sum, bias_up_sum = lax.psum(
+            (head_columns(jnp.stack(biases)[:, 7]), jnp.stack(smalls)[:, 6]), "dp"
+        )
+    units = w_up.shape[2]
+    mine = attn_sum.shape[1]
     return (
         state,
-        grad_state,
-        summed_qkv,
-        summed_bias_qv,
-        summed_out,
-        summed_bias_out,
-        summed_gain,
-        summed_shift,
-        summed_up,
-        summed_bias_up,
-        summed_down,
-        summed_bias_down,
+        grad,
+        jnp.moveaxis(attn_sum[:, :, depth:].reshape(layer_count, mine, 3, depth), 2, 1),
+        bias_qv_sum,
+        jnp.swapaxes(attn_sum[:, :, :depth], 1, 2),
+        shared[:, 5],
+        jnp.stack([shared[:, 3], shared[:, 1]], axis=1),
+        jnp.stack([shared[:, 4], shared[:, 2]], axis=1),
+        ffn_sum[:, :, :units],
+        bias_up_sum,
+        jnp.swapaxes(ffn_sum[:, :, units:], 1, 2),
+        shared[:, 0],
     )
 
 

time: 954 us -> 382 us (0.40)
  the two profiles are of different devices: /device:TPU:0 before, /device:TPU:4 now
where the time goes in v2:
time: 382 us; the launch traced here: 376 us
  Pallas kernels  337 us (88%)
  local copies, waits for them, and re-layouts  28.5 us (7%)
  other arithmetic  8.19 us (2%)
    pallas_call x2, Pallas kernels, attention_layer_back(): pl.pallas_call(functools.partial(attention_backward_kernel, count, behind...  126 us
    pallas_call x2, Pallas kernels, ffn_layer(): pl.pallas_call(ffn_forward_kernel, out_shape=(shape((rows, width)), shape...  76.6 us
    pallas_call x2, Pallas kernels, ffn_layer_back(): pl.pallas_call(functools.partial(ffn_backward_kernel, count, behind), out...  72.5 us
    pallas_call x2, Pallas kernels, attention_layer(): pl.pallas_call(attention_forward_kernel, out_shape=(shape((rows, width)),...  62 us

profile of v2, /device:TPU:4, one launch (start us, length us, event | category | flops | bytes accessed | tf_op | source)
XLA Modules:
  0.0 375.5 jit_solution(6182910120430423536)
XLA Ops:
  0.6 1.9 convert_element_type.6.state_ref
  2.6 1.7 broadcast_multiply_fusion
  4.9 2.2 copy.31.wqkv_ref
  7.5 0.7 broadcast_in_dim.42.bias_ref
  8.2 1.9 slice_bitcast_fusion.4
  10.1 1.4 fusion.12
  11.5 1.4 slice_bitcast_fusion.10
  13.6 31.0 %attention_fwd.2 = (f32[256,768]{1,0:T(8,128)}, bf16[256,768]{1,0:T(8,128)(2,1)}, f32[256,768]{1,0:T(8,128)}, f32[256,128]{1,0:T(8,128)}, bf16[4,256,768]{2,1,0:...) custom-call(f32[256,768]{1,0:T(8,128)} %convert_element_type.6.state, ...), custom_call_target="tpu_custom_call" | custom-call | tf_op jit(solution)/shard_map/attention_fwd/pallas_call | solution.py:293
  44.6 3.9 %slice_bitcast_fusion = (bf16[768,768]{1,0:T(8,128)(2,1)}, bf16[768,768]{1,0:T(8,128)(2,1)}, bf16[768,768]{1,0:T(8,128)(2,1)}, bf16[768,768]{1,0:T(8,128)(2,1)}) fusion(bf16[2,768,768]{2,1,0:T(8,128)(2,1)S(1)} %copy-done.2, bf16[2,768,768]{2,1,0:T(8,128)(2,1)} %param.23), kind=kLoop, calls=%fused_computation.2 | loop fusion | bytes 9437184 | tf_op jit(solution)/shard_map/squeeze | solution.py:1093
  49.1 38.2 %ffn_fwd.2 = (f32[256,768]{1,0:T(8,128)}, bf16[256,768]{1,0:T(8,128)(2,1)}, f32[256,768]{1,0:T(8,128)}, f32[256,128]{1,0:T(8,128)}, bf16[4,256,768]{2,1,0:T(8,12...) custom-call(f32[256,768]{1,0:T(8,128)} %get-tuple-element.68.state_ref, ...), custom_call_target="tpu_custom_call" | custom-call | tf_op jit(solution)/shard_map/ffn_fwd/pallas_call | solution.py:406
  87.3 2.2 copy.32.wqkv_ref
  89.5 0.7 broadcast_in_dim.44.bias_ref
  90.2 31.0 %attention_fwd.3 = (f32[256,768]{1,0:T(8,128)}, bf16[256,768]{1,0:T(8,128)(2,1)}, f32[256,768]{1,0:T(8,128)}, f32[256,128]{1,0:T(8,128)}, bf16[4,256,768]{2,1,0:...) custom-call(f32[256,768]{1,0:T(8,128)} %get-tuple-element.70.state_r, ...), custom_call_target="tpu_custom_call" | custom-call | tf_op jit(solution)/shard_map/attention_fwd/pallas_call | solution.py:293
  121.2 38.5 %ffn_fwd.3 = (f32[256,768]{1,0:T(8,128)}, bf16[256,768]{1,0:T(8,128)(2,1)}, f32[256,768]{1,0:T(8,128)}, f32[256,128]{1,0:T(8,128)}, bf16[4,256,768]{2,1,0:T(8,12...) custom-call(f32[256,768]{1,0:T(8,128)} %get-tuple-element.72.state_ref, ...), custom_call_target="tpu_custom_call" | custom-call | tf_op jit(solution)/shard_map/ffn_fwd/pallas_call | solution.py:406
  159.7 0.9 convert_element_type.7.refs_0_
  160.6 32.0 %ffn_bwd.2 = (f32[256,768]{1,0:T(8,128)}, bf16[256,768]{1,0:T(8,128)(2,1)}, f32[768,1536]{1,0:T(8,128)}, f32[8,768]{1,0:T(8,128)}) custom-call(f32[256,768]{1,0:T(8,128)} %convert_element_type.7.refs_0_, f32[256,768]{1,0:T(8,128)} %get-tuple-element.75.refs_1_, f32[256,128]{1,0:T(8,128)} %get-tuple-element.76.refs_2_, ...), custom_call_target="tpu_custom_call" | custom-call | tf_op jit(solution)/shard_map/ffn_bwd/pallas_call | solution.py:819
  192.7 1.1 copy.33.refs_2_
  194.7 2.1 fusion.6
  196.8 0.6 broadcast_in_dim.49.refs_15_
  197.5 56.5 %attention_bwd.2 = (f32[256,768]{1,0:T(8,128)}, f32[768,768]{1,0:T(8,128)}, f32[8,768]{1,0:T(8,128)}, f32[96,1536]{1,0:T(8,128)}, f32[8,768]{1,0:T(8,128)}) custom-call(bf16[256,768]{1,0:T(8,128)(2,1)} %get-tuple-element.82.refs_0_, f32[256,768]{1,0:T(8,128)} %get-tuple-element.83.refs_1_, bf16[768,384]{1,0:T(8,128)(2,1)} %copy.33.refs_2_, ...), custom_call_target="tpu_custom_call" | custom-call | tf_op jit(solution)/shard_map/attention_bwd/pallas_call | solution.py:1048
  254.0 40.4 %ffn_bwd.3 = (f32[256,768]{1,0:T(8,128)}, bf16[256,768]{1,0:T(8,128)(2,1)}, f32[768,1536]{1,0:T(8,128)}, f32[8,768]{1,0:T(8,128)}, f32[96,768]{1,0:T(8,128)}) custom-call(f32[256,768]{1,0:T(8,128)} %get-tuple-element.94.refs_0_, f32[256,768]{1,0:T(8,128)} %get-tuple-element.95.refs_1_, f32[256,128]{1,0:T(8,128)} %get-tuple-element.96.refs_2_, ...), custom_call_target="tpu_custom_call" | custom-call | tf_op jit(solution)/shard_map/ffn_bwd/pallas_call | solution.py:819
  294.5 1.1 copy.34.refs_2_
  295.5 69.2 %attention_bwd.3 = (f32[256,768]{1,0:T(8,128)}, f32[768,768]{1,0:T(8,128)}, f32[8,768]{1,0:T(8,128)}, f32[96,1536]{1,0:T(8,128)}, f32[8,768]{1,0:T(8,128)}, /*index=5*/f32[96,768]{1,0:T(8,128)}, f32[8,768]{1,0:T(8,128)}) custom-call(bf16[256,768]{1,0:T(8,128)(2,1)} %get-tuple-element.103.refs_0_, f32[256,768]{1,0:T(8,128)} %get-tuple-element.104.refs_1_, ...), custom_call_target="tpu_custom_call" | custom-call | tf_op jit(solution)/shard_map/attention_bwd/pallas_call | solution.py:1048
  364.8 1.2 fusion.2
  366.3 1.1 copy.36
  367.3 0.7 slice.208
  368.2 0.7 reshape_squeeze.3
  368.9 0.8 copy.37
  370.4 0.6 fusion.4
  371.0 1.1 fusion.1
  373.3 0.9 copy.47
  374.2 0.9 copy.48
  (60 shorter events, 4.9 us)
Async XLA Ops:
  4.9 2.2 copy-start.15
  4.9 6.6 %copy-start.12 = (f32[2,2,768]{2,1,0:T(2,128)S(1)}, f32[2,2,768]{2,1,0:T(2,128)}, u32[]{:S(2)}) copy-start(f32[2,2,768]{2,1,0:T(2,128)} %param.22) | copy-start | bytes 36868
  10.1 34.5 %copy-start.2 = (bf16[2,768,768]{2,1,0:T(8,128)(2,1)S(1)}, bf16[2,768,768]{2,1,0:T(8,128)(2,1)}, u32[]{:S(2)}) copy-start(bf16[2,768,768]{2,1,0:T(8,128)(2,1)} %param.25) | copy-start | bytes 7077892
  44.6 3.9 %copy-start.13 = (f32[2,768]{1,0:T(2,128)S(1)}, f32[2,768]{1,0:T(2,128)}, u32[]{:S(2)}) copy-start(f32[2,768]{1,0:T(2,128)} %param.26) | copy-start | bytes 18436
  44.6 3.9 %copy-start.14 = (f32[2,768]{1,0:T(2,128)S(1)}, f32[2,768]{1,0:T(2,128)}, u32[]{:S(2)}) copy-start(f32[2,768]{1,0:T(2,128)} %param.24) | copy-start | bytes 18436
  121.2 38.5 %copy-start.9 = (bf16[256,768]{1,0:T(8,128)(2,1)S(1)}, bf16[256,768]{1,0:T(8,128)(2,1)}, u32[]{:S(2)}) copy-start(bf16[256,768]{1,0:T(8,128)(2,1)} %param.15) | copy-start | bytes 1179652
  160.6 32.0 %copy-start.1 = (bf16[2,192,768]{2,1,0:T(8,128)(2,1)S(1)}, bf16[2,192,768]{2,1,0:T(8,128)(2,1)}, u32[]{:S(2)}) copy-start(bf16[2,192,768]{2,1,0:T(8,128)(2,1)} %param.19) | copy-start | bytes 1769476
  192.6 1.7 copy-start
  295.5 69.3 %copy-start.3 = (f32[96,768]{1,0:T(8,128)S(1)}, f32[96,768]{1,0:T(8,128)}, u32[]{:S(2)}) copy-start(f32[96,768]{1,0:T(8,128)} %get-tuple-element.118) | copy-start | bytes 884740
  364.8 2.6 copy-start.10
  364.8 4.1 %copy-start.4 = (f32[96,768]{1,0:T(8,128)S(1)}, f32[96,768]{1,0:T(8,128)}, u32[]{:S(2)}) copy-start(f32[96,768]{1,0:T(8,128)} %get-tuple-element.117) | copy-start | bytes 884740
  366.0 3.7 copy-start.11
  366.0 5.0 %copy-start.7 = (f32[96,1536]{1,0:T(8,128)S(1)}, f32[96,1536]{1,0:T(8,128)}, u32[]{:S(2)}) copy-start(f32[96,1536]{1,0:T(8,128)} %get-tuple-element.123) | copy-start | bytes 1769476
  366.0 5.0 %copy-start.8 = (f32[96,1536]{1,0:T(8,128)S(1)}, f32[96,1536]{1,0:T(8,128)}, u32[]{:S(2)}) copy-start(f32[96,1536]{1,0:T(8,128)} %get-tuple-element.122) | copy-start | bytes 1769476
  368.9 4.4 %copy-start.5 = (f32[256,768]{1,0:T(8,128)S(1)}, f32[256,768]{1,0:T(8,128)}, u32[]{:S(2)}) copy-start(f32[256,768]{1,0:T(8,128)} %get-tuple-element.206) | copy-start | bytes 2359300
  371.0 3.2 copy-start.6

commit v3 on v2

v3 whole, which is shorter than its diff:
```python
import functools
import math

import jax
import jax.numpy as jnp
from jax import lax
from jax.experimental import pallas as pl
from jax.experimental.pallas import tpu as pltpu
from jax.sharding import PartitionSpec as P

HDIM = 64
LEN = 1024
MEM = 10
LANES = 128
GROUP = 4
PIECES = 2
EPSILON = 1e-06
VMEM_BYTES = 56 * 1024 * 1024
HIGHEST = lax.Precision.HIGHEST
MESH = pl.DeviceIdType.MESH
F32 = jnp.float32
BF16 = jnp.bfloat16
VM = pl.BlockSpec(memory_space=pltpu.VMEM)
SM = pl.BlockSpec(memory_space=pltpu.SMEM)
ANY = pl.BlockSpec(memory_space=pl.ANY)


def dot(left, right):
    return jnp.dot(left, right, preferred_element_type=F32)


def dot_nt(left, right):
    return lax.dot_general(left, right, (((1,), (1,)), ((), ())), preferred_element_type=F32)


def remote(src, dst, send_sem, recv_sem, tensor_index):
    return pltpu.make_async_remote_copy(
        src_ref=src,
        dst_ref=dst,
        send_sem=send_sem,
        recv_sem=recv_sem,
        device_id={"tensor": tensor_index},
        device_id_type=MESH,
    )


def places():
    mine = lax.axis_index("tensor")
    chip = mine // 2
    core = mine - 2 * chip
    partner = mine + 1 - 2 * core
    across = mine + 2 - 4 * chip
    diagonal = across + 1 - 2 * core
    return mine, partner, across, diagonal


class Refs:
    def __init__(self, refs):
        self.refs = list(refs)

    def take(self, count):
        taken, self.refs = self.refs[:count], self.refs[count:]
        return taken

    def one(self):
        return self.take(1)[0]


class Moves:
    def __init__(self, sems):
        self.sems, self.used, self.pending = sems, 0, []

    def start(self, source, target):
        move = pltpu.make_async_copy(source, target, self.sems.at[self.used])
        self.used += 1
        move.start()
        return move

    def store(self, source, target):
        self.pending.append(self.start(source, target))

    def finish(self):
        for move in self.pending:
            move.wait()


def remote_dp(src, dst, send_sem, recv_sem, dp_index):
    return pltpu.make_async_remote_copy(
        src_ref=src,
        dst_ref=dst,
        send_sem=send_sem,
        recv_sem=recv_sem,
        device_id={"dp": dp_index},
        device_id_type=MESH,
    )


class Sequences:
    def __init__(self, count):
        self.pairs = count // 2
        self.index = lax.axis_index("dp")
        self.pair = self.index // 2
        self.side = self.index - 2 * self.pair
        self.neighbour = self.index + 1 - 2 * self.side

    def other_pair(self, offset):
        return lax.rem(self.pair + offset, self.pairs)

    def peer(self, offset):
        return 2 * self.other_pair(offset) + self.side

    def everyone(self):
        return [self.neighbour] + [self.peer(offset) for offset in range(1, self.pairs)]


class Entry:
    def __init__(self, sequences=None):
        barrier = pltpu.get_barrier_semaphore()
        group = places()[1:]
        others = sequences.everyone() if sequences is not None else []
        for other in group:
            pl.semaphore_signal(barrier, inc=1, device_id={"tensor": other}, device_id_type=MESH)
        for other in others:
            pl.semaphore_signal(barrier, inc=1, device_id={"dp": other}, device_id_type=MESH)
        self.barrier, self.count = barrier, len(group) + len(others)

    def wait(self):
        pl.semaphore_wait(self.barrier, self.count)


class Gather:
    def __init__(self, whole, send_sems, recv_sems):
        self.whole = whole
        self.mine, self.partner, self.across, self.diagonal = places()
        self.rows = whole.shape[1] // PIECES
        self.send_sems, self.recv_sems = send_sems, recv_sems

    def piece(self, chunk, part):
        return self.whole.at[chunk, pl.ds(part * self.rows, self.rows)]

    def to_partner(self):
        return remote(
            self.whole.at[self.mine], self.whole.at[self.mine],
            self.send_sems.at[0], self.recv_sems.at[0], self.partner,
        )

    def to_across(self, part):
        return remote(
            self.piece(self.mine, part), self.piece(self.mine, part),
            self.send_sems.at[1 + part], self.recv_sems.at[1 + part], self.across,
        )

    def onward(self, part):
        return remote(
            self.piece(self.across, part), self.piece(self.across, part),
            self.send_sems.at[1 + PIECES + part], self.recv_sems.at[1 + PIECES + part], self.partner,
        )

    def start(self):
        for part in range(PIECES):
            self.to_across(part).start()
        self.to_partner().start()

    def wait_partner(self):
        remote(
            self.whole.at[self.partner], self.whole.at[self.partner],
            self.send_sems.at[0], self.recv_sems.at[0], self.partner,
        ).wait_recv()

    def wait_across(self, part):
        remote(
            self.piece(self.across, part), self.piece(self.across, part),
            self.send_sems.at[1 + part], self.recv_sems.at[1 + part], self.across,
        ).wait_recv()

    def wait_diagonal(self, part):
        remote(
            self.piece(self.diagonal, part), self.piece(self.diagonal, part),
            self.send_sems.at[1 + PIECES + part], self.recv_sems.at[1 + PIECES + part], self.partner,
        ).wait_recv()

    def wait_sends(self):
        self.to_partner().wait_send()
        for part in range(PIECES):
            self.to_across(part).wait_send()
            self.onward(part).wait_send()


GATHER_SEMS = 1 + 2 * PIECES


def shape(dims, kind=F32):
    return jax.ShapeDtypeStruct(dims, kind)


def dma_sems(*dims):
    return pltpu.SemaphoreType.DMA(dims)


def params(collective_id):
    return pltpu.CompilerParams(
        collective_id=collective_id, has_side_effects=True, vmem_limit_bytes=VMEM_BYTES
    )


def layer_norm(total, gain, shift):
    row_mean = jnp.mean(total, axis=-1, keepdims=True)
    centered = total - row_mean
    spread = jnp.mean(centered * centered, axis=-1, keepdims=True)
    recip = lax.rsqrt(spread + EPSILON)
    normal = centered * recip
    return normal * gain + shift, normal, recip


def visible_keys(chunk, rows):
    first, last = chunk * rows, (chunk + 1) * rows - 1
    if first < MEM or last >= LEN - MEM:
        return LEN
    return max(last + 1, LEN // 2)


def query_limits(chunk, rows, prefix_len):
    spots = chunk * rows + lax.broadcasted_iota(jnp.int32, (1, rows), 1)
    limits = jnp.maximum(spots, prefix_len - 1)
    return jnp.where((spots < MEM) | (spots >= LEN - MEM), LEN - 1, limits)


def transposed(values):
    return values.astype(F32).T


def head_pairs(values, heads):
    wide = []
    for head in range(heads):
        columns = values[:, head * HDIM : (head + 1) * HDIM]
        wide.append(jnp.concatenate([columns, columns], axis=1))
    return wide


class Exchange:
    def __init__(self, terms, near, relay, total, far, sems):
        self.terms, self.near, self.relay, self.total, self.far = terms, near, relay, total, far
        self.n_send, self.n_recv, self.r_send, self.r_recv, self.f_send, self.f_recv = sems
        self.mine, self.partner, self.across, self.diagonal = places()
        self.rows = terms.shape[1] // PIECES

    def spot(self, part):
        return pl.ds(part * self.rows, self.rows)

    def near_copy(self, part):
        return remote(
            self.terms.at[self.partner, self.spot(part)], self.near.at[self.spot(part)],
            self.n_send.at[part], self.n_recv.at[part], self.partner,
        )

    def relay_copy(self, part):
        return remote(
            self.terms.at[self.diagonal, self.spot(part)], self.relay.at[self.spot(part)],
            self.r_send.at[part], self.r_recv.at[part], self.partner,
        )

    def far_copy(self, part):
        return remote(
            self.total.at[self.spot(part)], self.far.at[self.spot(part)],
            self.f_send.at[part], self.f_recv.at[part], self.across,
        )

    def pass_on(self, part):
        spot = self.spot(part)
        self.relay_copy(part).wait_recv()
        self.total[spot] = (self.terms[self.across, spot] + self.relay[spot]).astype(self.total.dtype)
        self.far_copy(part).start()

    def result(self, part):
        spot = self.spot(part)
        self.near_copy(part).wait_recv()
        self.far_copy(part).wait_recv()
        return (self.terms[self.mine, spot] + self.near[spot]) + self.far[spot].astype(F32)

    def wait_sends(self):
        for part in range(PIECES):
            self.near_copy(part).wait_send()
            self.relay_copy(part).wait_send()
            self.far_copy(part).wait_send()


def exchange_scratch(rows, width, kind):
    return [
        pltpu.VMEM((GROUP, rows, width), F32),
        pltpu.VMEM((rows, width), F32), pltpu.VMEM((rows, width), F32),
        pltpu.VMEM((rows, width), kind), pltpu.VMEM((rows, width), kind),
    ] + [dma_sems(PIECES)] * 6


def attention_forward_kernel(layer, *refs):
    refs = Refs(refs)
    state_hbm, low_ref, wqkv_hbm, bias_ref, wout_hbm, bias_out_ref, gain_ref, shift_ref, prefix_ref = refs.take(9)
    next_ref, next_low_ref, normal_ref, recip_ref = refs.take(4)
    saved_hbm = refs.take(8)
    saved = refs.take(8)
    whole_ref, qt_ref, q2_ref, kz_ref, kt_ref, v2_ref, ct_ref, stats_ref = saved
    state_ref, wqkv_ref, vt_ref, cf_ref, wo_ref = refs.take(5)
    moves = Moves(refs.one())
    g_send, g_recv, c_send, c_recv, w_send, w_recv = refs.take(6)
    mine, partner, across, diagonal = places()
    rows = low_ref.shape[0]
    heads = qt_ref.shape[0]
    root = 1.0 / math.sqrt(HDIM)
    entry = Entry()
    wqkv_in = moves.start(wqkv_hbm.at[layer], wqkv_ref)
    wout_in = moves.start(wout_hbm.at[layer], wo_ref.at[mine])
    state_in = moves.start(state_hbm, state_ref)
    gather = Gather(whole_ref, g_send, g_recv)
    whole_ref[mine] = low_ref[...]
    entry.wait()
    gather.start()
    lane_low = lax.broadcasted_iota(jnp.int32, (rows, LANES), 1) < HDIM

    def project(chunk):
        spots = pl.ds(pl.multiple_of(chunk * rows, rows), rows)
        values = whole_ref[chunk]
        query = (dot(values, wqkv_ref[0]) + bias_ref[layer, 0:1]) * root
        key = dot(values, wqkv_ref[1])
        value = dot(values, wqkv_ref[2]) + bias_ref[layer, 1:2]
        queries, keys, valuess = [head_pairs(each, heads) for each in (query, key, value)]
        query_t, key_t, value_t = [each.T.astype(BF16) for each in (query, key, value)]
        for head in range(heads):
            part = slice(head * HDIM, (head + 1) * HDIM)
            q2_ref[head, spots] = queries[head].astype(BF16)
            kz_ref[head, spots] = jnp.where(lane_low, keys[head], 0.0).astype(BF16)
            v2_ref[head, spots] = valuess[head].astype(BF16)
            for half in (slice(0, HDIM), slice(HDIM, 2 * HDIM)):
                qt_ref[head, half, spots] = query_t[part]
                kt_ref[head, half, spots] = key_t[part]
            vt_ref[head, :, spots] = value_t[part]

    def wout_to_partner(source):
        slot = 0 if source is mine else 2
        return remote(wo_ref.at[source], wo_ref.at[source], w_send.at[slot], w_recv.at[slot], partner)

    wout_to_across = remote(wo_ref.at[mine], wo_ref.at[mine], w_send.at[1], w_recv.at[1], across)
    wout_from_across = remote(wo_ref.at[across], wo_ref.at[across], w_send.at[1], w_recv.at[1], across)
    wout_from_partner = remote(wo_ref.at[partner], wo_ref.at[partner], w_send.at[0], w_recv.at[0], partner)
    wout_from_diagonal = remote(wo_ref.at[diagonal], wo_ref.at[diagonal], w_send.at[2], w_recv.at[2], partner)

    wqkv_in.wait()
    project(mine)
    gather.wait_partner()
    project(partner)
    wout_in.wait()
    for part in range(PIECES):
        gather.wait_across(part)
        gather.onward(part).start()
    wout_to_across.start()
    wout_to_partner(mine).start()
    project(across)
    for part in range(PIECES):
        gather.wait_diagonal(part)
    project(diagonal)
    for source, target in zip(saved[:6], saved_hbm[:6]):
        moves.store(source, target)

    def context_copy(step, chunk):
        return remote(ct_ref.at[chunk], cf_ref.at[mine], c_send.at[step], c_recv.at[step], chunk)

    def context_from(step, chunk):
        return remote(ct_ref.at[mine], cf_ref.at[chunk], c_send.at[step], c_recv.at[step], chunk)

    def attend(chunk):
        keys = visible_keys(chunk, rows)
        limits = query_limits(chunk, rows, prefix_ref[0])
        visible = lax.broadcasted_iota(jnp.int32, (keys, rows), 0) <= limits
        spots = pl.ds(chunk * rows, rows)

        def one_head(head, carry):
            scores = dot(kz_ref[head, pl.ds(0, keys)], qt_ref[head, :, spots])
            scores = jnp.where(visible, scores, -1e30)
            top = jnp.max(scores, axis=0, keepdims=True)
            expo = jnp.exp(scores - top)
            recip = 1.0 / jnp.sum(expo, axis=0, keepdims=True)
            probs = (expo * recip).astype(BF16)
            context = dot(vt_ref[head, :, pl.ds(0, keys)], probs)
            ct_ref[chunk, pl.ds(pl.multiple_of(head * HDIM, HDIM), HDIM)] = context.astype(BF16)
            first = lax.broadcasted_iota(jnp.int32, (8, rows), 0) == 0
            stats_ref[head, :, spots] = jnp.where(first, top, recip)
            return carry

        lax.fori_loop(0, heads, one_head, 0)

    chip, core = mine // 2, mine - 2 * (mine // 2)

    def one_step(step, carry):
        near = step // 2
        flip = lax.rem(lax.rem(step, 2) + near, 2)
        to_chip = (1 - near) * (1 - chip) + near * chip
        chunk = 2 * to_chip + core + flip * (1 - 2 * core)
        for each in range(GROUP):
            @pl.when(chunk == each)
            def _():
                attend(each)

        @pl.when(step < 3)
        def _():
            context_copy(step, chunk).start()

        @pl.when(step == 1)
        def _():
            wout_from_across.wait_recv()
            wout_to_partner(across).start()
        return carry

    lax.fori_loop(0, GROUP, one_step, 0)
    for source, target in zip(saved[6:], saved_hbm[6:]):
        moves.store(source, target)
    cf_ref[mine] = ct_ref[mine]
    wout_from_partner.wait_recv()
    wout_from_diagonal.wait_recv()
    for step, chunk in enumerate((across, diagonal, partner)):
        context_from(step, chunk).wait_recv()
    depth = GROUP * wo_ref.shape[1]
    context = transposed(cf_ref[...].reshape(depth, rows)).astype(BF16)
    state_in.wait()
    total = (
        state_ref[...].astype(F32) + dot(context, wo_ref[...].reshape(depth, -1)) + bias_out_ref[layer : layer + 1]
    )
    result, normal, recip = layer_norm(total, gain_ref[layer, 0:1], shift_ref[layer, 0:1])
    next_ref[...] = result
    next_low_ref[...] = result.astype(BF16)
    normal_ref[...] = normal
    recip_ref[...] = jnp.broadcast_to(recip, recip_ref.shape)
    gather.wait_sends()
    wout_to_across.wait_send()
    wout_to_partner(mine).wait_send()
    wout_to_partner(across).wait_send()
    for step, chunk in enumerate((across, diagonal, partner)):
        context_copy(step, chunk).wait_send()
    moves.finish()


def attention_layer(layer, state, low, wqkv, bias, wout, bias_out, gain, shift, prefix):
    rows, width = low.shape
    depth = wout.shape[1]
    heads = depth // HDIM
    tall = GROUP * rows
    saved = [
        ((GROUP, rows, width), BF16),
        ((heads, LANES, tall), BF16), ((heads, tall, LANES), BF16), ((heads, tall, LANES), BF16),
        ((heads, LANES, tall), BF16), ((heads, tall, LANES), BF16), ((GROUP, depth, rows), BF16),
        ((heads, 8, tall), F32),
    ]
    return pl.pallas_call(
        functools.partial(attention_forward_kernel, layer),
        out_shape=[
            shape((rows, width)), shape((rows, width), BF16), shape((rows, width)), shape((rows, LANES)),
        ] + [shape(*each) for each in saved],
        in_specs=[ANY, VM, ANY, VM, ANY, VM, VM, VM, SM],
        out_specs=[VM] * 4 + [ANY] * 8,
        scratch_shapes=[pltpu.VMEM(*each) for each in saved] + [
            pltpu.VMEM((rows, width), state.dtype),
            pltpu.VMEM(wqkv.shape[1:], BF16),
            pltpu.VMEM((heads, HDIM, tall), BF16),
            pltpu.VMEM((GROUP, depth, rows), BF16),
            pltpu.VMEM((GROUP, depth, width), BF16),
            dma_sems(11),
            dma_sems(GATHER_SEMS), dma_sems(GATHER_SEMS),
            dma_sems(3), dma_sems(3), dma_sems(3), dma_sems(3),
        ],
        compiler_params=params(1 + layer),
        name="attention_fwd",
    )(state, low, wqkv, bias, wout, bias_out, gain, shift, prefix)


def ffn_forward_kernel(layer, *refs):
    refs = Refs(refs)
    state_hbm, low_ref, wup_hbm, bias_up_ref, wdown_hbm, bias_down_ref, gain_ref, shift_ref = refs.take(8)
    next_ref, next_low_ref, normal_ref, recip_ref = refs.take(4)
    saved_hbm = refs.take(3)
    whole_ref, active_ref, slope_ref = refs.take(3)
    state_ref, wup_ref, wdown_ref = refs.take(3)
    moves = Moves(refs.one())
    exchange_refs = refs.take(11)
    g_send, g_recv = refs.take(2)
    mine, partner, across, diagonal = places()
    rows = low_ref.shape[0]
    part_rows = rows // PIECES
    entry = Entry()
    wup_in = moves.start(wup_hbm.at[layer], wup_ref)
    wdown_in = moves.start(wdown_hbm.at[layer], wdown_ref)
    state_in = moves.start(state_hbm, state_ref)
    gather = Gather(whole_ref, g_send, g_recv)
    whole_ref[mine] = low_ref[...]
    entry.wait()
    gather.start()
    exchange = Exchange(*exchange_refs[:5], exchange_refs[5:])
    terms_ref = exchange.terms

    def units(chunk, part):
        spot = exchange.spot(part)
        hidden = dot(whole_ref[chunk, spot], wup_ref[...]) + bias_up_ref[layer : layer + 1]
        below = 0.5 * (1.0 + lax.erf(hidden * math.sqrt(0.5)))
        density = jnp.exp(-0.5 * hidden * hidden) * (1.0 / math.sqrt(2.0 * math.pi))
        active = (hidden * below).astype(BF16)
        active_ref[chunk, spot] = active
        slope_ref[chunk, spot] = below + hidden * density
        terms_ref[chunk, spot] = dot(active, wdown_ref[...])

    wup_in.wait()
    wdown_in.wait()
    for part in range(PIECES):
        units(mine, part)
    for part in range(PIECES):
        gather.wait_across(part)
        gather.onward(part).start()
        units(across, part)
        gather.wait_diagonal(part)
        units(diagonal, part)
        exchange.relay_copy(part).start()
        if part > 0:
            exchange.pass_on(part - 1)
    gather.wait_partner()
    moves.store(whole_ref, saved_hbm[0])
    units(partner, 0)
    exchange.near_copy(0).start()
    exchange.pass_on(PIECES - 1)
    for part in range(1, PIECES):
        units(partner, part)
        exchange.near_copy(part).start()
    moves.store(active_ref, saved_hbm[1])
    moves.store(slope_ref, saved_hbm[2])
    state_in.wait()
    for part in range(PIECES):
        spot = exchange.spot(part)
        total = state_ref[spot] + exchange.result(part) + bias_down_ref[layer : layer + 1]
        result, normal, recip = layer_norm(total, gain_ref[layer, 1:2], shift_ref[layer, 1:2])
        next_ref[spot] = result
        next_low_ref[spot] = result.astype(BF16)
        normal_ref[spot] = normal
        recip_ref[spot] = jnp.broadcast_to(recip, (part_rows, LANES))
    gather.wait_sends()
    exchange.wait_sends()
    moves.finish()


def ffn_layer(layer, state, low, wup, bias_up, wdown, bias_down, gain, shift):
    rows, width = low.shape
    units = wup.shape[2]
    saved = [((GROUP, rows, width), BF16), ((GROUP, rows, units), BF16), ((GROUP, rows, units), F32)]
    return pl.pallas_call(
        functools.partial(ffn_forward_kernel, layer),
        out_shape=[
            shape((rows, width)), shape((rows, width), BF16), shape((rows, width)), shape((rows, LANES)),
        ] + [shape(*each) for each in saved],
        in_specs=[ANY, VM, ANY, VM, ANY, VM, VM, VM],
        out_specs=[VM] * 4 + [ANY] * 3,
        scratch_shapes=[pltpu.VMEM(*each) for each in saved]
        + [
            pltpu.VMEM((rows, width), F32), pltpu.VMEM(wup.shape[1:], BF16), pltpu.VMEM(wdown.shape[1:], BF16),
            dma_sems(6),
        ]
        + exchange_scratch(rows, width, F32)
        + [dma_sems(GATHER_SEMS), dma_sems(GATHER_SEMS)],
        compiler_params=params(3 + layer),
        name="ffn_fwd",
    )(state, low, wup, bias_up, wdown, bias_down, gain, shift)


def layer_norm_back(grad_in, normal, recip, gain):
    scaled = grad_in * gain
    inner = (
        scaled
        - jnp.mean(scaled, axis=-1, keepdims=True)
        - normal * jnp.mean(scaled * normal, axis=-1, keepdims=True)
    )
    return recip * inner


def column_sum(values):
    return jnp.sum(values, axis=0, keepdims=True)


def high_low(values):
    high = values.astype(BF16)
    return high, (values - high.astype(F32)).astype(BF16)


def dot_tn(left, right):
    return lax.dot_general(left, right, (((0,), (0,)), ((), ())), preferred_element_type=F32)


class PairSum:
    def __init__(self, sequences, source, half, columns, buffers, sems):
        self.at, self.source, self.half, self.columns = sequences, source, half, columns
        self.out, self.into = buffers
        self.sems = sems
        self.rows = half.shape[1]

    def terms(self, pair, side):
        start = pl.multiple_of((2 * pair + side) * self.rows, 16)
        return self.source[pl.ds(start, self.rows), self.columns]

    def copy(self):
        return remote_dp(
            self.out.at[:, :, self.columns], self.into.at[:, :, self.columns], *self.sems, self.at.neighbour
        )

    def start(self):
        for pair in range(self.at.pairs):
            self.out[pair, :, self.columns] = self.terms(pair, 1 - self.at.side).astype(BF16)
        self.copy().start()

    def finish(self):
        self.copy().wait_recv()
        for pair in range(self.at.pairs):
            own = self.terms(pair, self.at.side)
            self.half[pair, :, self.columns] = own + self.into[pair, :, self.columns].astype(F32)

    def wait_sends(self):
        self.copy().wait_send()


class OwnerSum:
    def __init__(self, sequences, half, result, columns, buffers, sems):
        self.at, self.half, self.result, self.columns = sequences, half, result, columns
        self.out, self.into = buffers
        self.sems = sems

    def copy(self, offset):
        return remote_dp(
            self.out.at[offset - 1, :, self.columns], self.into.at[offset - 1, :, self.columns],
            self.sems[0].at[offset - 1], self.sems[1].at[offset - 1], self.at.peer(offset),
        )

    def start(self):
        for offset in range(1, self.at.pairs):
            pair = self.at.other_pair(offset)
            self.out[offset - 1, :, self.columns] = self.half[pair, :, self.columns].astype(BF16)
            self.copy(offset).start()

    def finish(self):
        total = self.half[self.at.pair, :, self.columns]
        for offset in range(1, self.at.pairs):
            self.copy(offset).wait_recv()
            total = total + self.into[offset - 1, :, self.columns].astype(F32)
        self.result[:, self.columns] = total

    def wait_sends(self):
        for offset in range(1, self.at.pairs):
            self.copy(offset).wait_send()


def column_blocks(columns, blocks):
    step = columns // blocks
    return [slice(block * step, (block + 1) * step) for block in range(blocks)]


def pair_scratch(count, width, columns, blocks):
    dims = (count // 2, width // count, columns)
    return [pltpu.VMEM(dims, BF16), pltpu.VMEM(dims, BF16), dma_sems(blocks), dma_sems(blocks)]


def pair_sums(sequences, source, half, scratch, blocks):
    out, into, send, recv = scratch
    return [
        PairSum(sequences, source, half, columns, (out, into), (send.at[block], recv.at[block]))
        for block, columns in enumerate(column_blocks(source.shape[1], blocks))
    ]


def owner_scratch(count, width, columns, blocks):
    pairs = count // 2
    dims = (pairs - 1, width // count, columns)
    return [
        pltpu.VMEM(dims, BF16), pltpu.VMEM(dims, BF16), dma_sems(blocks, pairs - 1), dma_sems(blocks, pairs - 1)
    ]


def owner_sums(sequences, half, result, scratch, blocks):
    out, into, send, recv = scratch
    return [
        OwnerSum(sequences, half, result, columns, (out, into), (send.at[block], recv.at[block]))
        for block, columns in enumerate(column_blocks(result.shape[1], blocks))
    ]


class SmallSum:
    def __init__(self, sequences, source, result, shared_rows, slots, sems):
        self.at = sequences
        self.source, self.result, self.shared_rows = source, result, shared_rows
        self.group_slots, self.side_slots, self.pair_slots = slots
        self.g_send, self.g_recv, self.s_send, self.s_recv, self.p_send, self.p_recv = sems
        self.mine, self.partner, self.across, self.diagonal = places()

    def group_copy(self, index, to, slot):
        return remote(
            self.group_slots.at[slot], self.group_slots.at[slot],
            self.g_send.at[index], self.g_recv.at[index], to,
        )

    def start(self):
        if self.shared_rows:
            self.group_slots[self.mine] = self.source[...]
            for index, other in enumerate((self.partner, self.across, self.diagonal)):
                self.group_copy(index, other, self.mine).start()

    def side_copy(self, slot):
        return remote_dp(
            self.side_slots.at[slot], self.side_slots.at[slot],
            self.s_send.at[0], self.s_recv.at[0], self.at.neighbour,
        )

    def first(self):
        values = self.source[...]
        if self.shared_rows:
            for index, other in enumerate((self.partner, self.across, self.diagonal)):
                self.group_copy(index, other, other).wait_recv()
            total = self.group_slots[0]
            for slot in range(1, GROUP):
                total = total + self.group_slots[slot]
            shared = lax.broadcasted_iota(jnp.int32, values.shape, 0) < self.shared_rows
            values = jnp.where(shared, total, values)
        self.side_slots[self.at.side] = values
        self.side_copy(self.at.side).start()

    def pair_copy(self, offset, slot):
        return remote_dp(
            self.pair_slots.at[slot], self.pair_slots.at[slot],
            self.p_send.at[offset - 1], self.p_recv.at[offset - 1], self.at.peer(offset),
        )

    def second(self):
        self.side_copy(1 - self.at.side).wait_recv()
        self.pair_slots[self.at.pair] = self.side_slots[0] + self.side_slots[1]
        for offset in range(1, self.at.pairs):
            self.pair_copy(offset, self.at.pair).start()

    def third(self):
        for offset in range(1, self.at.pairs):
            self.pair_copy(offset, self.at.other_pair(self.at.pairs - offset)).wait_recv()
        total = self.pair_slots[0]
        for slot in range(1, self.at.pairs):
            total = total + self.pair_slots[slot]
        self.result[...] = total

    def wait_sends(self):
        if self.shared_rows:
            for index, other in enumerate((self.partner, self.across, self.diagonal)):
                self.group_copy(index, other, self.mine).wait_send()
        self.side_copy(self.at.side).wait_send()
        for offset in range(1, self.at.pairs):
            self.pair_copy(offset, self.at.pair).wait_send()


def small_sum_scratch(count, width):
    pairs = count // 2
    return [
        pltpu.VMEM((GROUP, 8, width), F32), pltpu.VMEM((2, 8, width), F32), pltpu.VMEM((pairs, 8, width), F32),
        dma_sems(3), dma_sems(3), dma_sems(1), dma_sems(1), dma_sems(pairs - 1), dma_sems(pairs - 1),
    ]


BLOCKS = 2


def ffn_backward_kernel(layer, count, split, behind, *refs):
    refs = Refs(refs)
    grad_ref, normal2_ref, recip2_ref, gain_ref, wdown_hbm, wup_hbm = refs.take(6)
    active_hbm, slope_hbm, normed_hbm, normal1_hbm, recip1_ref = refs.take(5)
    earlier_hbm = refs.one() if behind else None
    du_ref, low_ref, up_hbm, down_out, smalls_ref = refs.take(5)
    earlier_sum = refs.one() if behind else None
    df_ref, du2_ref, high_ref, lowbits_ref = refs.take(4)
    wdown_ref, wup_ref, active_ref, slope_ref, normed_ref, normal1_ref, up_ref, down_ref = refs.take(8)
    moves = Moves(refs.one())
    exchange_refs = refs.take(11)
    g_send, g_recv = refs.take(2)
    mine, partner, across, diagonal = places()
    rows, width = grad_ref.shape
    units = wup_ref.shape[1]
    tall = GROUP * rows
    sequences = Sequences(count) if split else None
    entry = Entry(sequences)
    wdown_in = moves.start(wdown_hbm.at[layer], wdown_ref)
    slope_in = moves.start(slope_hbm, slope_ref)
    wup_in = moves.start(wup_hbm.at[layer], wup_ref)
    earlier_pairs, earlier_owners, down_pairs = [], [], []
    if behind:
        earlier_ref, half_ref = refs.take(2)
        earlier_in = moves.start(earlier_hbm, earlier_ref)
        earlier_pairs = pair_sums(sequences, earlier_ref, half_ref, refs.take(4), BLOCKS)
        earlier_owners = owner_sums(sequences, half_ref, earlier_sum, refs.take(4), BLOCKS)
    if split:
        down_pairs = pair_sums(sequences, down_ref, down_out, refs.take(4), BLOCKS)
    active_in = moves.start(active_hbm, active_ref)
    normed_in = moves.start(normed_hbm, normed_ref)
    normal1_in = moves.start(normal1_hbm, normal1_ref)
    gather = Gather(df_ref, g_send, g_recv)
    exchange = Exchange(*exchange_refs[:5], exchange_refs[5:])
    terms_ref = exchange.terms
    grad = grad_ref[...].astype(F32)
    normal2 = normal2_ref[...]
    du2 = layer_norm_back(grad, normal2, recip2_ref[:, :1], gain_ref[layer, 1:2])
    du2_ref[...] = du2
    df_ref[mine] = du2.astype(BF16)
    entry.wait()
    gather.start()
    smalls_ref[0:1] = column_sum(du2)
    smalls_ref[1:2] = column_sum(grad * normal2)
    smalls_ref[2:3] = column_sum(grad)
    smalls_ref[6:8] = jnp.zeros((2, width), F32)
    if behind:
        earlier_in.wait()
        for item in earlier_pairs:
            item.start()

    def back(chunk, part):
        spot = exchange.spot(part)
        grad_active = dot_nt(df_ref[chunk, spot], wdown_ref[...])
        grad_hidden = grad_active * slope_ref[chunk, spot]
        smalls_ref[6:7] = smalls_ref[6:7] + column_sum(grad_hidden)
        high, low = high_low(grad_hidden)
        high_ref[chunk, spot] = high
        lowbits_ref[chunk, spot] = low
        terms_ref[chunk, spot] = dot_nt(high, wup_ref[...]) + dot_nt(low, wup_ref[...])

    wdown_in.wait()
    slope_in.wait()
    wup_in.wait()
    for part in range(PIECES):
        back(mine, part)
    for part in range(PIECES):
        gather.wait_across(part)
        gather.onward(part).start()
        back(across, part)
        gather.wait_diagonal(part)
        back(diagonal, part)
        exchange.relay_copy(part).start()
        if part > 0:
            exchange.pass_on(part - 1)
    gather.wait_partner()
    back(partner, 0)
    exchange.near_copy(0).start()
    exchange.pass_on(PIECES - 1)
    for pair, owner in zip(earlier_pairs, earlier_owners):
        pair.finish()
        owner.start()
    active_in.wait()
    down_ref[...] = dot_tn(df_ref[...].reshape(tall, width), active_ref[...].reshape(tall, units))
    if split:
        for item in down_pairs:
            item.start()
    else:
        moves.store(down_ref, down_out)
    for part in range(1, PIECES):
        back(partner, part)
        exchange.near_copy(part).start()
    normed_in.wait()
    normed = normed_ref[...].reshape(tall, width)
    up_ref[...] = dot_tn(normed, high_ref[...].reshape(tall, units)) + dot_tn(
        normed, lowbits_ref[...].reshape(tall, units)
    )
    moves.store(up_ref, up_hbm)
    normal1_in.wait()
    for part in range(PIECES):
        spot = exchange.spot(part)
        grad_normed = exchange.result(part) + du2_ref[spot]
        normal1 = normal1_ref[spot]
        du = layer_norm_back(grad_normed, normal1, recip1_ref[spot, :1], gain_ref[layer, 0:1])
        du_ref[spot] = du
        low_ref[spot] = du.astype(BF16)
        sums = (column_sum(grad_normed * normal1), column_sum(grad_normed), column_sum(du))
        for index, value in enumerate(sums):
            place = slice(3 + index, 4 + index)
            smalls_ref[place] = value if part == 0 else smalls_ref[place] + value
    for item in earlier_owners + down_pairs:
        item.finish()
    gather.wait_sends()
    exchange.wait_sends()
    for item in earlier_pairs + earlier_owners + down_pairs:
        item.wait_sends()
    moves.finish()


def ffn_layer_back(layer, count, split, grad, normal2, recip2, gain, wdown, wup, active, slope, normed, normal1, recip1, earlier):
    rows, width = grad.shape
    units = wup.shape[2]
    behind = split and earlier is not None
    share = width // count
    down = (count // 2, share, units) if split else (width, units)
    outs = [
        shape((rows, width)), shape((rows, width), BF16), shape((width, units)), shape(down), shape((8, width)),
    ]
    out_specs = [VM, VM, ANY, VM if split else ANY, VM]
    scratch = [
        pltpu.VMEM((GROUP, rows, width), BF16),
        pltpu.VMEM((rows, width), F32),
        pltpu.VMEM((GROUP, rows, units), BF16), pltpu.VMEM((GROUP, rows, units), BF16),
        pltpu.VMEM(wdown.shape[1:], BF16), pltpu.VMEM(wup.shape[1:], BF16),
        pltpu.VMEM(active.shape, BF16), pltpu.VMEM(slope.shape, F32), pltpu.VMEM(normed.shape, BF16),
        pltpu.VMEM((rows, width), F32), pltpu.VMEM((width, units), F32), pltpu.VMEM((width, units), F32),
        dma_sems(9),
    ]
    scratch += exchange_scratch(rows, width, BF16) + [dma_sems(GATHER_SEMS), dma_sems(GATHER_SEMS)]
    extra = []
    if behind:
        extra = [earlier]
        columns = earlier.shape[1]
        outs.append(shape((share, columns)))
        out_specs.append(VM)
        scratch += [pltpu.VMEM((width, columns), F32), pltpu.VMEM((count // 2, share, columns), F32)]
        scratch += pair_scratch(count, width, columns, BLOCKS) + owner_scratch(count, width, columns, BLOCKS)
    if split:
        scratch += pair_scratch(count, width, units, BLOCKS)
    return pl.pallas_call(
        functools.partial(ffn_backward_kernel, layer, count, split, behind),
        out_shape=outs,
        in_specs=[VM] * 4 + [ANY] * 6 + [VM] + [ANY] * len(extra),
        out_specs=out_specs,
        scratch_shapes=scratch,
        compiler_params=params(5 + layer),
        name="ffn_bwd",
    )(grad, normal2, recip2, gain, wdown, wup, active, slope, normed, normal1, recip1, *extra)


def attention_backward_kernel(layer, count, split, last, *refs):
    refs = Refs(refs)
    low_ref, du_hbm, wout_hbm, wqkv_hbm = refs.take(4)
    saved_hbm = refs.take(8)
    prefix_ref = refs.one()
    up_hbm, half_hbm, smalls_in, bias_in = refs.take(4) if split else (None,) * 4
    dx_ref, grads_hbm, bias_ref = refs.take(3)
    up_sum, down_sum, smalls_sum = refs.take(3) if split else (None,) * 3
    grads_sum, bias_sum = refs.take(2) if last else (None,) * 2
    saved = refs.take(8)
    whole_ref, qt_ref, q2_ref, kz_ref, kt_ref, v2_ref, ct_ref, stats_ref = saved
    du_ref, wout_ref, wqkv_ref, grads_ref = refs.take(4)
    do_ref, dc_ref, dct_ref, dq_ref, dk_ref, dv_ref, high_ref, lowbits_ref, xt_ref = refs.take(9)
    moves = Moves(refs.one())
    exchange_refs = refs.take(11)
    g_send, g_recv = refs.take(2)
    mine, partner, across, diagonal = places()
    rows, width = low_ref.shape
    heads = qt_ref.shape[0]
    depth = heads * HDIM
    scale = 1.0 / math.sqrt(HDIM)
    sequences = Sequences(count) if split else None
    entry = Entry(sequences)
    wout_in = moves.start(wout_hbm.at[layer], wout_ref)
    saved_in = [moves.start(source, target) for source, target in zip(saved_hbm, saved)]
    up_pairs, up_owners, down_owners, small = [], [], [], None
    own_pairs, own_owners, own_small = [], [], None
    if split:
        half_ref, up_ref, up_half, small_source = refs.take(4)
        half_in = moves.start(half_hbm, half_ref)
        up_in = moves.start(up_hbm, up_ref)
        down_owners = owner_sums(sequences, half_ref, down_sum, refs.take(4), BLOCKS)
        up_pairs = pair_sums(sequences, up_ref, up_half, refs.take(4), BLOCKS)
        up_owners = owner_sums(sequences, up_half, up_sum, refs.take(4), BLOCKS)
        small = SmallSum(sequences, small_source, smalls_sum, 6, refs.take(3), refs.take(6))
    if last:
        own_half = refs.one()
        own_pairs = pair_sums(sequences, grads_ref, own_half, refs.take(4), BLOCKS)
        own_owners = owner_sums(sequences, own_half, grads_sum, refs.take(4), BLOCKS)
        own_small = SmallSum(sequences, bias_ref, bias_sum, 0, refs.take(3), refs.take(6))
    wqkv_in = moves.start(wqkv_hbm.at[layer], wqkv_ref)
    du_in = moves.start(du_hbm, du_ref)
    gather = Gather(do_ref, g_send, g_recv)
    exchange = Exchange(*exchange_refs[:5], exchange_refs[5:])
    terms_ref = exchange.terms
    do_ref[mine] = low_ref[...]
    entry.wait()
    gather.start()
    if split:
        is_bias = lax.broadcasted_iota(jnp.int32, small_source.shape, 0) == 7
        small_source[...] = jnp.where(is_bias, bias_in[...], smalls_in[...])
        small.start()
        half_in.wait()
        for item in down_owners:
            item.start()
        up_in.wait()
        for item in up_pairs:
            item.start()
    dk_ref[...] = jnp.zeros_like(dk_ref)
    dv_ref[...] = jnp.zeros_like(dv_ref)
    lane_low = lax.broadcasted_iota(jnp.int32, (rows, LANES), 1) < HDIM

    def context_grad(chunk):
        spots = pl.ds(pl.multiple_of(chunk * rows, rows), rows)
        wide = head_pairs(dot_nt(do_ref[chunk], wout_ref[...]), heads)
        for head in range(heads):
            high = wide[head].astype(BF16).astype(F32)
            both = jnp.where(lane_low, high, wide[head] - high)
            dc_ref[head, spots] = both.astype(BF16)
            dct_ref[head, :, spots] = both.T.astype(BF16)

    def attend_back(chunk):
        keys = visible_keys(chunk, rows)
        limits = query_limits(chunk, rows, prefix_ref[0])
        visible = lax.broadcasted_iota(jnp.int32, (keys, rows), 0) <= limits
        spots = pl.ds(chunk * rows, rows)
        seen = pl.ds(0, keys)

        def one_head(head, carry):
            scores = dot(kz_ref[head, seen], qt_ref[head, :, spots])
            top = stats_ref[head, 0:1, spots]
            recip = stats_ref[head, 1:2, spots]
            probs = jnp.exp(jnp.where(visible, scores - top, -1e30)) * recip
            grad_probs = dot(v2_ref[head, seen], dct_ref[head, :, spots])
            inner = column_sum(probs * grad_probs)
            grad_scores = (probs * (grad_probs - inner)).astype(BF16)
            dv_ref[head, seen] = dv_ref[head, seen] + dot(probs.astype(BF16), dc_ref[head, spots])
            dk_ref[head, seen] = dk_ref[head, seen] + dot(grad_scores, q2_ref[head, spots])
            dq_ref[head, spots] = dot(kt_ref[head, :, seen], grad_scores).T * scale
            return carry

        lax.fori_loop(0, heads, one_head, 0)

    chip, core = mine // 2, mine - 2 * (mine // 2)

    def one_step(step, carry):
        near = 1 - step // 2
        flip = lax.rem(step, 2)
        to_chip = (1 - near) * (1 - chip) + near * chip
        chunk = 2 * to_chip + core + flip * (1 - 2 * core)

        @pl.when(step == 1)
        def _():
            gather.wait_partner()
            if split:
                small.first()

        @pl.when(step == 2)
        def _():
            for part in range(PIECES):
                gather.wait_across(part)
                gather.onward(part).start()
            if split:
                up_pairs[0].finish()
                up_owners[0].start()

        @pl.when(step == 3)
        def _():
            for part in range(PIECES):
                gather.wait_diagonal(part)
            if split:
                up_pairs[1].finish()
                up_owners[1].start()
                small.second()

        context_grad(chunk)
        for each in range(GROUP):
            @pl.when(chunk == each)
            def _():
                attend_back(each)
        return carry

    wout_in.wait()
    for move in saved_in:
        move.wait()
    lax.fori_loop(0, GROUP, one_step, 0)

    def pack_chunk(chunk, carry):
        spots = pl.ds(pl.multiple_of(chunk * rows, rows), rows)
        xt_ref[:, spots] = transposed(whole_ref[chunk]).astype(BF16)
        for kind, wide_ref in enumerate((dq_ref, dk_ref, dv_ref)):
            parts = []
            for head in range(heads):
                wide = wide_ref[head, spots]
                if kind == 2:
                    wide = wide + pltpu.roll(wide, HDIM, 1)
                parts.append(wide[:, :HDIM])
            values = jnp.concatenate(parts, axis=1)
            high_ref[kind, spots], lowbits_ref[kind, spots] = high_low(values)
            if kind != 1:
                place = slice((kind // 2) * depth, (kind // 2 + 1) * depth)
                bias_ref[:, place] = bias_ref[:, place] + column_sum(values)
        return carry

    bias_ref[...] = jnp.zeros_like(bias_ref)
    lax.fori_loop(0, GROUP, pack_chunk, 0)

    def weight_grads():
        out_wide = dot(ct_ref[0], do_ref[0])
        for chunk in range(1, GROUP):
            out_wide = out_wide + dot(ct_ref[chunk], do_ref[chunk])
        grads_ref[:, :depth] = out_wide.T
        for kind in range(3):
            place = slice((kind + 1) * depth, (kind + 2) * depth)
            grads_ref[:, place] = dot(xt_ref[...], high_ref[kind]) + dot(xt_ref[...], lowbits_ref[kind])

    def input_terms(chunk, part):
        spot = exchange.spot(part)
        spots = pl.ds(pl.multiple_of(chunk * rows + part * (rows // PIECES), rows // PIECES), rows // PIECES)
        total = None
        for kind in range(3):
            for values in (high_ref, lowbits_ref):
                term = dot_nt(values[kind, spots], wqkv_ref[kind])
                total = term if total is None else total + term
        terms_ref[chunk, spot] = total

    wqkv_in.wait()
    if last:
        weight_grads()
        own_small.first()
        for item in own_pairs:
            item.start()
    for part in range(PIECES):
        input_terms(diagonal, part)
        exchange.relay_copy(part).start()
        input_terms(across, part)
        if part > 0:
            exchange.pass_on(part - 1)
    input_terms(partner, 0)
    exchange.near_copy(0).start()
    exchange.pass_on(PIECES - 1)
    for part in range(1, PIECES):
        input_terms(partner, part)
        exchange.near_copy(part).start()
    if last:
        own_pairs[0].finish()
        own_owners[0].start()
    for part in range(PIECES):
        input_terms(mine, part)
    if not last:
        weight_grads()
        moves.store(grads_ref, grads_hbm)
    if split:
        small.third()
        for item in down_owners:
            item.finish()
    if last:
        own_pairs[1].finish()
        own_owners[1].start()
        own_small.second()
    for item in up_owners:
        item.finish()
    du_in.wait()
    for part in range(PIECES):
        spot = exchange.spot(part)
        dx_ref[spot] = exchange.result(part) + du_ref[spot]
    if last:
        own_small.third()
        for item in own_owners:
            item.finish()
        grads_hbm[...] = bias_ref[...]
    gather.wait_sends()
    exchange.wait_sends()
    for item in down_owners + up_pairs + up_owners + own_pairs + own_owners:
        item.wait_sends()
    for item in (small, own_small):
        if item is not None:
            item.wait_sends()
    moves.finish()


def attention_layer_back(layer, count, split, low, du, wout, wqkv, saved, prefix, extra):
    rows, width = low.shape
    last = split and layer == 0
    depth = wout.shape[1]
    heads = depth // HDIM
    tall = GROUP * rows
    columns = 4 * depth
    share = width // count
    outs = [shape((rows, width)), shape((8, width) if last else (width, columns)), shape((8, width))]
    out_specs = [VM, VM if last else ANY, VM]
    scratch = [pltpu.VMEM(each.shape, each.dtype) for each in saved]
    scratch += [
        pltpu.VMEM((rows, width), F32), pltpu.VMEM(wout.shape[1:], BF16), pltpu.VMEM(wqkv.shape[1:], BF16),
        pltpu.VMEM((width, columns), F32),
        pltpu.VMEM((GROUP, rows, width), BF16),
        pltpu.VMEM((heads, tall, LANES), BF16), pltpu.VMEM((heads, LANES, tall), BF16),
        pltpu.VMEM((heads, tall, LANES), F32), pltpu.VMEM((heads, tall, LANES), F32),
        pltpu.VMEM((heads, tall, LANES), F32),
        pltpu.VMEM((3, tall, depth), BF16), pltpu.VMEM((3, tall, depth), BF16),
        pltpu.VMEM((width, tall), BF16),
        dma_sems(14),
    ]
    scratch += exchange_scratch(rows, width, BF16) + [dma_sems(GATHER_SEMS), dma_sems(GATHER_SEMS)]
    if split:
        units = extra[0].shape[1]
        outs += [shape((share, units)), shape((share, units)), shape((8, width))]
        out_specs += [VM] * 3
        half = pltpu.VMEM((count // 2, share, units), F32)
        scratch += [half, pltpu.VMEM((width, units), F32), half, pltpu.VMEM((8, width), F32)]
        scratch += owner_scratch(count, width, units, BLOCKS)
        scratch += pair_scratch(count, width, units, BLOCKS) + owner_scratch(count, width, units, BLOCKS)
        scratch += small_sum_scratch(count, width)
    if last:
        outs += [shape((share, columns)), shape((8, width))]
        out_specs += [VM] * 2
        scratch += [pltpu.VMEM((count // 2, share, columns), F32)]
        scratch += pair_scratch(count, width, columns, BLOCKS) + owner_scratch(count, width, columns, BLOCKS)
        scratch += small_sum_scratch(count, width)
    return pl.pallas_call(
        functools.partial(attention_backward_kernel, layer, count, split, last),
        out_shape=outs,
        in_specs=[VM, ANY, ANY, ANY] + [ANY] * 8 + [SM] + ([ANY, ANY, VM, VM] if split else []),
        out_specs=out_specs,
        scratch_shapes=scratch,
        compiler_params=params(7 + layer),
        name="attention_bwd",
    )(low, du, wout, wqkv, *saved, prefix, *extra)


def results_kernel(depth, *refs):
    refs = Refs(refs)
    state_in, grad_in = refs.take(2)
    attn, up, down = refs.take(2), refs.take(2), refs.take(2)
    tail, smalls = refs.one(), refs.take(2)
    state, grad, wqkv, bias_qv, wout, bias_out, gain, shift, wup, bias_up, wdown, bias_down = refs.take(12)
    state[...] = state_in[...]
    grad[...] = grad_in[...]
    for layer in range(2):
        wout[layer] = attn[layer][:, :depth].T
        for kind in range(3):
            wqkv[layer, kind] = attn[layer][:, (kind + 1) * depth : (kind + 2) * depth]
        wup[layer] = up[layer][...]
        wdown[layer] = down[layer][...].T
        sums = smalls[layer]
        row = slice(layer, layer + 1)
        bias_down[row] = sums[0:1]
        gain[layer, 1:2] = sums[1:2]
        shift[layer, 1:2] = sums[2:3]
        gain[layer, 0:1] = sums[3:4]
        shift[layer, 0:1] = sums[4:5]
        bias_out[row] = sums[5:6]
        bias_up[row] = sums[6:7]
        biases = tail if layer == 0 else smalls[0]
        for kind in range(2):
            bias_qv[layer, kind : kind + 1] = biases[7:8, kind * depth : (kind + 1) * depth]


def results(state, grad, attn, up, down, tail, smalls, depth):
    rows, width = state.shape
    share, units = up[0].shape
    layers = len(attn)
    return pl.pallas_call(
        functools.partial(results_kernel, depth),
        out_shape=[
            shape((rows, width)), shape((rows, width)), shape((layers, 3, share, depth)),
            shape((layers, 2, depth)), shape((layers, depth, share)), shape((layers, width)),
            shape((layers, 2, width)), shape((layers, 2, width)), shape((layers, share, units)),
            shape((layers, units)), shape((layers, units, share)), shape((layers, width)),
        ],
        in_specs=[VM] * 11,
        out_specs=[VM] * 12,
        compiler_params=pltpu.CompilerParams(vmem_limit_bytes=VMEM_BYTES),
        name="results",
    )(state, grad, *attn, *up, *down, tail, *smalls)


def local(
    tokens,
    cotangent,
    prefix,
    w_qkv,
    bias_qv,
    w_out,
    bias_out,
    norm_gain,
    norm_bias,
    w_up,
    bias_up,
    w_down,
    bias_down,
):
    width = tokens.shape[1]
    layer_count = w_qkv.shape[0]
    depth = w_out.shape[1]
    state, low = tokens, tokens
    stored = []
    for layer in range(layer_count):
        state, low, normal1, recip1, *saved = attention_layer(
            layer, state, low, w_qkv, bias_qv, w_out, bias_out, norm_gain, norm_bias, prefix
        )
        state, low, normal2, recip2, normed, active, slope = ffn_layer(
            layer, state, low, w_up, bias_up, w_down, bias_down, norm_gain, norm_bias
        )
        stored.append(((normal2, recip2), (active, slope, normed, normal1, recip1), saved))
    count = lax.axis_size("dp")
    split = count > 2 and count % 2 == 0 and (width // count) % 16 == 0
    grad = cotangent
    bias = jnp.zeros((8, width), F32)
    earlier = None
    attn, up, down, smalls, biases = [], [], [], [], []
    for layer in reversed(range(layer_count)):
        second, middle, saved = stored[layer]
        du, low, up_grad, down_grad, small, *sums = ffn_layer_back(
            layer, count, split, grad, *second, norm_gain, w_down, w_up, *middle, earlier
        )
        attn = (sums + attn) if split else attn
        extra = (up_grad, down_grad, small, bias) if split else ()
        grad, earlier, bias, *sums = attention_layer_back(
            layer, count, split, low, du, w_out, w_qkv, saved, prefix, extra
        )
        if split:
            up.insert(0, sums[0])
            down.insert(0, sums[1])
            smalls.insert(0, sums[2])
            if layer == 0:
                attn.insert(0, sums[3])
                return results(state, grad, attn, up, down, sums[4], smalls, depth)
            continue
        attn.insert(0, earlier)
        up.insert(0, up_grad)
        down.insert(0, down_grad)
        smalls.insert(0, small)
        biases.insert(0, bias[7, : 2 * depth].reshape(2, depth))
    scatter = functools.partial(lax.psum_scatter, axis_name="dp", scatter_dimension=1, tiled=True)
    attn_sum, up_sum, down_sum = [scatter(jnp.stack(each)) for each in (attn, up, down)]
    shared = lax.psum(jnp.stack(smalls)[:, :6], ("dp", "tensor"))
    bias_qv_sum, bias_up_sum = lax.psum((jnp.stack(biases), jnp.stack(smalls)[:, 6]), "dp")
    share = attn_sum.shape[1]
    return (
        state,
        grad,
        jnp.moveaxis(attn_sum[:, :, depth:].reshape(layer_count, share, 3, depth), 2, 1),
        bias_qv_sum,
        jnp.swapaxes(attn_sum[:, :, :depth], 1, 2),
        shared[:, 5],
        jnp.stack([shared[:, 3], shared[:, 1]], axis=1),
        jnp.stack([shared[:, 4], shared[:, 2]], axis=1),
        up_sum,
        bias_up_sum,
        jnp.swapaxes(down_sum, 1, 2),
        shared[:, 0],
    )


def solution(mesh):
    in_specs = (
        P(("dp", "tensor"), None),
        P(("dp", "tensor"), None),
        P("dp"),
        P(None, None, None, "tensor"),
        P(None, None, "tensor"),
        P(None, "tensor", None),
        P(),
        P(),
        P(),
        P(None, None, "tensor"),
        P(None, "tensor"),
        P(None, "tensor", None),
        P(),
    )
    out_specs = (
        P(("dp", "tensor"), None),
        P(("dp", "tensor"), None),
        P(None, None, "dp", "tensor"),
        P(None, None, "tensor"),
        P(None, "tensor", "dp"),
        P(),
        P(),
        P(),
        P(None, "dp", "tensor"),
        P(None, "tensor"),
        P(None, "tensor", "dp"),
        P(),
    )
    return jax.shard_map(local, mesh=mesh, in_specs=in_specs, out_specs=out_specs, check_vma=False)
```

time: 382 us -> 324 us (0.85)
  the two profiles are of different devices: /device:TPU:4 before, /device:TPU:0 now
where the time goes in v3:
time: 324 us; the launch traced here: 320 us
  Pallas kernels  311 us (96%)
  local copies, waits for them, and re-layouts  6.85 us (2%)
    pallas_call x2, Pallas kernels, attention_layer_back(): pl.pallas_call(functools.partial(attention_backward_kernel, layer, count,...  100 us
    pallas_call x2, Pallas kernels, ffn_layer_back(): pl.pallas_call(functools.partial(ffn_backward_kernel, layer, count, split...  76.7 us
    pallas_call x2, Pallas kernels, ffn_layer(): pl.pallas_call(functools.partial(ffn_forward_kernel, layer), out_shape=[s...  70 us
    pallas_call x2, Pallas kernels, attention_layer(): pl.pallas_call(functools.partial(attention_forward_kernel, layer), out_sh...  60.2 us

profile of v3, /device:TPU:0, one launch (start us, length us, event | category | flops | bytes accessed | tf_op | source)
XLA Modules:
  0.0 319.7 jit_solution(10154486657960815710)
XLA Ops:
  0.6 4.0 %copy.25.refs_2_.refs_3_ = bf16[2,3,768,192]{3,2,1,0:T(8,128)(2,1)} copy(bf16[2,3,768,192]{2,3,1,0:T(8,128)(2,1)} %param.16) | data formatting | bytes 3538944 | tf_op args[3]
  5.3 31.1 %attention_fwd.2 = (f32[256,768]{1,0:T(8,128)}, bf16[256,768]{1,0:T(8,128)(2,1)}, f32[256,768]{1,0:T(8,128)}, f32[256,128]{1,0:T(8,128)}, bf16[4,256,768]{2,1,0:...) custom-call(bf16[256,768]{1,0:T(8,128)(2,1)} %refs_1_.1, ...), custom_call_target="tpu_custom_call" | custom-call | tf_op jit(solution)/shard_map/attention_fwd/pallas_call | solution.py:451
  36.5 34.8 %ffn_fwd.2 = (f32[256,768]{1,0:T(8,128)}, bf16[256,768]{1,0:T(8,128)(2,1)}, f32[256,768]{1,0:T(8,128)}, f32[256,128]{1,0:T(8,128)}, bf16[4,256,768]{2,1,0:T(8,12...) custom-call(f32[256,768]{1,0:T(8,128)} %get-tuple-element.72.refs_0_, ...), custom_call_target="tpu_custom_call" | custom-call | tf_op jit(solution)/shard_map/ffn_fwd/pallas_call | solution.py:548
  71.3 29.1 %attention_fwd.3 = (f32[256,768]{1,0:T(8,128)}, bf16[256,768]{1,0:T(8,128)(2,1)}, f32[256,768]{1,0:T(8,128)}, f32[256,128]{1,0:T(8,128)}, bf16[4,256,768]{2,1,0:...) custom-call(f32[256,768]{1,0:T(8,128)} %get-tuple-element.74.refs_0_, ...), custom_call_target="tpu_custom_call" | custom-call | tf_op jit(solution)/shard_map/attention_fwd/pallas_call | solution.py:451
  100.4 35.2 %ffn_fwd.3 = (f32[256,768]{1,0:T(8,128)}, bf16[256,768]{1,0:T(8,128)(2,1)}, f32[256,768]{1,0:T(8,128)}, f32[256,128]{1,0:T(8,128)}, bf16[4,256,768]{2,1,0:T(8,12...) custom-call(f32[256,768]{1,0:T(8,128)} %get-tuple-element.76.refs_0_, ...), custom_call_target="tpu_custom_call" | custom-call | tf_op jit(solution)/shard_map/ffn_fwd/pallas_call | solution.py:548
  135.6 39.2 %ffn_bwd.2 = (f32[256,768]{1,0:T(8,128)}, bf16[256,768]{1,0:T(8,128)(2,1)}, f32[768,768]{1,0:T(8,128)}, f32[4,96,768]{2,1,0:T(8,128)}, f32[8,768]{1,0:T(8,128)}) custom-call(bf16[256,768]{1,0:T(8,128)(2,1)} %refs_0_.3, f32[256,768]{1,0:T(8,128)} %get-tuple-element.79.refs_1_, f32[256,128]{1,0:T(8,128)} %get-tuple-element.80.refs_2_, f32[2,2,768]{2,1,0:T(2,128)} %refs_3_.13, ...), custom_call_target="tpu_custom_call" | custom-call | tf_op jit(solution)/shard_map/ffn_bwd/pallas_call | solution.py:913
  174.8 0.6 broadcast_in_dim.3.refs_16_
  175.4 42.3 %attention_bwd.2 = (f32[256,768]{1,0:T(8,128)}, f32[768,768]{1,0:T(8,128)}, f32[8,768]{1,0:T(8,128)}, f32[96,768]{1,0:T(8,128)}, f32[96,768]{1,0:T(8,128)}, /*index=5*/f32[8,768]{1,0:T(8,128)}) custom-call(bf16[256,768]{1,0:T(8,128)(2,1)} %get-tuple-element.86.refs_0_, f32[256,768]{1,0:T(8,128)} %get-tuple-element.87.refs_1_, bf16[2,192,768]{2,1,0:T(8,128)(2,1)} %refs_2_.9, ...), custom_call_target="tpu_custom_call" | custom-call | tf_op jit(solution)/shard_map/attention_bwd/pallas_call | solution.py:1193
  217.7 37.5 %ffn_bwd.3 = (f32[256,768]{1,0:T(8,128)}, bf16[256,768]{1,0:T(8,128)(2,1)}, f32[768,768]{1,0:T(8,128)}, f32[4,96,768]{2,1,0:T(8,128)}, f32[8,768]{1,0:T(8,128)}, /*index=5*/f32[96,768]{1,0:T(8,128)}) custom-call(f32[256,768]{1,0:T(8,128)} %get-tuple-element.99.refs_0_, f32[256,768]{1,0:T(8,128)} %get-tuple-element.100.refs_1_, ...), custom_call_target="tpu_custom_call" | custom-call | tf_op jit(solution)/shard_map/ffn_bwd/pallas_call | solution.py:913
  255.3 57.8 %attention_bwd.3 = (f32[256,768]{1,0:T(8,128)}, f32[8,768]{1,0:T(8,128)}, f32[8,768]{1,0:T(8,128)}, f32[96,768]{1,0:T(8,128)}, f32[96,768]{1,0:T(8,128)}, /*inde...) custom-call(bf16[256,768]{1,0:T(8,128)(2,1)} %get-tuple-element.108.refs_0_, ...), custom_call_target="tpu_custom_call" | custom-call | tf_op jit(solution)/shard_map/attention_bwd/pallas_call | solution.py:1193
  313.1 4.2 %results.1 = (f32[256,768]{1,0:T(8,128)}, f32[256,768]{1,0:T(8,128)}, f32[2,3,96,192]{3,2,1,0:T(8,128)}, f32[2,2,192]{2,1,0:T(2,128)}, f32[2,192,96]{2,1,0:T(8,1...) custom-call(f32[256,768]{1,0:T(8,128)} %get-tuple-element.78.refs_0_, ...), custom_call_target="tpu_custom_call" | custom-call | tf_op jit(solution)/shard_map/results/pallas_call | solution.py:1236
  317.3 2.2 copy.29

commit v4 on v3

--- a/solution.py
+++ b/solution.py
@@ -13,9 +13,8 @@
 MEM = 10
 LANES = 128
 GROUP = 4
-PIECES = 2
 EPSILON = 1e-06
-VMEM_BYTES = 56 * 1024 * 1024
+VMEM_BYTES = 62 * 1024 * 1024
 HIGHEST = lax.Precision.HIGHEST
 MESH = pl.DeviceIdType.MESH
 F32 = jnp.float32
@@ -129,10 +128,11 @@
 
 
 class Gather:
-    def __init__(self, whole, send_sems, recv_sems):
+    def __init__(self, whole, send_sems, recv_sems, pieces):
         self.whole = whole
+        self.pieces = pieces
         self.mine, self.partner, self.across, self.diagonal = places()
-        self.rows = whole.shape[1] // PIECES
+        self.rows = whole.shape[1] // pieces
         self.send_sems, self.recv_sems = send_sems, recv_sems
 
     def piece(self, chunk, part):
@@ -153,11 +153,11 @@
     def onward(self, part):
         return remote(
             self.piece(self.across, part), self.piece(self.across, part),
-            self.send_sems.at[1 + PIECES + part], self.recv_sems.at[1 + PIECES + part], self.partner,
+            self.send_sems.at[1 + self.pieces + part], self.recv_sems.at[1 + self.pieces + part], self.partner,
         )
 
     def start(self):
-        for part in range(PIECES):
+        for part in range(self.pieces):
             self.to_across(part).start()
         self.to_partner().start()
 
@@ -176,17 +176,23 @@
     def wait_diagonal(self, part):
         remote(
             self.piece(self.diagonal, part), self.piece(self.diagonal, part),
-            self.send_sems.at[1 + PIECES + part], self.recv_sems.at[1 + PIECES + part], self.partner,
+            self.send_sems.at[1 + self.pieces + part], self.recv_sems.at[1 + self.pieces + part], self.partner,
         ).wait_recv()
 
     def wait_sends(self):
         self.to_partner().wait_send()
-        for part in range(PIECES):
+        for part in range(self.pieces):
             self.to_across(part).wait_send()
             self.onward(part).wait_send()
 
 
-GATHER_SEMS = 1 + 2 * PIECES
+ATTN_PIECES = 2
+FFN_PIECES = 4
+BACK_PIECES = 2
+
+
+def gather_sems(pieces):
+    return [dma_sems(1 + 2 * pieces), dma_sems(1 + 2 * pieces)]
 
 
 def shape(dims, kind=F32):
@@ -238,11 +244,12 @@
 
 
 class Exchange:
-    def __init__(self, terms, near, relay, total, far, sems):
+    def __init__(self, terms, near, relay, total, far, sems, pieces):
         self.terms, self.near, self.relay, self.total, self.far = terms, near, relay, total, far
         self.n_send, self.n_recv, self.r_send, self.r_recv, self.f_send, self.f_recv = sems
         self.mine, self.partner, self.across, self.diagonal = places()
-        self.rows = terms.shape[1] // PIECES
+        self.pieces = pieces
+        self.rows = terms.shape[1] // pieces
 
     def spot(self, part):
         return pl.ds(part * self.rows, self.rows)
@@ -278,18 +285,18 @@
         return (self.terms[self.mine, spot] + self.near[spot]) + self.far[spot].astype(F32)
 
     def wait_sends(self):
-        for part in range(PIECES):
+        for part in range(self.pieces):
             self.near_copy(part).wait_send()
             self.relay_copy(part).wait_send()
             self.far_copy(part).wait_send()
 
 
-def exchange_scratch(rows, width, kind):
+def exchange_scratch(rows, width, kind, pieces):
     return [
         pltpu.VMEM((GROUP, rows, width), F32),
         pltpu.VMEM((rows, width), F32), pltpu.VMEM((rows, width), F32),
         pltpu.VMEM((rows, width), kind), pltpu.VMEM((rows, width), kind),
-    ] + [dma_sems(PIECES)] * 6
+    ] + [dma_sems(pieces)] * 6
 
 
 def attention_forward_kernel(layer, *refs):
@@ -310,7 +317,7 @@
     wqkv_in = moves.start(wqkv_hbm.at[layer], wqkv_ref)
     wout_in = moves.start(wout_hbm.at[layer], wo_ref.at[mine])
     state_in = moves.start(state_hbm, state_ref)
-    gather = Gather(whole_ref, g_send, g_recv)
+    gather = Gather(whole_ref, g_send, g_recv, ATTN_PIECES)
     whole_ref[mine] = low_ref[...]
     entry.wait()
     gather.start()
@@ -348,13 +355,13 @@
     gather.wait_partner()
     project(partner)
     wout_in.wait()
-    for part in range(PIECES):
+    for part in range(ATTN_PIECES):
         gather.wait_across(part)
         gather.onward(part).start()
     wout_to_across.start()
     wout_to_partner(mine).start()
     project(across)
-    for part in range(PIECES):
+    for part in range(ATTN_PIECES):
         gather.wait_diagonal(part)
     project(diagonal)
     for source, target in zip(saved[:6], saved_hbm[:6]):
@@ -462,7 +469,7 @@
             pltpu.VMEM((GROUP, depth, rows), BF16),
             pltpu.VMEM((GROUP, depth, width), BF16),
             dma_sems(11),
-            dma_sems(GATHER_SEMS), dma_sems(GATHER_SEMS),
+            *gather_sems(ATTN_PIECES),
             dma_sems(3), dma_sems(3), dma_sems(3), dma_sems(3),
         ],
         compiler_params=params(1 + layer),
@@ -482,16 +489,16 @@
     g_send, g_recv = refs.take(2)
     mine, partner, across, diagonal = places()
     rows = low_ref.shape[0]
-    part_rows = rows // PIECES
+    part_rows = rows // FFN_PIECES
     entry = Entry()
     wup_in = moves.start(wup_hbm.at[layer], wup_ref)
     wdown_in = moves.start(wdown_hbm.at[layer], wdown_ref)
     state_in = moves.start(state_hbm, state_ref)
-    gather = Gather(whole_ref, g_send, g_recv)
+    gather = Gather(whole_ref, g_send, g_recv, FFN_PIECES)
     whole_ref[mine] = low_ref[...]
     entry.wait()
     gather.start()
-    exchange = Exchange(*exchange_refs[:5], exchange_refs[5:])
+    exchange = Exchange(*exchange_refs[:5], exchange_refs[5:], FFN_PIECES)
     terms_ref = exchange.terms
 
     def units(chunk, part):
@@ -506,9 +513,9 @@
 
     wup_in.wait()
     wdown_in.wait()
-    for part in range(PIECES):
+    for part in range(FFN_PIECES):
         units(mine, part)
-    for part in range(PIECES):
+    for part in range(FFN_PIECES):
         gather.wait_across(part)
         gather.onward(part).start()
         units(across, part)
@@ -521,14 +528,14 @@
     moves.store(whole_ref, saved_hbm[0])
     units(partner, 0)
     exchange.near_copy(0).start()
-    exchange.pass_on(PIECES - 1)
-    for part in range(1, PIECES):
+    exchange.pass_on(FFN_PIECES - 1)
+    for part in range(1, FFN_PIECES):
         units(partner, part)
         exchange.near_copy(part).start()
     moves.store(active_ref, saved_hbm[1])
     moves.store(slope_ref, saved_hbm[2])
     state_in.wait()
-    for part in range(PIECES):
+    for part in range(FFN_PIECES):
         spot = exchange.spot(part)
         total = state_ref[spot] + exchange.result(part) + bias_down_ref[layer : layer + 1]
         result, normal, recip = layer_norm(total, gain_ref[layer, 1:2], shift_ref[layer, 1:2])
@@ -557,8 +564,8 @@
             pltpu.VMEM((rows, width), F32), pltpu.VMEM(wup.shape[1:], BF16), pltpu.VMEM(wdown.shape[1:], BF16),
             dma_sems(6),
         ]
-        + exchange_scratch(rows, width, F32)
-        + [dma_sems(GATHER_SEMS), dma_sems(GATHER_SEMS)],
+        + exchange_scratch(rows, width, F32, FFN_PIECES)
+        + gather_sems(FFN_PIECES),
         compiler_params=params(3 + layer),
         name="ffn_fwd",
     )(state, low, wup, bias_up, wdown, bias_down, gain, shift)
@@ -587,16 +594,16 @@
     return lax.dot_general(left, right, (((0,), (0,)), ((), ())), preferred_element_type=F32)
 
 
+def owner_rows(pair, side, rows):
+    return pl.ds(pl.multiple_of((2 * pair + side) * rows, 16), rows)
+
+
 class PairSum:
-    def __init__(self, sequences, source, half, columns, buffers, sems):
-        self.at, self.source, self.half, self.columns = sequences, source, half, columns
+    def __init__(self, sequences, source, columns, buffers, sems):
+        self.at, self.source, self.columns = sequences, source, columns
         self.out, self.into = buffers
         self.sems = sems
-        self.rows = half.shape[1]
-
-    def terms(self, pair, side):
-        start = pl.multiple_of((2 * pair + side) * self.rows, 16)
-        return self.source[pl.ds(start, self.rows), self.columns]
+        self.rows = self.out.shape[1]
 
     def copy(self):
         return remote_dp(
@@ -605,24 +612,29 @@
 
     def start(self):
         for pair in range(self.at.pairs):
-            self.out[pair, :, self.columns] = self.terms(pair, 1 - self.at.side).astype(BF16)
+            place = (owner_rows(pair, 1 - self.at.side, self.rows), self.columns)
+            self.out[pair, :, self.columns] = self.source[place].astype(BF16)
         self.copy().start()
 
     def finish(self):
         self.copy().wait_recv()
         for pair in range(self.at.pairs):
-            own = self.terms(pair, self.at.side)
-            self.half[pair, :, self.columns] = own + self.into[pair, :, self.columns].astype(F32)
+            place = (owner_rows(pair, self.at.side, self.rows), self.columns)
+            self.source[place] = self.source[place] + self.into[pair, :, self.columns].astype(F32)
 
     def wait_sends(self):
         self.copy().wait_send()
 
 
 class OwnerSum:
-    def __init__(self, sequences, half, result, columns, buffers, sems):
-        self.at, self.half, self.result, self.columns = sequences, half, result, columns
+    def __init__(self, sequences, source, result, columns, buffers, sems):
+        self.at, self.source, self.result, self.columns = sequences, source, result, columns
         self.out, self.into = buffers
         self.sems = sems
+        self.rows = result.shape[0]
+
+    def terms(self, pair):
+        return self.source[owner_rows(pair, self.at.side, self.rows), self.columns]
 
     def copy(self, offset):
         return remote_dp(
@@ -633,11 +645,11 @@
     def start(self):
         for offset in range(1, self.at.pairs):
             pair = self.at.other_pair(offset)
-            self.out[offset - 1, :, self.columns] = self.half[pair, :, self.columns].astype(BF16)
+            self.out[offset - 1, :, self.columns] = self.terms(pair).astype(BF16)
             self.copy(offset).start()
 
     def finish(self):
-        total = self.half[self.at.pair, :, self.columns]
+        total = self.terms(self.at.pair)
         for offset in range(1, self.at.pairs):
             self.copy(offset).wait_recv()
             total = total + self.into[offset - 1, :, self.columns].astype(F32)
@@ -648,22 +660,19 @@
             self.copy(offset).wait_send()
 
 
-def column_blocks(columns, blocks):
-    step = columns // blocks
-    return [slice(block * step, (block + 1) * step) for block in range(blocks)]
+def halves(columns):
+    return (slice(0, columns // 2), slice(columns // 2, columns))
+
+
+def tile_blocks(columns):
+    tiles = columns // LANES
+    ends = [0, 1, 1 + (tiles - 1) * 2 // 5, 1 + (tiles - 1) * 4 // 5, tiles]
+    return [slice(first * LANES, end * LANES) for first, end in zip(ends, ends[1:])]
 
 
 def pair_scratch(count, width, columns, blocks):
     dims = (count // 2, width // count, columns)
     return [pltpu.VMEM(dims, BF16), pltpu.VMEM(dims, BF16), dma_sems(blocks), dma_sems(blocks)]
-
-
-def pair_sums(sequences, source, half, scratch, blocks):
-    out, into, send, recv = scratch
-    return [
-        PairSum(sequences, source, half, columns, (out, into), (send.at[block], recv.at[block]))
-        for block, columns in enumerate(column_blocks(source.shape[1], blocks))
-    ]
 
 
 def owner_scratch(count, width, columns, blocks):
@@ -674,12 +683,37 @@
     ]
 
 
-def owner_sums(sequences, half, result, scratch, blocks):
-    out, into, send, recv = scratch
-    return [
-        OwnerSum(sequences, half, result, columns, (out, into), (send.at[block], recv.at[block]))
-        for block, columns in enumerate(column_blocks(result.shape[1], blocks))
-    ]
+def total_scratch(count, width, columns, blocks):
+    return pair_scratch(count, width, columns, blocks) + owner_scratch(count, width, columns, blocks)
+
+
+def total_sums(sequences, source, result, scratch, blocks):
+    first_out, first_in, n_send, n_recv, second_out, second_in, p_send, p_recv = scratch
+    sums = []
+    for block, columns in enumerate(blocks):
+        pair = PairSum(sequences, source, columns, (first_out, first_in), (n_send.at[block], n_recv.at[block]))
+        owner = OwnerSum(
+            sequences, source, result, columns, (second_out, second_in), (p_send.at[block], p_recv.at[block])
+        )
+        sums.append(BlockSum(pair, owner))
+    return sums
+
+
+TOTAL_REFS = 8
+
+
+class BlockSum:
+    def __init__(self, pair, owner):
+        self.pair, self.owner = pair, owner
+        self.start, self.finish = pair.start, owner.finish
+
+    def turn(self):
+        self.pair.finish()
+        self.owner.start()
+
+    def wait_sends(self):
+        self.pair.wait_sends()
+        self.owner.wait_sends()
 
 
 class SmallSum:
@@ -758,230 +792,161 @@
     ]
 
 
-BLOCKS = 2
-
-
-def ffn_backward_kernel(layer, count, split, behind, *refs):
+def layer_backward_kernel(layer, count, split, behind, last, *refs):
     refs = Refs(refs)
-    grad_ref, normal2_ref, recip2_ref, gain_ref, wdown_hbm, wup_hbm = refs.take(6)
-    active_hbm, slope_hbm, normed_hbm, normal1_hbm, recip1_ref = refs.take(5)
-    earlier_hbm = refs.one() if behind else None
-    du_ref, low_ref, up_hbm, down_out, smalls_ref = refs.take(5)
+    grad_ref, normal2_ref, recip2_ref, gain_ref, recip1_ref = refs.take(5)
+    wdown_hbm, wup_hbm, active_hbm, slope_hbm, normed_hbm, normal1_hbm, wout_hbm, wqkv_hbm = refs.take(8)
+    whole_hbm, *saved_hbm = refs.take(8)
+    prefix_ref = refs.one()
+    earlier_hbm, bias_in = refs.take(2) if behind else (None,) * 2
+    dx_ref, bias_ref = refs.take(2)
+    grads_hbm = None if last else refs.one()
+    up_out, down_out, smalls_out = refs.take(3)
     earlier_sum = refs.one() if behind else None
-    df_ref, du2_ref, high_ref, lowbits_ref = refs.take(4)
-    wdown_ref, wup_ref, active_ref, slope_ref, normed_ref, normal1_ref, up_ref, down_ref = refs.take(8)
+    grads_sum, bias_sum = refs.take(2) if last else (None,) * 2
+    df_ref, do_ref, du_ref, high_ref, lowbits_ref = refs.take(5)
+    wdown_ref, wup_ref, active_ref, wide_ref, normed_ref, normal1_ref = refs.take(6)
+    up_ref, down_ref, grads_ref, smalls_ref = refs.take(4)
+    saved = refs.take(7)
+    qt_ref, q2_ref, kz_ref, kt_ref, v2_ref, ct_ref, stats_ref = saved
+    wout_ref, wqkv_ref, wqkv_t_ref = refs.take(3)
+    dc_ref, dct_ref, dv_ref, xt_ref = refs.take(4)
     moves = Moves(refs.one())
     exchange_refs = refs.take(11)
-    g_send, g_recv = refs.take(2)
+    first_sems, second_sems = refs.take(2), refs.take(2)
     mine, partner, across, diagonal = places()
     rows, width = grad_ref.shape
     units = wup_ref.shape[1]
     tall = GROUP * rows
+    part_rows = rows // BACK_PIECES
+    heads = qt_ref.shape[0]
+    depth = heads * HDIM
+    span = width // 3
+    scale = 1.0 / math.sqrt(HDIM)
     sequences = Sequences(count) if split else None
     entry = Entry(sequences)
     wdown_in = moves.start(wdown_hbm.at[layer], wdown_ref)
-    slope_in = moves.start(slope_hbm, slope_ref)
     wup_in = moves.start(wup_hbm.at[layer], wup_ref)
-    earlier_pairs, earlier_owners, down_pairs = [], [], []
+    slope_in = [
+        moves.start(slope_hbm.at[chunk], wide_ref.at[pl.ds(chunk * rows, rows)]) for chunk in range(GROUP)
+    ]
+    earlier, ups, downs, own, small, own_small = [], [], [], [], None, None
     if behind:
-        earlier_ref, half_ref = refs.take(2)
-        earlier_in = moves.start(earlier_hbm, earlier_ref)
-        earlier_pairs = pair_sums(sequences, earlier_ref, half_ref, refs.take(4), BLOCKS)
-        earlier_owners = owner_sums(sequences, half_ref, earlier_sum, refs.take(4), BLOCKS)
+        earlier_in = moves.start(earlier_hbm, grads_ref)
+        earlier = total_sums(sequences, grads_ref, earlier_sum, refs.take(TOTAL_REFS), halves(width))
     if split:
-        down_pairs = pair_sums(sequences, down_ref, down_out, refs.take(4), BLOCKS)
+        downs = total_sums(sequences, down_ref, down_out, refs.take(TOTAL_REFS), halves(units))
+        ups = total_sums(sequences, up_ref, up_out, refs.take(TOTAL_REFS), halves(units))
+        small = SmallSum(sequences, smalls_ref, smalls_out, 6, refs.take(3), refs.take(6))
+    if last:
+        own = total_sums(sequences, grads_ref, grads_sum, refs.take(TOTAL_REFS), tile_blocks(width))
+        own_small = SmallSum(sequences, bias_ref, bias_sum, 0, refs.take(3), refs.take(6))
     active_in = moves.start(active_hbm, active_ref)
     normed_in = moves.start(normed_hbm, normed_ref)
     normal1_in = moves.start(normal1_hbm, normal1_ref)
-    gather = Gather(df_ref, g_send, g_recv)
-    exchange = Exchange(*exchange_refs[:5], exchange_refs[5:])
+    wout_in = moves.start(wout_hbm.at[layer], wout_ref)
+    wqkv_in = moves.start(wqkv_hbm.at[layer], wqkv_ref)
+    saved_in = [moves.start(source, target) for source, target in zip(saved_hbm, saved)]
+    first_gather = Gather(df_ref, *first_sems, BACK_PIECES)
+    second_gather = Gather(do_ref, *second_sems, BACK_PIECES)
+    exchange = Exchange(*exchange_refs[:5], exchange_refs[5:], BACK_PIECES)
     terms_ref = exchange.terms
+
     grad = grad_ref[...].astype(F32)
     normal2 = normal2_ref[...]
     du2 = layer_norm_back(grad, normal2, recip2_ref[:, :1], gain_ref[layer, 1:2])
-    du2_ref[...] = du2
+    du_ref[...] = du2
     df_ref[mine] = du2.astype(BF16)
     entry.wait()
-    gather.start()
+    first_gather.start()
     smalls_ref[0:1] = column_sum(du2)
     smalls_ref[1:2] = column_sum(grad * normal2)
     smalls_ref[2:3] = column_sum(grad)
-    smalls_ref[6:8] = jnp.zeros((2, width), F32)
+    smalls_ref[6:7] = jnp.zeros((1, width), F32)
+    smalls_ref[7:8] = bias_in[7:8] if behind else jnp.zeros((1, width), F32)
+    wdown_in.wait()
+    wdown_ref[...] = transposed(wdown_ref[...]).astype(BF16)
+    wup_in.wait()
+    wup_ref[...] = transposed(wup_ref[...]).astype(BF16)
     if behind:
         earlier_in.wait()
-        for item in earlier_pairs:
+        for item in earlier:
             item.start()
 
+    def part_spots(chunk, part):
+        return pl.ds(pl.multiple_of(chunk * rows + part * part_rows, part_rows), part_rows)
+
     def back(chunk, part):
-        spot = exchange.spot(part)
-        grad_active = dot_nt(df_ref[chunk, spot], wdown_ref[...])
-        grad_hidden = grad_active * slope_ref[chunk, spot]
+        spot, spots = exchange.spot(part), part_spots(chunk, part)
+        grad_active = dot(df_ref[chunk, spot], wdown_ref[...])
+        grad_hidden = grad_active * wide_ref[spots]
         smalls_ref[6:7] = smalls_ref[6:7] + column_sum(grad_hidden)
         high, low = high_low(grad_hidden)
-        high_ref[chunk, spot] = high
-        lowbits_ref[chunk, spot] = low
-        terms_ref[chunk, spot] = dot_nt(high, wup_ref[...]) + dot_nt(low, wup_ref[...])
-
-    wdown_in.wait()
-    slope_in.wait()
-    wup_in.wait()
-    for part in range(PIECES):
+        high_ref[spots] = high
+        lowbits_ref[spots] = low
+        terms_ref[chunk, spot] = dot(high, wup_ref[...]) + dot(low, wup_ref[...])
+
+    for move in slope_in:
+        move.wait()
+    for part in range(BACK_PIECES):
         back(mine, part)
-    for part in range(PIECES):
-        gather.wait_across(part)
-        gather.onward(part).start()
+    for part in range(BACK_PIECES):
+        first_gather.wait_across(part)
+        first_gather.onward(part).start()
         back(across, part)
-        gather.wait_diagonal(part)
+        first_gather.wait_diagonal(part)
         back(diagonal, part)
         exchange.relay_copy(part).start()
         if part > 0:
             exchange.pass_on(part - 1)
-    gather.wait_partner()
+        if behind and part == 0:
+            earlier[0].turn()
+    first_gather.wait_partner()
     back(partner, 0)
     exchange.near_copy(0).start()
-    exchange.pass_on(PIECES - 1)
-    for pair, owner in zip(earlier_pairs, earlier_owners):
-        pair.finish()
-        owner.start()
+    exchange.pass_on(BACK_PIECES - 1)
     active_in.wait()
     down_ref[...] = dot_tn(df_ref[...].reshape(tall, width), active_ref[...].reshape(tall, units))
-    if split:
-        for item in down_pairs:
-            item.start()
-    else:
-        moves.store(down_ref, down_out)
-    for part in range(1, PIECES):
+    for item in downs:
+        item.start()
+    for part in range(1, BACK_PIECES):
         back(partner, part)
         exchange.near_copy(part).start()
+    if behind:
+        earlier[1].turn()
     normed_in.wait()
     normed = normed_ref[...].reshape(tall, width)
-    up_ref[...] = dot_tn(normed, high_ref[...].reshape(tall, units)) + dot_tn(
-        normed, lowbits_ref[...].reshape(tall, units)
-    )
-    moves.store(up_ref, up_hbm)
+    up_ref[...] = dot_tn(normed, high_ref[...]) + dot_tn(normed, lowbits_ref[...])
+    for item in ups:
+        item.start()
+    whole_in = moves.start(whole_hbm, normed_ref)
+    if not split:
+        moves.store(down_ref, down_out)
+        moves.store(up_ref, up_out)
     normal1_in.wait()
-    for part in range(PIECES):
+    for part in range(BACK_PIECES):
         spot = exchange.spot(part)
-        grad_normed = exchange.result(part) + du2_ref[spot]
+        grad_normed = exchange.result(part) + du_ref[spot]
         normal1 = normal1_ref[spot]
         du = layer_norm_back(grad_normed, normal1, recip1_ref[spot, :1], gain_ref[layer, 0:1])
         du_ref[spot] = du
-        low_ref[spot] = du.astype(BF16)
+        do_ref[mine, spot] = du.astype(BF16)
+        second_gather.to_across(part).start()
         sums = (column_sum(grad_normed * normal1), column_sum(grad_normed), column_sum(du))
         for index, value in enumerate(sums):
             place = slice(3 + index, 4 + index)
             smalls_ref[place] = value if part == 0 else smalls_ref[place] + value
-    for item in earlier_owners + down_pairs:
-        item.finish()
-    gather.wait_sends()
+    second_gather.to_partner().start()
+    if split:
+        small.start()
+    else:
+        smalls_out[...] = smalls_ref[...]
     exchange.wait_sends()
-    for item in earlier_pairs + earlier_owners + down_pairs:
-        item.wait_sends()
-    moves.finish()
-
-
-def ffn_layer_back(layer, count, split, grad, normal2, recip2, gain, wdown, wup, active, slope, normed, normal1, recip1, earlier):
-    rows, width = grad.shape
-    units = wup.shape[2]
-    behind = split and earlier is not None
-    share = width // count
-    down = (count // 2, share, units) if split else (width, units)
-    outs = [
-        shape((rows, width)), shape((rows, width), BF16), shape((width, units)), shape(down), shape((8, width)),
-    ]
-    out_specs = [VM, VM, ANY, VM if split else ANY, VM]
-    scratch = [
-        pltpu.VMEM((GROUP, rows, width), BF16),
-        pltpu.VMEM((rows, width), F32),
-        pltpu.VMEM((GROUP, rows, units), BF16), pltpu.VMEM((GROUP, rows, units), BF16),
-        pltpu.VMEM(wdown.shape[1:], BF16), pltpu.VMEM(wup.shape[1:], BF16),
-        pltpu.VMEM(active.shape, BF16), pltpu.VMEM(slope.shape, F32), pltpu.VMEM(normed.shape, BF16),
-        pltpu.VMEM((rows, width), F32), pltpu.VMEM((width, units), F32), pltpu.VMEM((width, units), F32),
-        dma_sems(9),
-    ]
-    scratch += exchange_scratch(rows, width, BF16) + [dma_sems(GATHER_SEMS), dma_sems(GATHER_SEMS)]
-    extra = []
-    if behind:
-        extra = [earlier]
-        columns = earlier.shape[1]
-        outs.append(shape((share, columns)))
-        out_specs.append(VM)
-        scratch += [pltpu.VMEM((width, columns), F32), pltpu.VMEM((count // 2, share, columns), F32)]
-        scratch += pair_scratch(count, width, columns, BLOCKS) + owner_scratch(count, width, columns, BLOCKS)
-    if split:
-        scratch += pair_scratch(count, width, units, BLOCKS)
-    return pl.pallas_call(
-        functools.partial(ffn_backward_kernel, layer, count, split, behind),
-        out_shape=outs,
-        in_specs=[VM] * 4 + [ANY] * 6 + [VM] + [ANY] * len(extra),
-        out_specs=out_specs,
-        scratch_shapes=scratch,
-        compiler_params=params(5 + layer),
-        name="ffn_bwd",
-    )(grad, normal2, recip2, gain, wdown, wup, active, slope, normed, normal1, recip1, *extra)
-
-
-def attention_backward_kernel(layer, count, split, last, *refs):
-    refs = Refs(refs)
-    low_ref, du_hbm, wout_hbm, wqkv_hbm = refs.take(4)
-    saved_hbm = refs.take(8)
-    prefix_ref = refs.one()
-    up_hbm, half_hbm, smalls_in, bias_in = refs.take(4) if split else (None,) * 4
-    dx_ref, grads_hbm, bias_ref = refs.take(3)
-    up_sum, down_sum, smalls_sum = refs.take(3) if split else (None,) * 3
-    grads_sum, bias_sum = refs.take(2) if last else (None,) * 2
-    saved = refs.take(8)
-    whole_ref, qt_ref, q2_ref, kz_ref, kt_ref, v2_ref, ct_ref, stats_ref = saved
-    du_ref, wout_ref, wqkv_ref, grads_ref = refs.take(4)
-    do_ref, dc_ref, dct_ref, dq_ref, dk_ref, dv_ref, high_ref, lowbits_ref, xt_ref = refs.take(9)
-    moves = Moves(refs.one())
-    exchange_refs = refs.take(11)
-    g_send, g_recv = refs.take(2)
-    mine, partner, across, diagonal = places()
-    rows, width = low_ref.shape
-    heads = qt_ref.shape[0]
-    depth = heads * HDIM
-    scale = 1.0 / math.sqrt(HDIM)
-    sequences = Sequences(count) if split else None
-    entry = Entry(sequences)
-    wout_in = moves.start(wout_hbm.at[layer], wout_ref)
-    saved_in = [moves.start(source, target) for source, target in zip(saved_hbm, saved)]
-    up_pairs, up_owners, down_owners, small = [], [], [], None
-    own_pairs, own_owners, own_small = [], [], None
-    if split:
-        half_ref, up_ref, up_half, small_source = refs.take(4)
-        half_in = moves.start(half_hbm, half_ref)
-        up_in = moves.start(up_hbm, up_ref)
-        down_owners = owner_sums(sequences, half_ref, down_sum, refs.take(4), BLOCKS)
-        up_pairs = pair_sums(sequences, up_ref, up_half, refs.take(4), BLOCKS)
-        up_owners = owner_sums(sequences, up_half, up_sum, refs.take(4), BLOCKS)
-        small = SmallSum(sequences, small_source, smalls_sum, 6, refs.take(3), refs.take(6))
-    if last:
-        own_half = refs.one()
-        own_pairs = pair_sums(sequences, grads_ref, own_half, refs.take(4), BLOCKS)
-        own_owners = owner_sums(sequences, own_half, grads_sum, refs.take(4), BLOCKS)
-        own_small = SmallSum(sequences, bias_ref, bias_sum, 0, refs.take(3), refs.take(6))
-    wqkv_in = moves.start(wqkv_hbm.at[layer], wqkv_ref)
-    du_in = moves.start(du_hbm, du_ref)
-    gather = Gather(do_ref, g_send, g_recv)
-    exchange = Exchange(*exchange_refs[:5], exchange_refs[5:])
-    terms_ref = exchange.terms
-    do_ref[mine] = low_ref[...]
-    entry.wait()
-    gather.start()
-    if split:
-        is_bias = lax.broadcasted_iota(jnp.int32, small_source.shape, 0) == 7
-        small_source[...] = jnp.where(is_bias, bias_in[...], smalls_in[...])
-        small.start()
-        half_in.wait()
-        for item in down_owners:
-            item.start()
-        up_in.wait()
-        for item in up_pairs:
-            item.start()
-    dk_ref[...] = jnp.zeros_like(dk_ref)
+    first_gather.wait_sends()
+
+    lane_low = lax.broadcasted_iota(jnp.int32, (rows, LANES), 1) < HDIM
+    wide_ref[:, width // 2 :] = jnp.zeros((tall, width // 2), F32)
     dv_ref[...] = jnp.zeros_like(dv_ref)
-    lane_low = lax.broadcasted_iota(jnp.int32, (rows, LANES), 1) < HDIM
 
     def context_grad(chunk):
         spots = pl.ds(pl.multiple_of(chunk * rows, rows), rows)
@@ -992,118 +957,137 @@
             dc_ref[head, spots] = both.astype(BF16)
             dct_ref[head, :, spots] = both.T.astype(BF16)
 
-    def attend_back(chunk):
+    def attend_back(chunk, head):
         keys = visible_keys(chunk, rows)
         limits = query_limits(chunk, rows, prefix_ref[0])
         visible = lax.broadcasted_iota(jnp.int32, (keys, rows), 0) <= limits
         spots = pl.ds(chunk * rows, rows)
         seen = pl.ds(0, keys)
-
-        def one_head(head, carry):
-            scores = dot(kz_ref[head, seen], qt_ref[head, :, spots])
-            top = stats_ref[head, 0:1, spots]
-            recip = stats_ref[head, 1:2, spots]
-            probs = jnp.exp(jnp.where(visible, scores - top, -1e30)) * recip
-            grad_probs = dot(v2_ref[head, seen], dct_ref[head, :, spots])
-            inner = column_sum(probs * grad_probs)
-            grad_scores = (probs * (grad_probs - inner)).astype(BF16)
-            dv_ref[head, seen] = dv_ref[head, seen] + dot(probs.astype(BF16), dc_ref[head, spots])
-            dk_ref[head, seen] = dk_ref[head, seen] + dot(grad_scores, q2_ref[head, spots])
-            dq_ref[head, spots] = dot(kt_ref[head, :, seen], grad_scores).T * scale
-            return carry
-
-        lax.fori_loop(0, heads, one_head, 0)
+        dq_lanes = pl.ds(pl.multiple_of(head * LANES, LANES), LANES)
+        dk_lanes = pl.ds(pl.multiple_of((heads + head) * LANES, LANES), LANES)
+        scores = dot(kz_ref[head, seen], qt_ref[head, :, spots])
+        top = stats_ref[head, 0:1, spots]
+        recip = stats_ref[head, 1:2, spots]
+        probs = jnp.exp(jnp.where(visible, scores - top, -1e30)) * recip
+        grad_probs = dot(v2_ref[head, seen], dct_ref[head, :, spots])
+        inner = column_sum(probs * grad_probs)
+        grad_scores = (probs * (grad_probs - inner)).astype(BF16)
+        dv_ref[head, seen] = dv_ref[head, seen] + dot(probs.astype(BF16), dc_ref[head, spots])
+        wide_ref[seen, dk_lanes] = wide_ref[seen, dk_lanes] + dot(grad_scores, q2_ref[head, spots])
+        wide_ref[spots, dq_lanes] = dot(kt_ref[head, :, seen], grad_scores).T * scale
 
     chip, core = mine // 2, mine - 2 * (mine // 2)
 
-    def one_step(step, carry):
+    def weight_grad_out():
+        out_wide = dot(ct_ref[0], do_ref[0])
+        for chunk in range(1, GROUP):
+            out_wide = out_wide + dot(ct_ref[chunk], do_ref[chunk])
+        grads_ref[:, :depth] = out_wide.T
+
+    def gathered(step):
+        if step == 1:
+            second_gather.wait_partner()
+        if step == 2:
+            for part in range(BACK_PIECES):
+                second_gather.wait_across(part)
+                second_gather.onward(part).start()
+        if step == 3:
+            for part in range(BACK_PIECES):
+                second_gather.wait_diagonal(part)
+
+    beside = {heads: [lambda: gathered(1)], 2 * heads: [lambda: gathered(2)], 3 * heads: [lambda: gathered(3)]}
+    if split:
+        beside[heads].append(downs[0].turn)
+        beside[2 * heads].append(small.first)
+        beside[2 * heads].append(downs[1].turn)
+        beside[4 * heads - 1] = [ups[0].turn]
+        for item in earlier:
+            beside[2 * heads].append(item.finish)
+    if last:
+        beside[3 * heads] += [weight_grad_out, own[0].start]
+
+    def one_turn(turn, carry):
+        step = turn // heads
+        head = lax.rem(turn, heads)
         near = 1 - step // 2
         flip = lax.rem(step, 2)
         to_chip = (1 - near) * (1 - chip) + near * chip
         chunk = 2 * to_chip + core + flip * (1 - 2 * core)
-
-        @pl.when(step == 1)
+        for when in sorted(beside):
+            @pl.when(turn == when)
+            def _():
+                for action in beside[when]:
+                    action()
+
+        @pl.when(head == 0)
         def _():
-            gather.wait_partner()
-            if split:
-                small.first()
-
-        @pl.when(step == 2)
-        def _():
-            for part in range(PIECES):
-                gather.wait_across(part)
-                gather.onward(part).start()
-            if split:
-                up_pairs[0].finish()
-                up_owners[0].start()
-
-        @pl.when(step == 3)
-        def _():
-            for part in range(PIECES):
-                gather.wait_diagonal(part)
-            if split:
-                up_pairs[1].finish()
-                up_owners[1].start()
-                small.second()
-
-        context_grad(chunk)
+            context_grad(chunk)
+
         for each in range(GROUP):
             @pl.when(chunk == each)
             def _():
-                attend_back(each)
+                attend_back(each, head)
         return carry
 
     wout_in.wait()
+    wqkv_in.wait()
+    for kind in range(3):
+        wqkv_t_ref[kind] = transposed(wqkv_ref[kind]).astype(BF16)
     for move in saved_in:
         move.wait()
-    lax.fori_loop(0, GROUP, one_step, 0)
+    lax.fori_loop(0, GROUP * heads, one_turn, 0)
+
+    def kind_lanes(kind):
+        return slice(kind * span, kind * span + depth)
 
     def pack_chunk(chunk, carry):
         spots = pl.ds(pl.multiple_of(chunk * rows, rows), rows)
-        xt_ref[:, spots] = transposed(whole_ref[chunk]).astype(BF16)
-        for kind, wide_ref in enumerate((dq_ref, dk_ref, dv_ref)):
+        xt_ref[:, spots] = transposed(normed_ref[chunk]).astype(BF16)
+        for kind in range(3):
             parts = []
             for head in range(heads):
-                wide = wide_ref[head, spots]
-                if kind == 2:
+                if kind < 2:
+                    wide = wide_ref[spots, slice((kind * heads + head) * LANES, (kind * heads + head + 1) * LANES)]
+                else:
+                    wide = dv_ref[head, spots]
                     wide = wide + pltpu.roll(wide, HDIM, 1)
                 parts.append(wide[:, :HDIM])
             values = jnp.concatenate(parts, axis=1)
-            high_ref[kind, spots], lowbits_ref[kind, spots] = high_low(values)
+            high, low = high_low(values)
+            high_ref[spots, kind_lanes(kind)] = high
+            lowbits_ref[spots, kind_lanes(kind)] = low
             if kind != 1:
                 place = slice((kind // 2) * depth, (kind // 2 + 1) * depth)
                 bias_ref[:, place] = bias_ref[:, place] + column_sum(values)
         return carry
 
     bias_ref[...] = jnp.zeros_like(bias_ref)
+    whole_in.wait()
     lax.fori_loop(0, GROUP, pack_chunk, 0)
 
-    def weight_grads():
-        out_wide = dot(ct_ref[0], do_ref[0])
-        for chunk in range(1, GROUP):
-            out_wide = out_wide + dot(ct_ref[chunk], do_ref[chunk])
-        grads_ref[:, :depth] = out_wide.T
-        for kind in range(3):
-            place = slice((kind + 1) * depth, (kind + 2) * depth)
-            grads_ref[:, place] = dot(xt_ref[...], high_ref[kind]) + dot(xt_ref[...], lowbits_ref[kind])
+    def weight_grad(kind):
+        place = slice((kind + 1) * depth, (kind + 2) * depth)
+        lanes = kind_lanes(kind)
+        grads_ref[:, place] = dot(xt_ref[...], high_ref[:, lanes]) + dot(xt_ref[...], lowbits_ref[:, lanes])
 
     def input_terms(chunk, part):
-        spot = exchange.spot(part)
-        spots = pl.ds(pl.multiple_of(chunk * rows + part * (rows // PIECES), rows // PIECES), rows // PIECES)
+        spots = part_spots(chunk, part)
         total = None
         for kind in range(3):
             for values in (high_ref, lowbits_ref):
-                term = dot_nt(values[kind, spots], wqkv_ref[kind])
+                term = dot(values[spots, kind_lanes(kind)], wqkv_t_ref[kind])
                 total = term if total is None else total + term
-        terms_ref[chunk, spot] = total
-
-    wqkv_in.wait()
+        terms_ref[chunk, exchange.spot(part)] = total
+
     if last:
-        weight_grads()
         own_small.first()
-        for item in own_pairs:
-            item.start()
-    for part in range(PIECES):
+        weight_grad(0)
+        own[1].start()
+        weight_grad(1)
+        weight_grad(2)
+        own[2].start()
+        own[3].start()
+    for part in range(BACK_PIECES):
         input_terms(diagonal, part)
         exchange.relay_copy(part).start()
         input_terms(across, part)
@@ -1111,40 +1095,40 @@
             exchange.pass_on(part - 1)
     input_terms(partner, 0)
     exchange.near_copy(0).start()
-    exchange.pass_on(PIECES - 1)
-    for part in range(1, PIECES):
+    exchange.pass_on(BACK_PIECES - 1)
+    for part in range(1, BACK_PIECES):
         input_terms(partner, part)
         exchange.near_copy(part).start()
+    for part in range(BACK_PIECES):
+        input_terms(mine, part)
+    if split:
+        ups[1].turn()
+        small.second()
     if last:
-        own_pairs[0].finish()
-        own_owners[0].start()
-    for part in range(PIECES):
-        input_terms(mine, part)
-    if not last:
-        weight_grads()
+        own[0].turn()
+        own[1].turn()
+        own[2].turn()
+        own[3].turn()
+        own_small.second()
+    else:
+        weight_grad_out()
+        for kind in range(3):
+            weight_grad(kind)
         moves.store(grads_ref, grads_hbm)
+    for item in downs + ups:
+        item.finish()
+    for part in range(BACK_PIECES):
+        spot = exchange.spot(part)
+        dx_ref[spot] = exchange.result(part) + du_ref[spot]
     if split:
         small.third()
-        for item in down_owners:
-            item.finish()
-    if last:
-        own_pairs[1].finish()
-        own_owners[1].start()
-        own_small.second()
-    for item in up_owners:
-        item.finish()
-    du_in.wait()
-    for part in range(PIECES):
-        spot = exchange.spot(part)
-        dx_ref[spot] = exchange.result(part) + du_ref[spot]
     if last:
         own_small.third()
-        for item in own_owners:
+        for item in own:
             item.finish()
-        grads_hbm[...] = bias_ref[...]
-    gather.wait_sends()
+    second_gather.wait_sends()
     exchange.wait_sends()
-    for item in down_owners + up_pairs + up_owners + own_pairs + own_owners:
+    for item in earlier + downs + ups + own:
         item.wait_sends()
     for item in (small, own_small):
         if item is not None:
@@ -1152,53 +1136,63 @@
     moves.finish()
 
 
-def attention_layer_back(layer, count, split, low, du, wout, wqkv, saved, prefix, extra):
-    rows, width = low.shape
-    last = split and layer == 0
-    depth = wout.shape[1]
+def layer_back(layer, count, split, grad, normal2, recip2, gain, recip1, hbm, prefix, earlier):
+    rows, width = grad.shape
+    wdown, wup, active, slope, normed, normal1, wout, wqkv, *saved = hbm
+    units, depth = wup.shape[2], wout.shape[1]
     heads = depth // HDIM
     tall = GROUP * rows
+    share = width // count
+    behind = split and earlier is not None
+    last = split and layer == 0
     columns = 4 * depth
-    share = width // count
-    outs = [shape((rows, width)), shape((8, width) if last else (width, columns)), shape((8, width))]
-    out_specs = [VM, VM if last else ANY, VM]
-    scratch = [pltpu.VMEM(each.shape, each.dtype) for each in saved]
+    if not (columns == width == units == 2 * heads * LANES):
+        raise ValueError("unsupported sizes")
+    outs, out_specs = [shape((rows, width)), shape((8, width))], [VM, VM]
+    if not last:
+        outs.append(shape((width, columns)))
+        out_specs.append(ANY)
+    outs += [shape((share if split else width, units))] * 2 + [shape((8, width))]
+    out_specs += [VM, VM, VM] if split else [ANY, ANY, VM]
+    if behind:
+        outs.append(shape((share, columns)))
+        out_specs.append(VM)
+    if last:
+        outs += [shape((share, columns)), shape((8, width))]
+        out_specs += [VM, VM]
+    whole_rows = pltpu.VMEM((GROUP, rows, width), BF16)
+    square = pltpu.VMEM((width, units), F32)
+    scratch = [
+        whole_rows, whole_rows, pltpu.VMEM((rows, width), F32),
+        pltpu.VMEM((tall, units), BF16), pltpu.VMEM((tall, units), BF16),
+        pltpu.VMEM(wdown.shape[1:], BF16), pltpu.VMEM(wup.shape[1:], BF16), whole_rows,
+        pltpu.VMEM((tall, units), F32), whole_rows, pltpu.VMEM((rows, width), F32),
+        square, square, square, pltpu.VMEM((8, width), F32),
+    ]
+    scratch += [pltpu.VMEM(each.shape, each.dtype) for each in saved[1:]]
     scratch += [
-        pltpu.VMEM((rows, width), F32), pltpu.VMEM(wout.shape[1:], BF16), pltpu.VMEM(wqkv.shape[1:], BF16),
-        pltpu.VMEM((width, columns), F32),
-        pltpu.VMEM((GROUP, rows, width), BF16),
+        pltpu.VMEM(wout.shape[1:], BF16), pltpu.VMEM(wqkv.shape[1:], BF16), pltpu.VMEM((3, depth, width), BF16),
         pltpu.VMEM((heads, tall, LANES), BF16), pltpu.VMEM((heads, LANES, tall), BF16),
-        pltpu.VMEM((heads, tall, LANES), F32), pltpu.VMEM((heads, tall, LANES), F32),
-        pltpu.VMEM((heads, tall, LANES), F32),
-        pltpu.VMEM((3, tall, depth), BF16), pltpu.VMEM((3, tall, depth), BF16),
-        pltpu.VMEM((width, tall), BF16),
-        dma_sems(14),
+        pltpu.VMEM((heads, tall, LANES), F32), pltpu.VMEM((width, tall), BF16),
+        dma_sems(24),
     ]
-    scratch += exchange_scratch(rows, width, BF16) + [dma_sems(GATHER_SEMS), dma_sems(GATHER_SEMS)]
+    scratch += exchange_scratch(rows, width, BF16, BACK_PIECES) + gather_sems(BACK_PIECES) + gather_sems(BACK_PIECES)
+    if behind:
+        scratch += total_scratch(count, width, columns, 2)
     if split:
-        units = extra[0].shape[1]
-        outs += [shape((share, units)), shape((share, units)), shape((8, width))]
-        out_specs += [VM] * 3
-        half = pltpu.VMEM((count // 2, share, units), F32)
-        scratch += [half, pltpu.VMEM((width, units), F32), half, pltpu.VMEM((8, width), F32)]
-        scratch += owner_scratch(count, width, units, BLOCKS)
-        scratch += pair_scratch(count, width, units, BLOCKS) + owner_scratch(count, width, units, BLOCKS)
+        scratch += total_scratch(count, width, units, 2) + total_scratch(count, width, units, 2)
         scratch += small_sum_scratch(count, width)
     if last:
-        outs += [shape((share, columns)), shape((8, width))]
-        out_specs += [VM] * 2
-        scratch += [pltpu.VMEM((count // 2, share, columns), F32)]
-        scratch += pair_scratch(count, width, columns, BLOCKS) + owner_scratch(count, width, columns, BLOCKS)
-        scratch += small_sum_scratch(count, width)
+        scratch += total_scratch(count, width, columns, 4) + small_sum_scratch(count, width)
     return pl.pallas_call(
-        functools.partial(attention_backward_kernel, layer, count, split, last),
+        functools.partial(layer_backward_kernel, layer, count, split, behind, last),
         out_shape=outs,
-        in_specs=[VM, ANY, ANY, ANY] + [ANY] * 8 + [SM] + ([ANY, ANY, VM, VM] if split else []),
+        in_specs=[VM] * 5 + [ANY] * 16 + [SM] + ([ANY, VM] if behind else []),
         out_specs=out_specs,
         scratch_shapes=scratch,
-        compiler_params=params(7 + layer),
-        name="attention_bwd",
-    )(low, du, wout, wqkv, *saved, prefix, *extra)
+        compiler_params=params(5 + layer),
+        name="layer_bwd",
+    )(grad, normal2, recip2, gain, recip1, *hbm, prefix, *(earlier if behind else ()))
 
 
 def results_kernel(depth, *refs):
@@ -1279,28 +1273,27 @@
     count = lax.axis_size("dp")
     split = count > 2 and count % 2 == 0 and (width // count) % 16 == 0
     grad = cotangent
-    bias = jnp.zeros((8, width), F32)
     earlier = None
     attn, up, down, smalls, biases = [], [], [], [], []
     for layer in reversed(range(layer_count)):
-        second, middle, saved = stored[layer]
-        du, low, up_grad, down_grad, small, *sums = ffn_layer_back(
-            layer, count, split, grad, *second, norm_gain, w_down, w_up, *middle, earlier
-        )
-        attn = (sums + attn) if split else attn
-        extra = (up_grad, down_grad, small, bias) if split else ()
-        grad, earlier, bias, *sums = attention_layer_back(
-            layer, count, split, low, du, w_out, w_qkv, saved, prefix, extra
-        )
+        (normal2, recip2), (active, slope, normed, normal1, recip1), saved = stored[layer]
+        hbm = (w_down, w_up, active, slope, normed, normal1, w_out, w_qkv, *saved)
+        grad, bias, *rest = layer_back(
+            layer, count, split, grad, normal2, recip2, norm_gain, recip1, hbm, prefix, earlier
+        )
+        if split and layer == 0:
+            up_sum, down_sum, small, *rest = rest
+            attn = rest[: len(rest) - 2] + attn
+            attn.insert(0, rest[-2])
+            return results(
+                state, grad, attn, [up_sum] + up, [down_sum] + down, rest[-1], [small] + smalls, depth
+            )
+        attn_grad, up_grad, down_grad, small, *rest = rest
         if split:
-            up.insert(0, sums[0])
-            down.insert(0, sums[1])
-            smalls.insert(0, sums[2])
-            if layer == 0:
-                attn.insert(0, sums[3])
-                return results(state, grad, attn, up, down, sums[4], smalls, depth)
-            continue
-        attn.insert(0, earlier)
+            earlier = (attn_grad, bias)
+            attn = rest + attn
+        else:
+            attn.insert(0, attn_grad)
         up.insert(0, up_grad)
         down.insert(0, down_grad)
         smalls.insert(0, small)

time: 324 us -> 287 us (0.89)
  Pallas kernels: 311 us -> 274 us
    pallas_call x4 -> x2, Pallas kernels: 177 us -> 147 us  [layer_back(): pl.pallas_call(functools.partial(layer_backward_kernel, layer, count, spl...]
    pallas_call x2, Pallas kernels: 70 us -> 63.2 us  [ffn_layer(): pl.pallas_call(functools.partial(ffn_forward_kernel, layer), out_shape=[s...]
where the time goes in v4:
time: 287 us; the launch traced here: 282 us
  Pallas kernels  274 us (95%)
  local copies, waits for them, and re-layouts  6.24 us (2%)
    pallas_call x2, Pallas kernels, layer_back(): pl.pallas_call(functools.partial(layer_backward_kernel, layer, count, spl...  147 us
    pallas_call x2, Pallas kernels, ffn_layer(): pl.pallas_call(functools.partial(ffn_forward_kernel, layer), out_shape=[s...  63.2 us
    pallas_call x2, Pallas kernels, attention_layer(): pl.pallas_call(functools.partial(attention_forward_kernel, layer), out_sh...  60.2 us

profile of v4, /device:TPU:0, one launch (start us, length us, event | category | flops | bytes accessed | tf_op | source)
XLA Modules:
  0.0 282.2 jit_solution(933306646812491013)
XLA Ops:
  1.3 4.0 %copy.25.refs_2_.refs_12_ = bf16[2,3,768,192]{3,2,1,0:T(8,128)(2,1)} copy(bf16[2,3,768,192]{2,3,1,0:T(8,128)(2,1)} %param.16) | data formatting | bytes 3538944 | tf_op args[3]
  5.3 31.2 %attention_fwd.2 = (f32[256,768]{1,0:T(8,128)}, bf16[256,768]{1,0:T(8,128)(2,1)}, f32[256,768]{1,0:T(8,128)}, f32[256,128]{1,0:T(8,128)}, bf16[4,256,768]{2,1,0:...) custom-call(bf16[256,768]{1,0:T(8,128)(2,1)} %refs_1_.1, ...), custom_call_target="tpu_custom_call" | custom-call | tf_op jit(solution)/shard_map/attention_fwd/pallas_call | solution.py:458
  36.6 31.4 %ffn_fwd.2 = (f32[256,768]{1,0:T(8,128)}, bf16[256,768]{1,0:T(8,128)(2,1)}, f32[256,768]{1,0:T(8,128)}, f32[256,128]{1,0:T(8,128)}, bf16[4,256,768]{2,1,0:T(8,12...) custom-call(f32[256,768]{1,0:T(8,128)} %get-tuple-element.62.refs_0_, ...), custom_call_target="tpu_custom_call" | custom-call | tf_op jit(solution)/shard_map/ffn_fwd/pallas_call | solution.py:555
  68.0 28.9 %attention_fwd.3 = (f32[256,768]{1,0:T(8,128)}, bf16[256,768]{1,0:T(8,128)(2,1)}, f32[256,768]{1,0:T(8,128)}, f32[256,128]{1,0:T(8,128)}, bf16[4,256,768]{2,1,0:...) custom-call(f32[256,768]{1,0:T(8,128)} %get-tuple-element.64.refs_0_, ...), custom_call_target="tpu_custom_call" | custom-call | tf_op jit(solution)/shard_map/attention_fwd/pallas_call | solution.py:458
  97.0 31.8 %ffn_fwd.3 = (f32[256,768]{1,0:T(8,128)}, bf16[256,768]{1,0:T(8,128)(2,1)}, f32[256,768]{1,0:T(8,128)}, f32[256,128]{1,0:T(8,128)}, bf16[4,256,768]{2,1,0:T(8,12...) custom-call(f32[256,768]{1,0:T(8,128)} %get-tuple-element.66.refs_0_, ...), custom_call_target="tpu_custom_call" | custom-call | tf_op jit(solution)/shard_map/ffn_fwd/pallas_call | solution.py:555
  128.7 63.0 %layer_bwd.2 = (f32[256,768]{1,0:T(8,128)}, f32[8,768]{1,0:T(8,128)}, f32[768,768]{1,0:T(8,128)}, f32[96,768]{1,0:T(8,128)}, f32[96,768]{1,0:T(8,128)}, /*index=5*/f32[8,768]{1,0:T(8,128)}) custom-call(bf16[256,768]{1,0:T(8,128)(2,1)} %refs_0_.3, f32[256,768]{1,0:T(8,128)} %get-tuple-element.69.refs_1_, f32[256,128]{1,0:T(8,128)} %get-tuple-element.70.refs_2_, ...), custom_call_target="tpu_custom_call" | custom-call | tf_op jit(solution)/shard_map/layer_bwd/pallas_call | solution.py:1187
  191.7 83.8 %layer_bwd.3 = (f32[256,768]{1,0:T(8,128)}, f32[8,768]{1,0:T(8,128)}, f32[96,768]{1,0:T(8,128)}, f32[96,768]{1,0:T(8,128)}, f32[8,768]{1,0:T(8,128)}, /*index=5*...) custom-call(f32[256,768]{1,0:T(8,128)} %get-tuple-element.84.refs_0_, f32[256,768]{1,0:T(8,128)} %get-tuple-element.85.refs_1_, ...), custom_call_target="tpu_custom_call" | custom-call | tf_op jit(solution)/shard_map/layer_bwd/pallas_call | solution.py:1187
  275.5 4.2 %results.1 = (f32[256,768]{1,0:T(8,128)}, f32[256,768]{1,0:T(8,128)}, f32[2,3,96,192]{3,2,1,0:T(8,128)}, f32[2,2,192]{2,1,0:T(2,128)}, f32[2,192,96]{2,1,0:T(8,1...) custom-call(f32[256,768]{1,0:T(8,128)} %get-tuple-element.68.refs_0_, ...), custom_call_target="tpu_custom_call" | custom-call | tf_op jit(solution)/shard_map/results/pallas_call | solution.py:1230
  279.7 2.2 copy.29

commit v5 on v4

--- a/solution.py
+++ b/solution.py
@@ -299,16 +299,20 @@
     ] + [dma_sems(pieces)] * 6
 
 
-def attention_forward_kernel(layer, *refs):
+def layer_forward_kernel(layer, *refs):
     refs = Refs(refs)
-    state_hbm, low_ref, wqkv_hbm, bias_ref, wout_hbm, bias_out_ref, gain_ref, shift_ref, prefix_ref = refs.take(9)
-    next_ref, next_low_ref, normal_ref, recip_ref = refs.take(4)
-    saved_hbm = refs.take(8)
+    state_hbm, low_ref, wqkv_hbm, bias_ref, wout_hbm, bias_out_ref, gain_ref, shift_ref = refs.take(8)
+    wup_hbm, bias_up_ref, wdown_hbm, bias_down_ref, prefix_ref = refs.take(5)
+    next_ref, next_low_ref, normal1_ref, recip1_ref, normal2_ref, recip2_ref = refs.take(6)
+    saved_hbm, ffn_saved_hbm = refs.take(8), refs.take(3)
     saved = refs.take(8)
     whole_ref, qt_ref, q2_ref, kz_ref, kt_ref, v2_ref, ct_ref, stats_ref = saved
     state_ref, wqkv_ref, vt_ref, cf_ref, wo_ref = refs.take(5)
+    normed_ref, active_ref, slope_ref = refs.take(3)
+    total_ref, wup_ref, wdown_ref = refs.take(3)
     moves = Moves(refs.one())
     g_send, g_recv, c_send, c_recv, w_send, w_recv = refs.take(6)
+    exchange_refs, second_sems = refs.take(11), refs.take(2)
     mine, partner, across, diagonal = places()
     rows = low_ref.shape[0]
     heads = qt_ref.shape[0]
@@ -317,6 +321,8 @@
     wqkv_in = moves.start(wqkv_hbm.at[layer], wqkv_ref)
     wout_in = moves.start(wout_hbm.at[layer], wo_ref.at[mine])
     state_in = moves.start(state_hbm, state_ref)
+    wup_in = moves.start(wup_hbm.at[layer], wup_ref)
+    wdown_in = moves.start(wdown_hbm.at[layer], wdown_ref)
     gather = Gather(whole_ref, g_send, g_recv, ATTN_PIECES)
     whole_ref[mine] = low_ref[...]
     entry.wait()
@@ -326,9 +332,9 @@
     def project(chunk):
         spots = pl.ds(pl.multiple_of(chunk * rows, rows), rows)
         values = whole_ref[chunk]
-        query = (dot(values, wqkv_ref[0]) + bias_ref[layer, 0:1]) * root
-        key = dot(values, wqkv_ref[1])
-        value = dot(values, wqkv_ref[2]) + bias_ref[layer, 1:2]
+        query = (dot_nt(values, wqkv_ref[0]) + bias_ref[layer, 0:1]) * root
+        key = dot_nt(values, wqkv_ref[1])
+        value = dot_nt(values, wqkv_ref[2]) + bias_ref[layer, 1:2]
         queries, keys, valuess = [head_pairs(each, heads) for each in (query, key, value)]
         query_t, key_t, value_t = [each.T.astype(BF16) for each in (query, key, value)]
         for head in range(heads):
@@ -427,26 +433,79 @@
     depth = GROUP * wo_ref.shape[1]
     context = transposed(cf_ref[...].reshape(depth, rows)).astype(BF16)
     state_in.wait()
-    total = (
+    total_ref[...] = (
         state_ref[...].astype(F32) + dot(context, wo_ref[...].reshape(depth, -1)) + bias_out_ref[layer : layer + 1]
     )
-    result, normal, recip = layer_norm(total, gain_ref[layer, 0:1], shift_ref[layer, 0:1])
-    next_ref[...] = result
-    next_low_ref[...] = result.astype(BF16)
-    normal_ref[...] = normal
-    recip_ref[...] = jnp.broadcast_to(recip, recip_ref.shape)
+    second = Gather(normed_ref, *second_sems, FFN_PIECES)
+    exchange = Exchange(*exchange_refs[:5], exchange_refs[5:], FFN_PIECES)
+    terms_ref = exchange.terms
+    part_rows = rows // FFN_PIECES
+    for part in range(FFN_PIECES):
+        spot = exchange.spot(part)
+        result, normal, recip = layer_norm(total_ref[spot], gain_ref[layer, 0:1], shift_ref[layer, 0:1])
+        normed_ref[mine, spot] = result.astype(BF16)
+        second.to_across(part).start()
+        total_ref[spot] = result
+        normal1_ref[spot] = normal
+        recip1_ref[spot] = jnp.broadcast_to(recip, (part_rows, LANES))
+    second.to_partner().start()
     gather.wait_sends()
     wout_to_across.wait_send()
     wout_to_partner(mine).wait_send()
     wout_to_partner(across).wait_send()
     for step, chunk in enumerate((across, diagonal, partner)):
         context_copy(step, chunk).wait_send()
+
+    def units(chunk, part):
+        spot = exchange.spot(part)
+        hidden = dot(normed_ref[chunk, spot], wup_ref[...]) + bias_up_ref[layer : layer + 1]
+        below = 0.5 * (1.0 + lax.erf(hidden * math.sqrt(0.5)))
+        density = jnp.exp(-0.5 * hidden * hidden) * (1.0 / math.sqrt(2.0 * math.pi))
+        active = (hidden * below).astype(BF16)
+        active_ref[chunk, spot] = active
+        slope_ref[chunk, spot] = below + hidden * density
+        terms_ref[chunk, spot] = dot(active, wdown_ref[...])
+
+    wup_in.wait()
+    wdown_in.wait()
+    for part in range(FFN_PIECES):
+        units(mine, part)
+    for part in range(FFN_PIECES):
+        second.wait_across(part)
+        second.onward(part).start()
+        units(across, part)
+        second.wait_diagonal(part)
+        units(diagonal, part)
+        exchange.relay_copy(part).start()
+        if part > 0:
+            exchange.pass_on(part - 1)
+    second.wait_partner()
+    moves.store(normed_ref, ffn_saved_hbm[0])
+    units(partner, 0)
+    exchange.near_copy(0).start()
+    exchange.pass_on(FFN_PIECES - 1)
+    for part in range(1, FFN_PIECES):
+        units(partner, part)
+        exchange.near_copy(part).start()
+    moves.store(active_ref, ffn_saved_hbm[1])
+    moves.store(slope_ref, ffn_saved_hbm[2])
+    for part in range(FFN_PIECES):
+        spot = exchange.spot(part)
+        total = total_ref[spot] + exchange.result(part) + bias_down_ref[layer : layer + 1]
+        result, normal, recip = layer_norm(total, gain_ref[layer, 1:2], shift_ref[layer, 1:2])
+        next_ref[spot] = result
+        next_low_ref[spot] = result.astype(BF16)
+        normal2_ref[spot] = normal
+        recip2_ref[spot] = jnp.broadcast_to(recip, (part_rows, LANES))
+    second.wait_sends()
+    exchange.wait_sends()
     moves.finish()
 
 
-def attention_layer(layer, state, low, wqkv, bias, wout, bias_out, gain, shift, prefix):
+def layer_forward(layer, state, low, wqkv, bias, wout, bias_out, gain, shift, wup, bias_up, wdown, bias_down, prefix):
     rows, width = low.shape
     depth = wout.shape[1]
+    units = wup.shape[2]
     heads = depth // HDIM
     tall = GROUP * rows
     saved = [
@@ -455,120 +514,29 @@
         ((heads, LANES, tall), BF16), ((heads, tall, LANES), BF16), ((GROUP, depth, rows), BF16),
         ((heads, 8, tall), F32),
     ]
+    ffn_saved = [((GROUP, rows, width), BF16), ((GROUP, rows, units), BF16), ((GROUP, rows, units), F32)]
+    norms = [shape((rows, width)), shape((rows, LANES))]
     return pl.pallas_call(
-        functools.partial(attention_forward_kernel, layer),
-        out_shape=[
-            shape((rows, width)), shape((rows, width), BF16), shape((rows, width)), shape((rows, LANES)),
-        ] + [shape(*each) for each in saved],
-        in_specs=[ANY, VM, ANY, VM, ANY, VM, VM, VM, SM],
-        out_specs=[VM] * 4 + [ANY] * 8,
+        functools.partial(layer_forward_kernel, layer),
+        out_shape=[shape((rows, width)), shape((rows, width), BF16)] + norms + norms
+        + [shape(*each) for each in saved + ffn_saved],
+        in_specs=[ANY, VM, ANY, VM, ANY, VM, VM, VM, ANY, VM, ANY, VM, SM],
+        out_specs=[VM] * 6 + [ANY] * 11,
         scratch_shapes=[pltpu.VMEM(*each) for each in saved] + [
             pltpu.VMEM((rows, width), state.dtype),
             pltpu.VMEM(wqkv.shape[1:], BF16),
             pltpu.VMEM((heads, HDIM, tall), BF16),
             pltpu.VMEM((GROUP, depth, rows), BF16),
             pltpu.VMEM((GROUP, depth, width), BF16),
-            dma_sems(11),
+        ] + [pltpu.VMEM(*each) for each in ffn_saved] + [
+            pltpu.VMEM((rows, width), F32), pltpu.VMEM(wup.shape[1:], BF16), pltpu.VMEM(wdown.shape[1:], BF16),
+            dma_sems(16),
             *gather_sems(ATTN_PIECES),
             dma_sems(3), dma_sems(3), dma_sems(3), dma_sems(3),
-        ],
+        ] + exchange_scratch(rows, width, F32, FFN_PIECES) + gather_sems(FFN_PIECES),
         compiler_params=params(1 + layer),
-        name="attention_fwd",
-    )(state, low, wqkv, bias, wout, bias_out, gain, shift, prefix)
-
-
-def ffn_forward_kernel(layer, *refs):
-    refs = Refs(refs)
-    state_hbm, low_ref, wup_hbm, bias_up_ref, wdown_hbm, bias_down_ref, gain_ref, shift_ref = refs.take(8)
-    next_ref, next_low_ref, normal_ref, recip_ref = refs.take(4)
-    saved_hbm = refs.take(3)
-    whole_ref, active_ref, slope_ref = refs.take(3)
-    state_ref, wup_ref, wdown_ref = refs.take(3)
-    moves = Moves(refs.one())
-    exchange_refs = refs.take(11)
-    g_send, g_recv = refs.take(2)
-    mine, partner, across, diagonal = places()
-    rows = low_ref.shape[0]
-    part_rows = rows // FFN_PIECES
-    entry = Entry()
-    wup_in = moves.start(wup_hbm.at[layer], wup_ref)
-    wdown_in = moves.start(wdown_hbm.at[layer], wdown_ref)
-    state_in = moves.start(state_hbm, state_ref)
-    gather = Gather(whole_ref, g_send, g_recv, FFN_PIECES)
-    whole_ref[mine] = low_ref[...]
-    entry.wait()
-    gather.start()
-    exchange = Exchange(*exchange_refs[:5], exchange_refs[5:], FFN_PIECES)
-    terms_ref = exchange.terms
-
-    def units(chunk, part):
-        spot = exchange.spot(part)
-        hidden = dot(whole_ref[chunk, spot], wup_ref[...]) + bias_up_ref[layer : layer + 1]
-        below = 0.5 * (1.0 + lax.erf(hidden * math.sqrt(0.5)))
-        density = jnp.exp(-0.5 * hidden * hidden) * (1.0 / math.sqrt(2.0 * math.pi))
-        active = (hidden * below).astype(BF16)
-        active_ref[chunk, spot] = active
-        slope_ref[chunk, spot] = below + hidden * density
-        terms_ref[chunk, spot] = dot(active, wdown_ref[...])
-
-    wup_in.wait()
-    wdown_in.wait()
-    for part in range(FFN_PIECES):
-        units(mine, part)
-    for part in range(FFN_PIECES):
-        gather.wait_across(part)
-        gather.onward(part).start()
-        units(across, part)
-        gather.wait_diagonal(part)
-        units(diagonal, part)
-        exchange.relay_copy(part).start()
-        if part > 0:
-            exchange.pass_on(part - 1)
-    gather.wait_partner()
-    moves.store(whole_ref, saved_hbm[0])
-    units(partner, 0)
-    exchange.near_copy(0).start()
-    exchange.pass_on(FFN_PIECES - 1)
-    for part in range(1, FFN_PIECES):
-        units(partner, part)
-        exchange.near_copy(part).start()
-    moves.store(active_ref, saved_hbm[1])
-    moves.store(slope_ref, saved_hbm[2])
-    state_in.wait()
-    for part in range(FFN_PIECES):
-        spot = exchange.spot(part)
-        total = state_ref[spot] + exchange.result(part) + bias_down_ref[layer : layer + 1]
-        result, normal, recip = layer_norm(total, gain_ref[layer, 1:2], shift_ref[layer, 1:2])
-        next_ref[spot] = result
-        next_low_ref[spot] = result.astype(BF16)
-        normal_ref[spot] = normal
-        recip_ref[spot] = jnp.broadcast_to(recip, (part_rows, LANES))
-    gather.wait_sends()
-    exchange.wait_sends()
-    moves.finish()
-
-
-def ffn_layer(layer, state, low, wup, bias_up, wdown, bias_down, gain, shift):
-    rows, width = low.shape
-    units = wup.shape[2]
-    saved = [((GROUP, rows, width), BF16), ((GROUP, rows, units), BF16), ((GROUP, rows, units), F32)]
-    return pl.pallas_call(
-        functools.partial(ffn_forward_kernel, layer),
-        out_shape=[
-            shape((rows, width)), shape((rows, width), BF16), shape((rows, width)), shape((rows, LANES)),
-        ] + [shape(*each) for each in saved],
-        in_specs=[ANY, VM, ANY, VM, ANY, VM, VM, VM],
-        out_specs=[VM] * 4 + [ANY] * 3,
-        scratch_shapes=[pltpu.VMEM(*each) for each in saved]
-        + [
-            pltpu.VMEM((rows, width), F32), pltpu.VMEM(wup.shape[1:], BF16), pltpu.VMEM(wdown.shape[1:], BF16),
-            dma_sems(6),
-        ]
-        + exchange_scratch(rows, width, F32, FFN_PIECES)
-        + gather_sems(FFN_PIECES),
-        compiler_params=params(3 + layer),
-        name="ffn_fwd",
-    )(state, low, wup, bias_up, wdown, bias_down, gain, shift)
+        name="layer_fwd",
+    )(state, low, wqkv, bias, wout, bias_out, gain, shift, wup, bias_up, wdown, bias_down, prefix)
 
 
 def layer_norm_back(grad_in, normal, recip, gain):
@@ -687,16 +655,26 @@
     return pair_scratch(count, width, columns, blocks) + owner_scratch(count, width, columns, blocks)
 
 
+def pair_sums(sequences, source, scratch, blocks):
+    out, into, send, recv = scratch
+    return [
+        PairSum(sequences, source, columns, (out, into), (send.at[block], recv.at[block]))
+        for block, columns in enumerate(blocks)
+    ]
+
+
+def owner_sums(sequences, source, result, scratch, blocks):
+    out, into, send, recv = scratch
+    return [
+        OwnerSum(sequences, source, result, columns, (out, into), (send.at[block], recv.at[block]))
+        for block, columns in enumerate(blocks)
+    ]
+
+
 def total_sums(sequences, source, result, scratch, blocks):
-    first_out, first_in, n_send, n_recv, second_out, second_in, p_send, p_recv = scratch
-    sums = []
-    for block, columns in enumerate(blocks):
-        pair = PairSum(sequences, source, columns, (first_out, first_in), (n_send.at[block], n_recv.at[block]))
-        owner = OwnerSum(
-            sequences, source, result, columns, (second_out, second_in), (p_send.at[block], p_recv.at[block])
-        )
-        sums.append(BlockSum(pair, owner))
-    return sums
+    pairs = pair_sums(sequences, source, scratch[:4], blocks)
+    owners = owner_sums(sequences, source, result, scratch[4:], blocks)
+    return [BlockSum(pair, owner) for pair, owner in zip(pairs, owners)]
 
 
 TOTAL_REFS = 8
@@ -809,7 +787,7 @@
     up_ref, down_ref, grads_ref, smalls_ref = refs.take(4)
     saved = refs.take(7)
     qt_ref, q2_ref, kz_ref, kt_ref, v2_ref, ct_ref, stats_ref = saved
-    wout_ref, wqkv_ref, wqkv_t_ref = refs.take(3)
+    wout_ref, wqkv_ref = refs.take(2)
     dc_ref, dct_ref, dv_ref, xt_ref = refs.take(4)
     moves = Moves(refs.one())
     exchange_refs = refs.take(11)
@@ -833,7 +811,7 @@
     earlier, ups, downs, own, small, own_small = [], [], [], [], None, None
     if behind:
         earlier_in = moves.start(earlier_hbm, grads_ref)
-        earlier = total_sums(sequences, grads_ref, earlier_sum, refs.take(TOTAL_REFS), halves(width))
+        earlier = owner_sums(sequences, grads_ref, earlier_sum, refs.take(4), halves(width))
     if split:
         downs = total_sums(sequences, down_ref, down_out, refs.take(TOTAL_REFS), halves(units))
         ups = total_sums(sequences, up_ref, up_out, refs.take(TOTAL_REFS), halves(units))
@@ -841,6 +819,8 @@
     if last:
         own = total_sums(sequences, grads_ref, grads_sum, refs.take(TOTAL_REFS), tile_blocks(width))
         own_small = SmallSum(sequences, bias_ref, bias_sum, 0, refs.take(3), refs.take(6))
+    elif split:
+        own = pair_sums(sequences, grads_ref, refs.take(4), tile_blocks(width))
     active_in = moves.start(active_hbm, active_ref)
     normed_in = moves.start(normed_hbm, normed_ref)
     normal1_in = moves.start(normal1_hbm, normal1_ref)
@@ -899,8 +879,6 @@
         exchange.relay_copy(part).start()
         if part > 0:
             exchange.pass_on(part - 1)
-        if behind and part == 0:
-            earlier[0].turn()
     first_gather.wait_partner()
     back(partner, 0)
     exchange.near_copy(0).start()
@@ -912,13 +890,11 @@
     for part in range(1, BACK_PIECES):
         back(partner, part)
         exchange.near_copy(part).start()
-    if behind:
-        earlier[1].turn()
     normed_in.wait()
     normed = normed_ref[...].reshape(tall, width)
     up_ref[...] = dot_tn(normed, high_ref[...]) + dot_tn(normed, lowbits_ref[...])
-    for item in ups:
-        item.start()
+    if split:
+        ups[0].start()
     whole_in = moves.start(whole_hbm, normed_ref)
     if not split:
         moves.store(down_ref, down_out)
@@ -997,13 +973,11 @@
 
     beside = {heads: [lambda: gathered(1)], 2 * heads: [lambda: gathered(2)], 3 * heads: [lambda: gathered(3)]}
     if split:
-        beside[heads].append(downs[0].turn)
-        beside[2 * heads].append(small.first)
-        beside[2 * heads].append(downs[1].turn)
-        beside[4 * heads - 1] = [ups[0].turn]
+        plan = [(2, downs[0].turn), (6, small.first), (6, ups[1].start), (5, downs[1].turn), (9, ups[0].turn), (11, small.second)]
+        for when, action in plan:
+            beside.setdefault(when, []).append(action)
         for item in earlier:
             beside[2 * heads].append(item.finish)
-    if last:
         beside[3 * heads] += [weight_grad_out, own[0].start]
 
     def one_turn(turn, carry):
@@ -1031,8 +1005,6 @@
 
     wout_in.wait()
     wqkv_in.wait()
-    for kind in range(3):
-        wqkv_t_ref[kind] = transposed(wqkv_ref[kind]).astype(BF16)
     for move in saved_in:
         move.wait()
     lax.fori_loop(0, GROUP * heads, one_turn, 0)
@@ -1075,12 +1047,15 @@
         total = None
         for kind in range(3):
             for values in (high_ref, lowbits_ref):
-                term = dot(values[spots, kind_lanes(kind)], wqkv_t_ref[kind])
+                term = dot(values[spots, kind_lanes(kind)], wqkv_ref[kind])
                 total = term if total is None else total + term
         terms_ref[chunk, exchange.spot(part)] = total
 
+    if split:
+        ups[1].turn()
     if last:
         own_small.first()
+    if split:
         weight_grad(0)
         own[1].start()
         weight_grad(1)
@@ -1101,16 +1076,13 @@
         exchange.near_copy(part).start()
     for part in range(BACK_PIECES):
         input_terms(mine, part)
-    if split:
-        ups[1].turn()
-        small.second()
     if last:
         own[0].turn()
         own[1].turn()
         own[2].turn()
         own[3].turn()
         own_small.second()
-    else:
+    if not split:
         weight_grad_out()
         for kind in range(3):
             weight_grad(kind)
@@ -1124,8 +1096,10 @@
         small.third()
     if last:
         own_small.third()
-        for item in own:
-            item.finish()
+    for item in own:
+        item.finish()
+    if split and not last:
+        moves.store(grads_ref, grads_hbm)
     second_gather.wait_sends()
     exchange.wait_sends()
     for item in earlier + downs + ups + own:
@@ -1171,19 +1145,21 @@
     ]
     scratch += [pltpu.VMEM(each.shape, each.dtype) for each in saved[1:]]
     scratch += [
-        pltpu.VMEM(wout.shape[1:], BF16), pltpu.VMEM(wqkv.shape[1:], BF16), pltpu.VMEM((3, depth, width), BF16),
+        pltpu.VMEM(wout.shape[1:], BF16), pltpu.VMEM(wqkv.shape[1:], BF16),
         pltpu.VMEM((heads, tall, LANES), BF16), pltpu.VMEM((heads, LANES, tall), BF16),
         pltpu.VMEM((heads, tall, LANES), F32), pltpu.VMEM((width, tall), BF16),
         dma_sems(24),
     ]
     scratch += exchange_scratch(rows, width, BF16, BACK_PIECES) + gather_sems(BACK_PIECES) + gather_sems(BACK_PIECES)
     if behind:
-        scratch += total_scratch(count, width, columns, 2)
+        scratch += owner_scratch(count, width, columns, 2)
     if split:
         scratch += total_scratch(count, width, units, 2) + total_scratch(count, width, units, 2)
         scratch += small_sum_scratch(count, width)
     if last:
         scratch += total_scratch(count, width, columns, 4) + small_sum_scratch(count, width)
+    elif split:
+        scratch += pair_scratch(count, width, columns, 4)
     return pl.pallas_call(
         functools.partial(layer_backward_kernel, layer, count, split, behind, last),
         out_shape=outs,
@@ -1208,7 +1184,7 @@
         for kind in range(3):
             wqkv[layer, kind] = attn[layer][:, (kind + 1) * depth : (kind + 2) * depth]
         wup[layer] = up[layer][...]
-        wdown[layer] = down[layer][...].T
+        wdown[layer] = down[layer][...]
         sums = smalls[layer]
         row = slice(layer, layer + 1)
         bias_down[row] = sums[0:1]
@@ -1227,19 +1203,20 @@
     rows, width = state.shape
     share, units = up[0].shape
     layers = len(attn)
-    return pl.pallas_call(
+    outs = pl.pallas_call(
         functools.partial(results_kernel, depth),
         out_shape=[
             shape((rows, width)), shape((rows, width)), shape((layers, 3, share, depth)),
             shape((layers, 2, depth)), shape((layers, depth, share)), shape((layers, width)),
             shape((layers, 2, width)), shape((layers, 2, width)), shape((layers, share, units)),
-            shape((layers, units)), shape((layers, units, share)), shape((layers, width)),
+            shape((layers, units)), shape((layers, share, units)), shape((layers, width)),
         ],
         in_specs=[VM] * 11,
         out_specs=[VM] * 12,
         compiler_params=pltpu.CompilerParams(vmem_limit_bytes=VMEM_BYTES),
         name="results",
     )(state, grad, *attn, *up, *down, tail, *smalls)
+    return (*outs[:10], jnp.swapaxes(outs[10], 1, 2), outs[11])
 
 
 def local(
@@ -1260,16 +1237,16 @@
     width = tokens.shape[1]
     layer_count = w_qkv.shape[0]
     depth = w_out.shape[1]
+    w_qkv = jnp.swapaxes(w_qkv, 2, 3)
     state, low = tokens, tokens
     stored = []
     for layer in range(layer_count):
-        state, low, normal1, recip1, *saved = attention_layer(
-            layer, state, low, w_qkv, bias_qv, w_out, bias_out, norm_gain, norm_bias, prefix
+        state, low, normal1, recip1, normal2, recip2, *saved = layer_forward(
+            layer, state, low, w_qkv, bias_qv, w_out, bias_out, norm_gain, norm_bias, w_up, bias_up, w_down,
+            bias_down, prefix,
         )
-        state, low, normal2, recip2, normed, active, slope = ffn_layer(
-            layer, state, low, w_up, bias_up, w_down, bias_down, norm_gain, norm_bias
-        )
-        stored.append(((normal2, recip2), (active, slope, normed, normal1, recip1), saved))
+        normed, active, slope = saved[8:]
+        stored.append(((normal2, recip2), (active, slope, normed, normal1, recip1), saved[:8]))
     count = lax.axis_size("dp")
     split = count > 2 and count % 2 == 0 and (width // count) % 16 == 0
     grad = cotangent

time: 287 us -> 270 us (0.941)
  Pallas kernels: 274 us -> 265 us
  local copies, waits for them, and re-layouts: 6.24 us -> 0 us
    pallas_call x4 -> x2, Pallas kernels: 123 us -> 116 us  [layer_forward(): pl.pallas_call(functools.partial(layer_forward_kernel, layer), out_shape=...]
    unnamed x1 -> x0, local copies, waits for them, and re-layouts: 4.03 us -> none
where the time goes in v5:
time: 270 us; the launch traced here: 266 us
  Pallas kernels  265 us (98%)
    pallas_call x2, Pallas kernels, layer_back(): pl.pallas_call(functools.partial(layer_backward_kernel, layer, count, spl...  144 us
    pallas_call x2, Pallas kernels, layer_forward(): pl.pallas_call(functools.partial(layer_forward_kernel, layer), out_shape=...  116 us

profile of v5, /device:TPU:0, one launch (start us, length us, event | category | flops | bytes accessed | tf_op | source)
XLA Modules:
  0.0 266.1 jit_solution(2237970170068403468)
XLA Ops:
  1.3 59.0 %layer_fwd.2 = (f32[256,768]{1,0:T(8,128)}, bf16[256,768]{1,0:T(8,128)(2,1)}, f32[256,768]{1,0:T(8,128)}, f32[256,128]{1,0:T(8,128)}, f32[256,768]{1,0:T(8,128)}...) custom-call(bf16[256,768]{1,0:T(8,128)(2,1)} %refs_1_.1, ...), custom_call_target="tpu_custom_call" | custom-call | tf_op jit(solution)/shard_map/layer_fwd/pallas_call | solution.py:519
  60.3 57.3 %layer_fwd.3 = (f32[256,768]{1,0:T(8,128)}, bf16[256,768]{1,0:T(8,128)(2,1)}, f32[256,768]{1,0:T(8,128)}, f32[256,128]{1,0:T(8,128)}, f32[256,768]{1,0:T(8,128)}...) custom-call(f32[256,768]{1,0:T(8,128)} %get-tuple-element.70.refs_0_, ...), custom_call_target="tpu_custom_call" | custom-call | tf_op jit(solution)/shard_map/layer_fwd/pallas_call | solution.py:519
  117.7 68.8 %layer_bwd.2 = (f32[256,768]{1,0:T(8,128)}, f32[8,768]{1,0:T(8,128)}, f32[768,768]{1,0:T(8,128)}, f32[96,768]{1,0:T(8,128)}, f32[96,768]{1,0:T(8,128)}, /*index=5*/f32[8,768]{1,0:T(8,128)}) custom-call(bf16[256,768]{1,0:T(8,128)(2,1)} %refs_0_.3, f32[256,768]{1,0:T(8,128)} %get-tuple-element.73.refs_1_, f32[256,128]{1,0:T(8,128)} %get-tuple-element.74.refs_2_, ...), custom_call_target="tpu_custom_call" | custom-call | tf_op jit(solution)/shard_map/layer_bwd/pallas_call | solution.py:1163
  186.5 75.4 %layer_bwd.3 = (f32[256,768]{1,0:T(8,128)}, f32[8,768]{1,0:T(8,128)}, f32[96,768]{1,0:T(8,128)}, f32[96,768]{1,0:T(8,128)}, f32[8,768]{1,0:T(8,128)}, /*index=5*...) custom-call(f32[256,768]{1,0:T(8,128)} %get-tuple-element.88.refs_0_, f32[256,768]{1,0:T(8,128)} %get-tuple-element.89.refs_1_, ...), custom_call_target="tpu_custom_call" | custom-call | tf_op jit(solution)/shard_map/layer_bwd/pallas_call | solution.py:1163
  261.9 4.0 %results.1 = (f32[256,768]{1,0:T(8,128)}, f32[256,768]{1,0:T(8,128)}, f32[2,3,96,192]{3,2,1,0:T(8,128)}, f32[2,2,192]{2,1,0:T(2,128)}, f32[2,192,96]{2,1,0:T(8,1...) custom-call(f32[256,768]{1,0:T(8,128)} %get-tuple-element.72.refs_0_, ...), custom_call_target="tpu_custom_call" | custom-call | tf_op jit(solution)/shard_map/results/pallas_call | solution.py:1206

commit v6 on v5

--- a/solution.py
+++ b/solution.py
@@ -973,7 +973,9 @@
 
     beside = {heads: [lambda: gathered(1)], 2 * heads: [lambda: gathered(2)], 3 * heads: [lambda: gathered(3)]}
     if split:
-        plan = [(2, downs[0].turn), (6, small.first), (6, ups[1].start), (5, downs[1].turn), (9, ups[0].turn), (11, small.second)]
+        turns = (2, 5, 9) if last else (3, 6, 11)
+        plan = [(turns[0], downs[0].turn), (6, small.first), (6, ups[1].start), (turns[1], downs[1].turn)]
+        plan += [(turns[2], ups[0].turn), (11, small.second)]
         for when, action in plan:
             beside.setdefault(when, []).append(action)
         for item in earlier:
@@ -1051,9 +1053,8 @@
                 total = term if total is None else total + term
         terms_ref[chunk, exchange.spot(part)] = total
 
-    if split:
+    if last:
         ups[1].turn()
-    if last:
         own_small.first()
     if split:
         weight_grad(0)
@@ -1076,6 +1077,8 @@
         exchange.near_copy(part).start()
     for part in range(BACK_PIECES):
         input_terms(mine, part)
+    if split and not last:
+        ups[1].turn()
     if last:
         own[0].turn()
         own[1].turn()

time: 270 us -> 270 us (level)
  no operation moved by 1% of the time
where the time goes in v6:
time: 270 us; the launch traced here: 266 us
  Pallas kernels  264 us (98%)
    pallas_call x2, Pallas kernels, layer_back(): pl.pallas_call(functools.partial(layer_backward_kernel, layer, count, spl...  144 us
    pallas_call x2, Pallas kernels, layer_forward(): pl.pallas_call(functools.partial(layer_forward_kernel, layer), out_shape=...  116 us

profile of v6, /device:TPU:0, one launch (start us, length us, event | category | flops | bytes accessed | tf_op | source)
XLA Modules:
  0.0 265.6 jit_solution(6726770144453639799)
XLA Ops:
  1.3 59.0 %layer_fwd.2 = (f32[256,768]{1,0:T(8,128)}, bf16[256,768]{1,0:T(8,128)(2,1)}, f32[256,768]{1,0:T(8,128)}, f32[256,128]{1,0:T(8,128)}, f32[256,768]{1,0:T(8,128)}...) custom-call(bf16[256,768]{1,0:T(8,128)(2,1)} %refs_1_.1, ...), custom_call_target="tpu_custom_call" | custom-call | tf_op jit(solution)/shard_map/layer_fwd/pallas_call | solution.py:519
  60.3 57.3 %layer_fwd.3 = (f32[256,768]{1,0:T(8,128)}, bf16[256,768]{1,0:T(8,128)(2,1)}, f32[256,768]{1,0:T(8,128)}, f32[256,128]{1,0:T(8,128)}, f32[256,768]{1,0:T(8,128)}...) custom-call(f32[256,768]{1,0:T(8,128)} %get-tuple-element.70.refs_0_, ...), custom_call_target="tpu_custom_call" | custom-call | tf_op jit(solution)/shard_map/layer_fwd/pallas_call | solution.py:519
  117.7 67.9 %layer_bwd.2 = (f32[256,768]{1,0:T(8,128)}, f32[8,768]{1,0:T(8,128)}, f32[768,768]{1,0:T(8,128)}, f32[96,768]{1,0:T(8,128)}, f32[96,768]{1,0:T(8,128)}, /*index=5*/f32[8,768]{1,0:T(8,128)}) custom-call(bf16[256,768]{1,0:T(8,128)(2,1)} %refs_0_.3, f32[256,768]{1,0:T(8,128)} %get-tuple-element.73.refs_1_, f32[256,128]{1,0:T(8,128)} %get-tuple-element.74.refs_2_, ...), custom_call_target="tpu_custom_call" | custom-call | tf_op jit(solution)/shard_map/layer_bwd/pallas_call | solution.py:1166
  185.6 75.8 %layer_bwd.3 = (f32[256,768]{1,0:T(8,128)}, f32[8,768]{1,0:T(8,128)}, f32[96,768]{1,0:T(8,128)}, f32[96,768]{1,0:T(8,128)}, f32[8,768]{1,0:T(8,128)}, /*index=5*...) custom-call(f32[256,768]{1,0:T(8,128)} %get-tuple-element.88.refs_0_, f32[256,768]{1,0:T(8,128)} %get-tuple-element.89.refs_1_, ...), custom_call_target="tpu_custom_call" | custom-call | tf_op jit(solution)/shard_map/layer_bwd/pallas_call | solution.py:1166
  261.4 4.0 %results.1 = (f32[256,768]{1,0:T(8,128)}, f32[256,768]{1,0:T(8,128)}, f32[2,3,96,192]{3,2,1,0:T(8,128)}, f32[2,2,192]{2,1,0:T(2,128)}, f32[2,192,96]{2,1,0:T(8,1...) custom-call(f32[256,768]{1,0:T(8,128)} %get-tuple-element.72.refs_0_, ...), custom_call_target="tpu_custom_call" | custom-call | tf_op jit(solution)/shard_map/results/pallas_call | solution.py:1209
